TPU v7x, 128 devices: a whole 4x4x4 slice. The times are simulated.
128 devices in a mesh: seq: 4 (over z), shard: 2 (over x_hi), dp: 16 (over y, x_lo, core).
Axes of the slice: x: 4 (x_hi: 2, x_lo: 2; x = x_hi * 2 + x_lo), y: 4, z: 4, core: 2. Of those that a mesh axis runs over, the one named last changes fastest.
Arguments:
- inputs: float32 [64, 320, 1024], P(('shard', 'dp'), 'seq'), may hold values from -6 to 6
- segment_ids: int32 [64, 320], P(('shard', 'dp'), 'seq'), may hold values from 0 to 2, never falling along the last dimension, each value on 1 to 160 neighbouring positions
- weight_qkv: bfloat16 [2, 1024, 3072], P(None, ('seq', 'shard')), may hold values from -30 to 30
- weight_out: bfloat16 [2, 1024, 1024], P(None, ('seq', 'shard')), may hold values from -0.75 to 0.75
- weight_up: bfloat16 [2, 1024, 4096], P(None, ('seq', 'shard')), may hold values from -0.1875 to 0.1875
- weight_down: bfloat16 [2, 4096, 1024], P(None, ('seq', 'shard')), may hold values from -0.09375 to 0.09375
- bias_qv: bfloat16 [2, 2048], P(None, ('seq', 'shard')), may hold values from -3 to 3
- bias_out: bfloat16 [2, 1024], P(None, ('seq', 'shard')), may hold values from -3 to 3
- bias_up: bfloat16 [2, 4096], P(None, ('seq', 'shard')), may hold values from -3 to 3
- bias_down: bfloat16 [2, 1024], P(None, ('seq', 'shard')), may hold values from -3 to 3
- gain_one: bfloat16 [2, 1024], P(None, ('seq', 'shard')), may hold values from 0.5 to 1.5
- shift_one: bfloat16 [2, 1024], P(None, ('seq', 'shard')), may hold values from -3 to 3
- gain_two: bfloat16 [2, 1024], P(None, ('seq', 'shard')), may hold values from 0.5 to 1.5
- shift_two: bfloat16 [2, 1024], P(None, ('seq', 'shard')), may hold values from -3 to 3
- cotangent: float32 [64, 320, 1024], P(('shard', 'dp'), 'seq'), may hold values from -0.75 to 0.75
Outputs:
- outputs: float32 [64, 320, 1024], P(('shard', 'dp'), 'seq')
- input_grad: float32 [64, 320, 1024], P(('shard', 'dp'), 'seq')
- grad_weight_qkv: float32 [2, 1024, 3072], P(None, ('seq', 'shard'))
- grad_weight_out: float32 [2, 1024, 1024], P(None, ('seq', 'shard'))
- grad_weight_up: float32 [2, 1024, 4096], P(None, ('seq', 'shard'))
- grad_weight_down: float32 [2, 4096, 1024], P(None, ('seq', 'shard'))
- grad_bias_qv: float32 [2, 2048], P(None, ('seq', 'shard'))
- grad_bias_out: float32 [2, 1024], P(None, ('seq', 'shard'))
- grad_bias_up: float32 [2, 4096], P(None, ('seq', 'shard'))
- grad_bias_down: float32 [2, 1024], P(None, ('seq', 'shard'))
- grad_gain_one: float32 [2, 1024], P(None, ('seq', 'shard'))
- grad_shift_one: float32 [2, 1024], P(None, ('seq', 'shard'))
- grad_gain_two: float32 [2, 1024], P(None, ('seq', 'shard'))
- grad_shift_two: float32 [2, 1024], P(None, ('seq', 'shard'))
All inputs are finite; a program needn't handle non-finite values.
Results may differ from a plain program's by a relative error of at most 0.03.
Values may be sent and summed in bfloat16 or wider, within the bound.
A program may use at most 256 MiB of HBM per device.

v0:
```python
import math

import jax
import jax.numpy as jnp
from jax import lax
from jax.sharding import PartitionSpec as P

H = 16


NORM_EPS = 1e-05
GELU_COEF = 0.7978845608028654
CUBIC_COEF = 0.044715


def layer_norm(state, gain, shift):
    center = state - jnp.mean(state, axis=-1, keepdims=True)
    factor = lax.rsqrt(jnp.mean(center * center, axis=-1, keepdims=True) + NORM_EPS)
    normed = center * factor
    return (normed, factor, normed * gain.astype(jnp.float32) + shift.astype(jnp.float32))


def norm_backward(d_act, normed, factor, gain):
    d_norm = d_act * gain.astype(jnp.float32)
    return factor * (
        d_norm
        - jnp.mean(d_norm, axis=-1, keepdims=True)
        - normed * jnp.mean(d_norm * normed, axis=-1, keepdims=True)
    )


def gelu_pair(pre_act):
    cubic = pre_act * pre_act * pre_act
    tangent = jnp.tanh(GELU_COEF * (pre_act + CUBIC_COEF * cubic))
    gelu_value = 0.5 * pre_act * (1.0 + tangent)
    gelu_slope = 0.5 * (1.0 + tangent) + 0.5 * pre_act * (1.0 - tangent * tangent) * GELU_COEF * (
        1.0 + 3.0 * CUBIC_COEF * pre_act * pre_act
    )
    return (gelu_value, gelu_slope)


def local_product(form, left, right):
    return jnp.einsum(form, left, right, preferred_element_type=jnp.float32)


def masked_scores(queries, keys_all, allowed, scale):
    raw_scores = local_product("bqhd,bkhd->bhqk", queries, keys_all) * scale
    return jnp.where(allowed[:, None], raw_scores, -jnp.inf)


def per_device(
    inputs,
    segment_ids,
    weight_qkv,
    weight_out,
    weight_up,
    weight_down,
    bias_qv,
    bias_out,
    bias_up,
    bias_down,
    gain_one,
    shift_one,
    gain_two,
    shift_two,
    cotangent,
):
    batch, rows_dev, width = inputs.shape
    heads = H
    head_dim = width // heads
    length = rows_dev * lax.axis_size("seq")
    rows_here = batch * rows_dev
    scale = 1.0 / math.sqrt(head_dim)
    layers = weight_qkv.shape[0]
    query_pos = lax.axis_index("seq") * rows_dev + jnp.arange(rows_dev, dtype=jnp.int32)
    key_pos = jnp.arange(length, dtype=jnp.int32)
    causal = query_pos[:, None] >= key_pos[None, :]
    state = inputs.reshape(rows_here, width)
    records = []
    for layer_at in range(layers):
        gathered = (
            lax.all_gather(weight_qkv[layer_at], ("seq", "shard"), axis=0, tiled=True),
            lax.all_gather(weight_out[layer_at], ("seq", "shard"), axis=0, tiled=True),
            lax.all_gather(weight_up[layer_at], ("seq", "shard"), axis=0, tiled=True),
            lax.all_gather(weight_down[layer_at], ("seq", "shard"), axis=0, tiled=True),
            lax.all_gather(bias_qv[layer_at], ("seq", "shard"), axis=0, tiled=True),
            lax.all_gather(bias_out[layer_at], ("seq", "shard"), axis=0, tiled=True),
            lax.all_gather(bias_up[layer_at], ("seq", "shard"), axis=0, tiled=True),
            lax.all_gather(bias_down[layer_at], ("seq", "shard"), axis=0, tiled=True),
            lax.all_gather(gain_one[layer_at], ("seq", "shard"), axis=0, tiled=True),
            lax.all_gather(shift_one[layer_at], ("seq", "shard"), axis=0, tiled=True),
            lax.all_gather(gain_two[layer_at], ("seq", "shard"), axis=0, tiled=True),
            lax.all_gather(shift_two[layer_at], ("seq", "shard"), axis=0, tiled=True),
        )
        (
            full_qkv,
            full_out,
            full_up,
            full_down,
            full_bqv,
            full_bout,
            full_bup,
            full_bdown,
            full_gone,
            full_sone,
            full_gtwo,
            full_stwo,
        ) = gathered
        norm_one, factor_one, act_one = layer_norm(state, full_gone, full_sone)
        act_one = act_one.astype(jnp.bfloat16)
        bias_qkv = jnp.concatenate(
            [
                full_bqv[:width].astype(jnp.float32),
                jnp.zeros((width,), jnp.float32),
                full_bqv[width:].astype(jnp.float32),
            ]
        )
        qkv = (jnp.dot(act_one, full_qkv, preferred_element_type=jnp.float32) + bias_qkv).astype(
            jnp.bfloat16
        )
        qkv = qkv.reshape(batch, rows_dev, 3, heads, head_dim)
        queries, keys_local, values_local = (qkv[:, :, 0], qkv[:, :, 1], qkv[:, :, 2])
        keys_all, values_all, key_segments = (
            lax.all_gather(keys_local, "seq", axis=1, tiled=True),
            lax.all_gather(values_local, "seq", axis=1, tiled=True),
            lax.all_gather(segment_ids, "seq", axis=1, tiled=True),
        )
        allowed = (segment_ids[:, :, None] == key_segments[:, None, :]) & causal[None]
        scores = masked_scores(queries, keys_all, allowed, scale)
        row_top = jnp.max(scores, axis=-1, keepdims=True)
        lse = row_top + jnp.log(jnp.sum(jnp.exp(scores - row_top), axis=-1, keepdims=True))
        probs = jnp.exp(scores - lse).astype(jnp.bfloat16)
        attn = (
            local_product("bhqk,bkhd->bqhd", probs, values_all)
            .astype(jnp.bfloat16)
            .reshape(rows_here, width)
        )
        middle = (
            state
            + jnp.dot(attn, full_out, preferred_element_type=jnp.float32)
            + full_bout.astype(jnp.float32)
        )
        norm_two, factor_two, act_two = layer_norm(middle, full_gtwo, full_stwo)
        act_two = act_two.astype(jnp.bfloat16)
        pre_act = jnp.dot(act_two, full_up, preferred_element_type=jnp.float32) + full_bup.astype(
            jnp.float32
        )
        gelu_value, gelu_slope = gelu_pair(pre_act)
        hidden = gelu_value.astype(jnp.bfloat16)
        state = (
            middle
            + jnp.dot(hidden, full_down, preferred_element_type=jnp.float32)
            + full_bdown.astype(jnp.float32)
        )
        records.append(
            (
                norm_one,
                factor_one,
                act_one,
                queries,
                keys_all,
                values_all,
                allowed,
                lse,
                attn,
                norm_two,
                factor_two,
                act_two,
                gelu_slope,
                hidden,
            )
        )
    grad_state = cotangent.reshape(rows_here, width)
    share_list = [None] * layers
    for layer_at in reversed(range(layers)):
        gathered = (
            lax.all_gather(weight_qkv[layer_at], ("seq", "shard"), axis=0, tiled=True),
            lax.all_gather(weight_out[layer_at], ("seq", "shard"), axis=0, tiled=True),
            lax.all_gather(weight_up[layer_at], ("seq", "shard"), axis=0, tiled=True),
            lax.all_gather(weight_down[layer_at], ("seq", "shard"), axis=0, tiled=True),
            lax.all_gather(bias_qv[layer_at], ("seq", "shard"), axis=0, tiled=True),
            lax.all_gather(bias_out[layer_at], ("seq", "shard"), axis=0, tiled=True),
            lax.all_gather(bias_up[layer_at], ("seq", "shard"), axis=0, tiled=True),
            lax.all_gather(bias_down[layer_at], ("seq", "shard"), axis=0, tiled=True),
            lax.all_gather(gain_one[layer_at], ("seq", "shard"), axis=0, tiled=True),
            lax.all_gather(shift_one[layer_at], ("seq", "shard"), axis=0, tiled=True),
            lax.all_gather(gain_two[layer_at], ("seq", "shard"), axis=0, tiled=True),
            lax.all_gather(shift_two[layer_at], ("seq", "shard"), axis=0, tiled=True),
        )
        (
            full_qkv,
            full_out,
            full_up,
            full_down,
            full_bqv,
            full_bout,
            full_bup,
            full_bdown,
            full_gone,
            full_sone,
            full_gtwo,
            full_stwo,
        ) = gathered
        (
            norm_one,
            factor_one,
            act_one,
            queries,
            keys_all,
            values_all,
            allowed,
            lse,
            attn,
            norm_two,
            factor_two,
            act_two,
            gelu_slope,
            hidden,
        ) = records[layer_at]
        grad_low = grad_state.astype(jnp.bfloat16)
        grad_b_down = jnp.sum(grad_state, axis=0)
        d_pre = jnp.dot(grad_low, full_down.T, preferred_element_type=jnp.float32) * gelu_slope
        d_pre_low = d_pre.astype(jnp.bfloat16)
        grad_b_up = jnp.sum(d_pre, axis=0)
        d_act_two = jnp.dot(d_pre_low, full_up.T, preferred_element_type=jnp.float32)
        grad_g_two = jnp.sum(d_act_two * norm_two, axis=0)
        grad_s_two = jnp.sum(d_act_two, axis=0)
        grad_middle = grad_state + norm_backward(d_act_two, norm_two, factor_two, full_gtwo)
        grad_attn_low = grad_middle.astype(jnp.bfloat16)
        grad_b_out = jnp.sum(grad_middle, axis=0)
        d_attn = jnp.dot(grad_attn_low, full_out.T, preferred_element_type=jnp.float32).astype(
            jnp.bfloat16
        )
        d_attn = d_attn.reshape(batch, rows_dev, heads, head_dim)
        attn_heads = attn.reshape(batch, rows_dev, heads, head_dim)
        scores = masked_scores(queries, keys_all, allowed, scale)
        prob_full = jnp.exp(scores - lse)
        probs = prob_full.astype(jnp.bfloat16)
        delta = jnp.sum(d_attn.astype(jnp.float32) * attn_heads.astype(jnp.float32), axis=-1)
        delta = jnp.transpose(delta, (0, 2, 1))[..., None]
        d_prob = local_product("bqhd,bkhd->bhqk", d_attn, values_all)
        d_scores = (prob_full * (d_prob - delta)).astype(jnp.bfloat16)
        d_query = local_product("bhqk,bkhd->bqhd", d_scores, keys_all) * scale
        key_terms = local_product("bhqk,bqhd->bkhd", d_scores, queries) * scale
        value_terms = local_product("bhqk,bqhd->bkhd", probs, d_attn)
        d_key, d_value = (
            lax.psum_scatter(
                key_terms.astype(jnp.bfloat16), "seq", scatter_dimension=1, tiled=True
            ).astype(jnp.float32),
            lax.psum_scatter(
                value_terms.astype(jnp.bfloat16), "seq", scatter_dimension=1, tiled=True
            ).astype(jnp.float32),
        )
        d_query = d_query.reshape(rows_here, width)
        d_value = d_value.reshape(rows_here, width)
        d_qkv = jnp.concatenate([d_query, d_key.reshape(rows_here, width), d_value], axis=1).astype(
            jnp.bfloat16
        )
        grad_b_qv = jnp.concatenate([jnp.sum(d_query, axis=0), jnp.sum(d_value, axis=0)])
        d_act_one = jnp.dot(d_qkv, full_qkv.T, preferred_element_type=jnp.float32)
        grad_g_one = jnp.sum(d_act_one * norm_one, axis=0)
        grad_s_one = jnp.sum(d_act_one, axis=0)
        grad_state = grad_middle + norm_backward(d_act_one, norm_one, factor_one, full_gone)
        grad_w_qkv = jnp.dot(act_one.T, d_qkv, preferred_element_type=jnp.float32)
        grad_w_out = jnp.dot(attn.T, grad_attn_low, preferred_element_type=jnp.float32)
        grad_w_up = jnp.dot(act_two.T, d_pre_low, preferred_element_type=jnp.float32)
        grad_w_down = jnp.dot(hidden.T, grad_low, preferred_element_type=jnp.float32)
        shares = (
            lax.psum_scatter(
                grad_w_qkv.astype(jnp.bfloat16), ("seq", "shard"), scatter_dimension=0, tiled=True
            ).astype(jnp.float32),
            lax.psum_scatter(
                grad_w_out.astype(jnp.bfloat16), ("seq", "shard"), scatter_dimension=0, tiled=True
            ).astype(jnp.float32),
            lax.psum_scatter(
                grad_w_up.astype(jnp.bfloat16), ("seq", "shard"), scatter_dimension=0, tiled=True
            ).astype(jnp.float32),
            lax.psum_scatter(
                grad_w_down.astype(jnp.bfloat16), ("seq", "shard"), scatter_dimension=0, tiled=True
            ).astype(jnp.float32),
            lax.psum_scatter(
                grad_b_qv.astype(jnp.bfloat16), ("seq", "shard"), scatter_dimension=0, tiled=True
            ).astype(jnp.float32),
            lax.psum_scatter(
                grad_b_out.astype(jnp.bfloat16), ("seq", "shard"), scatter_dimension=0, tiled=True
            ).astype(jnp.float32),
            lax.psum_scatter(
                grad_b_up.astype(jnp.bfloat16), ("seq", "shard"), scatter_dimension=0, tiled=True
            ).astype(jnp.float32),
            lax.psum_scatter(
                grad_b_down.astype(jnp.bfloat16), ("seq", "shard"), scatter_dimension=0, tiled=True
            ).astype(jnp.float32),
            lax.psum_scatter(
                grad_g_one.astype(jnp.bfloat16), ("seq", "shard"), scatter_dimension=0, tiled=True
            ).astype(jnp.float32),
            lax.psum_scatter(
                grad_s_one.astype(jnp.bfloat16), ("seq", "shard"), scatter_dimension=0, tiled=True
            ).astype(jnp.float32),
            lax.psum_scatter(
                grad_g_two.astype(jnp.bfloat16), ("seq", "shard"), scatter_dimension=0, tiled=True
            ).astype(jnp.float32),
            lax.psum_scatter(
                grad_s_two.astype(jnp.bfloat16), ("seq", "shard"), scatter_dimension=0, tiled=True
            ).astype(jnp.float32),
        )
        shares = (
            lax.psum(shares[0].astype(jnp.bfloat16), "dp").astype(jnp.float32),
            lax.psum(shares[1].astype(jnp.bfloat16), "dp").astype(jnp.float32),
            lax.psum(shares[2].astype(jnp.bfloat16), "dp").astype(jnp.float32),
            lax.psum(shares[3].astype(jnp.bfloat16), "dp").astype(jnp.float32),
            lax.psum(shares[4].astype(jnp.bfloat16), "dp").astype(jnp.float32),
            lax.psum(shares[5].astype(jnp.bfloat16), "dp").astype(jnp.float32),
            lax.psum(shares[6].astype(jnp.bfloat16), "dp").astype(jnp.float32),
            lax.psum(shares[7].astype(jnp.bfloat16), "dp").astype(jnp.float32),
            lax.psum(shares[8].astype(jnp.bfloat16), "dp").astype(jnp.float32),
            lax.psum(shares[9].astype(jnp.bfloat16), "dp").astype(jnp.float32),
            lax.psum(shares[10].astype(jnp.bfloat16), "dp").astype(jnp.float32),
            lax.psum(shares[11].astype(jnp.bfloat16), "dp").astype(jnp.float32),
        )
        share_list[layer_at] = shares
    stacked = tuple(
        (
            jnp.stack([share_list[layer_at][member_at] for layer_at in range(layers)])
            for member_at in range(12)
        )
    )
    return (
        state.reshape(batch, rows_dev, width),
        grad_state.reshape(batch, rows_dev, width),
        stacked[0],
        stacked[1],
        stacked[2],
        stacked[3],
        stacked[4],
        stacked[5],
        stacked[6],
        stacked[7],
        stacked[8],
        stacked[9],
        stacked[10],
        stacked[11],
    )


def solution(mesh):
    in_specs = (
        P(("shard", "dp"), "seq", None),
        P(("shard", "dp"), "seq"),
        P(None, ("seq", "shard"), None),
        P(None, ("seq", "shard"), None),
        P(None, ("seq", "shard"), None),
        P(None, ("seq", "shard"), None),
        P(None, ("seq", "shard")),
        P(None, ("seq", "shard")),
        P(None, ("seq", "shard")),
        P(None, ("seq", "shard")),
        P(None, ("seq", "shard")),
        P(None, ("seq", "shard")),
        P(None, ("seq", "shard")),
        P(None, ("seq", "shard")),
        P(("shard", "dp"), "seq", None),
    )
    out_specs = (
        P(("shard", "dp"), "seq", None),
        P(("shard", "dp"), "seq", None),
        P(None, ("seq", "shard"), None),
        P(None, ("seq", "shard"), None),
        P(None, ("seq", "shard"), None),
        P(None, ("seq", "shard"), None),
        P(None, ("seq", "shard")),
        P(None, ("seq", "shard")),
        P(None, ("seq", "shard")),
        P(None, ("seq", "shard")),
        P(None, ("seq", "shard")),
        P(None, ("seq", "shard")),
        P(None, ("seq", "shard")),
        P(None, ("seq", "shard")),
    )
    return jax.shard_map(
        per_device, mesh=mesh, in_specs=in_specs, out_specs=out_specs, check_vma=False
    )
```

profile of v0, /device:TPU:1, one launch (start us, length us, event | category | flops | bytes accessed | tf_op | source)
XLA Modules:
  0.0 2080.2 jit_solution(7049784337945528115)
XLA Ops:
  10.6 21.6 %all-gather.1 = bf16[1,1024]{1,0:T(2,128)(2,1)S(1)} all-gather(bf16[1,128]{1,0:T(2,128)(2,1)S(1)} %get-tuple-element.117), channel_id=3, replica_groups=mesh['seq'=4,'shard'=2,'dp'=16] {'seq','shard'}, dimensions={1}, use_global_device_ids=true | all-gather | bytes 2304 | tf_op jit(solution)/shard_map/all_gather | solution.py:91
  46.7 17.7 all-gather.17
  64.4 15.4 all-gather.3
  80.0 23.1 %all-gather.42.cloned.1.call-done = bf16[1,1024,3072]{2,1,0:T(8,128)(2,1)} async-done(((bf16[1,128,3072]{2,1,0:T(8,128)(2,1)}), bf16[1,1024,3072]{2,1,0:T(8,128)(2,1)}) %all-gather.42.cloned.1.call-update) | async-done | bytes 6291472 | tf_op jit(solution)/shard_map/all_gather | solution.py:82
  121.6 15.0 all-gather.13
  136.6 17.5 all-gather.7
  159.5 26.4 %all-gather.11 = bf16[1,4096]{1,0:T(2,128)(2,1)S(1)} all-gather(bf16[1,512]{1,0:T(2,128)(2,1)S(1)} %get-tuple-element.103), channel_id=13, replica_groups=mesh['seq'=4,'shard'=2,'dp'=16] {'seq','shard'}, dimensions={1}, use_global_device_ids=true | all-gather | bytes 9216 | tf_op jit(solution)/shard_map/all_gather | solution.py:88
  185.9 15.1 all-gather.9
  201.1 17.3 all-gather.8
  233.1 17.8 all-gather.14
  271.0 77.1 %all-gather.50.cloned.1.call-done = bf16[1,1024,4096]{2,1,0:T(8,128)(2,1)} async-done(((bf16[1,128,4096]{2,1,0:T(8,128)(2,1)}), bf16[1,1024,4096]{2,1,0:T(8,128)(2,1)}) %all-gather.50.cloned.1.call-update) | async-done | bytes 8388624 | tf_op jit(solution)/shard_map/all_gather | solution.py:84
  354.6 101.3 %all-gather.52.cloned.1.call-done = bf16[1,4096,1024]{2,1,0:T(8,128)(2,1)} async-done(((bf16[1,512,1024]{2,1,0:T(8,128)(2,1)}), bf16[1,4096,1024]{2,1,0:T(8,128)(2,1)}) %all-gather.52.cloned.1.call-update) | async-done | bytes 8388624 | tf_op jit(solution)/shard_map/all_gather | solution.py:85
  462.3 82.8 %all-gather.54.cloned.1.call-done = bf16[1,1024,3072]{2,1,0:T(8,128)(2,1)} async-done(((bf16[1,128,3072]{2,1,0:T(8,128)(2,1)}), bf16[1,1024,3072]{2,1,0:T(8,128)(2,1)}) %all-gather.54.cloned.1.call-update) | async-done | bytes 6291472 | tf_op jit(solution)/shard_map/all_gather | solution.py:82
  574.6 25.5 %all-gather.25 = bf16[1,4096]{1,0:T(2,128)(2,1)S(1)} all-gather(bf16[1,512]{1,0:T(2,128)(2,1)S(1)} %get-tuple-element.102), channel_id=27, replica_groups=mesh['seq'=4,'shard'=2,'dp'=16] {'seq','shard'}, dimensions={1}, use_global_device_ids=true | all-gather | bytes 9216 | tf_op jit(solution)/shard_map/all_gather | solution.py:88
  600.1 17.0 all-gather.23
  617.1 15.5 all-gather.22
  651.6 31.2 %all-gather.60.cloned.1.call-done = bf16[1,1024,1024]{2,1,0:T(8,128)(2,1)} async-done(((bf16[1,128,1024]{2,1,0:T(8,128)(2,1)}), bf16[1,1024,1024]{2,1,0:T(8,128)(2,1)}) %all-gather.60.cloned.1.call-update) | async-done | bytes 2097168 | tf_op jit(solution)/shard_map/all_gather | solution.py:83
  685.3 104.9 %all-gather.62.cloned.1.call-done = bf16[1,1024,4096]{2,1,0:T(8,128)(2,1)} async-done(((bf16[1,128,4096]{2,1,0:T(8,128)(2,1)}), bf16[1,1024,4096]{2,1,0:T(8,128)(2,1)}) %all-gather.62.cloned.1.call-update) | async-done | bytes 8388624 | tf_op jit(solution)/shard_map/all_gather | solution.py:84
  796.8 101.3 %all-gather.64.cloned.1.call-done = bf16[1,4096,1024]{2,1,0:T(8,128)(2,1)} async-done(((bf16[1,512,1024]{2,1,0:T(8,128)(2,1)}), bf16[1,4096,1024]{2,1,0:T(8,128)(2,1)}) %all-gather.64.cloned.1.call-update) | async-done | bytes 8388624 | tf_op jit(solution)/shard_map/all_gather | solution.py:85
  955.6 23.5 %reduce-scatter.39.cloned.1.call-done = bf16[80,2048]{1,0:T(8,128)(2,1)} async-done(((bf16[320,2048]{1,0:T(8,128)(2,1)}), bf16[80,2048]{1,0:T(8,128)(2,1)}) %reduce-scatter.39.cloned.1.call-update) | async-done | bytes 327696
  1104.4 50.1 %reduce-scatter.27.cloned.1.call-done = bf16[128,1024]{1,0:T(8,128)(2,1)} async-done(((bf16[1024,1024]{1,0:T(8,128)(2,1)}), bf16[128,1024]{1,0:T(8,128)(2,1)}) %reduce-scatter.27.cloned.1.call-update) | async-done | bytes 262160 | tf_op jit(solution)/shard_map/reduce_scatter | solution.py:272
  1154.5 78.1 %reduce-scatter.25.cloned.1.call-done = bf16[128,1024]{1,0:T(8,128)(2,1)} async-done(((bf16[1024,1024]{1,0:T(8,128)(2,1)}), bf16[128,1024]{1,0:T(8,128)(2,1)}) %reduce-scatter.25.cloned.1.call-update) | async-done | bytes 262160 | tf_op jit(solution)/shard_map/reduce_scatter | solution.py:272
  1232.6 102.1 %reduce-scatter.23.cloned.1.call-done = bf16[128,3072]{1,0:T(8,128)(2,1)} async-done(((bf16[1024,3072]{1,0:T(8,128)(2,1)}), bf16[128,3072]{1,0:T(8,128)(2,1)}) %reduce-scatter.23.cloned.1.call-update) | async-done | bytes 786448 | tf_op jit(solution)/shard_map/reduce_scatter | solution.py:269
  1334.7 116.9 %reduce-scatter.31.cloned.1.call-done = bf16[128,4096]{1,0:T(8,128)(2,1)} async-done(((bf16[1024,4096]{1,0:T(8,128)(2,1)}), bf16[128,4096]{1,0:T(8,128)(2,1)}) %reduce-scatter.31.cloned.1.call-update) | async-done | bytes 1048592 | tf_op jit(solution)/shard_map/reduce_scatter | solution.py:275
  1451.6 116.2 %reduce-scatter.35.cloned.1.call-done = bf16[512,1024]{1,0:T(8,128)(2,1)} async-done(((bf16[4096,1024]{1,0:T(8,128)(2,1)}), bf16[512,1024]{1,0:T(8,128)(2,1)}) %reduce-scatter.35.cloned.1.call-update) | async-done | bytes 1048592 | tf_op jit(solution)/shard_map/reduce_scatter | solution.py:278
  1567.8 100.3 %reduce-scatter.21.cloned.1.call-done = bf16[128,3072]{1,0:T(8,128)(2,1)} async-done(((bf16[1024,3072]{1,0:T(8,128)(2,1)}), bf16[128,3072]{1,0:T(8,128)(2,1)}) %reduce-scatter.21.cloned.1.call-update) | async-done | bytes 786448 | tf_op jit(solution)/shard_map/reduce_scatter | solution.py:269
  1668.1 117.1 %reduce-scatter.29.cloned.1.call-done = bf16[128,4096]{1,0:T(8,128)(2,1)} async-done(((bf16[1024,4096]{1,0:T(8,128)(2,1)}), bf16[128,4096]{1,0:T(8,128)(2,1)}) %reduce-scatter.29.cloned.1.call-update) | async-done | bytes 1048592 | tf_op jit(solution)/shard_map/reduce_scatter | solution.py:275
  1785.2 116.5 %reduce-scatter.33.cloned.1.call-done = bf16[512,1024]{1,0:T(8,128)(2,1)} async-done(((bf16[4096,1024]{1,0:T(8,128)(2,1)}), bf16[512,1024]{1,0:T(8,128)(2,1)}) %reduce-scatter.33.cloned.1.call-update) | async-done | bytes 1048592 | tf_op jit(solution)/shard_map/reduce_scatter | solution.py:278
  1901.8 15.2 all-gather.27
  1933.0 35.0 %all-reduce.18 = (bf16[2048]{0:T(1024)(128)(2,1)S(1)}, bf16[2048]{0:T(1024)(128)(2,1)S(1)}, bf16[1024]{0:T(1024)(128)(2,1)S(1)}, bf16[1024]{0:T(1024)(128)(2,1)S...) all-reduce(bf16[2048]{0:T(1024)(128)(2,1)S(1)} %pad_maximum_fusion., ...), channel_id=43, replica_groups=mesh['seq'=4,'shard'=2,'dp'=16] {'seq','shard'}, use_global_device_ids=true, to_apply=%region_48.49.clone | all-reduce | flops 24576 | bytes 98304
  1969.3 60.1 %all-reduce.16 = (bf16[1,256]{1,0:T(2,128)(2,1)S(1)}, bf16[1,256]{1,0:T(2,128)(2,1)S(1)}, bf16[1,128]{1,0:T(2,128)(2,1)S(1)}, bf16[1,128]{1,0:T(2,128)(2,1)S(1)}...) all-reduce(bf16[1,256]{1,0:T(2,128)(2,1)S(1)} %stack.185, ...), channel_id=1, replica_groups=mesh['seq'=4,'shard'=2,'dp'=16] {'dp'}, use_global_device_ids=true, to_apply=%region_49.50 | all-reduce | flops 3072 | bytes 12288 | tf_op jit(solution)/shard_map/psum | solution.py:311
  2035.1 29.1 %all-reduce.21.cloned.1.call-done = (bf16[1,128,3072]{2,1,0:T(8,128)(2,1)}, bf16[1,128,3072]{2,1,0:T(8,128)(2,1)}, bf16[1,128,1024]{2,1,0:T(8,128)(2,1)}, bf16[1...) async-done(((bf16[1,128,3072]{2,1,0:T(8,128)(2,1)}, ...) | async-done | bytes 6291472 | tf_op jit(solution)/shard_map/psum | solution.py:307
  (389 shorter events, 358.6 us)
Async XLA Ops:
  7.2 95.9 %all-gather.42.cloned.1.call-start = ((), (), s32[]{:S(2)}) async-start(), calls=%async_computation.20 | async-start | bytes 7077888 | tf_op jit(solution)/shard_map/all_gather | solution.py:82
  10.0 241.8 %all-gather.44.cloned.1.call-start = ((), (), s32[]{:S(2)}) async-start(), calls=%async_computation.21 | async-start | bytes 3276800 | tf_op jit(solution)/shard_map/all_gather | solution.py:125
  113.0 144.3 %all-gather.46.cloned.1.call-start = ((), (), s32[]{:S(2)}) async-start(), calls=%async_computation.22 | async-start | bytes 3276800 | tf_op jit(solution)/shard_map/all_gather | solution.py:124
  114.0 154.5 %all-gather.48.cloned.1.call-start = ((), (), s32[]{:S(2)}) async-start(), calls=%async_computation.23 | async-start | bytes 2359296 | tf_op jit(solution)/shard_map/all_gather | solution.py:83
  116.0 232.1 %all-gather.50.cloned.1.call-start = ((), (), s32[]{:S(2)}) async-start(), calls=%async_computation.24 | async-start | bytes 9437184 | tf_op jit(solution)/shard_map/all_gather | solution.py:84
  117.6 133.5 %copy-start.32 = (bf16[2,80,1,16,64]{4,3,2,1,0:T(8,128)(2,1)S(1)}, bf16[2,80,1,16,64]{4,3,2,1,0:T(8,128)(2,1)}, u32[]{:S(2)}) copy-start(bf16[2,80,1,16,64]{4,3,2,1,0:T(8,128)(2,1)} %get-tuple-element.83) | copy-start | bytes 983044
  117.6 338.3 %all-gather.52.cloned.1.call-start = ((), (), s32[]{:S(2)}) async-start(), calls=%async_computation.25 | async-start | bytes 9437184 | tf_op jit(solution)/shard_map/all_gather | solution.py:85
  120.8 424.3 %all-gather.54.cloned.1.call-start = ((), (), s32[]{:S(2)}) async-start(), calls=%async_computation.26 | async-start | bytes 7077888 | tf_op jit(solution)/shard_map/all_gather | solution.py:82
  121.5 513.2 %all-gather.56.cloned.1.call-start = ((), (), s32[]{:S(2)}) async-start(), calls=%async_computation.27 | async-start | bytes 3276800 | tf_op jit(solution)/shard_map/all_gather | solution.py:125
  462.1 220.7 %copy-start.9 = (f32[160,1024]{1,0:T(8,128)}, f32[160,1024]{1,0:T(8,128)S(1)}, u32[]{:S(2)}) copy-start(f32[160,1024]{1,0:T(8,128)S(1)} %get-tuple-element.123) | copy-start | bytes 1966084
  555.4 84.6 %all-gather.58.cloned.1.call-start = ((), (), s32[]{:S(2)}) async-start(), calls=%async_computation.28 | async-start | bytes 3276800 | tf_op jit(solution)/shard_map/all_gather | solution.py:124
  557.6 125.2 %all-gather.60.cloned.1.call-start = ((), (), s32[]{:S(2)}) async-start(), calls=%async_computation.29 | async-start | bytes 2359296 | tf_op jit(solution)/shard_map/all_gather | solution.py:83
  558.2 232.0 %all-gather.62.cloned.1.call-start = ((), (), s32[]{:S(2)}) async-start(), calls=%async_computation.30 | async-start | bytes 9437184 | tf_op jit(solution)/shard_map/all_gather | solution.py:84
  558.9 339.1 %all-gather.64.cloned.1.call-start = ((), (), s32[]{:S(2)}) async-start(), calls=%async_computation.31 | async-start | bytes 9437184 | tf_op jit(solution)/shard_map/all_gather | solution.py:85
  559.5 393.2 %reduce-scatter.37.cloned.1.call-start = ((), (), s32[]{:S(2)}) async-start(), calls=%async_computation.32 | async-start | bytes 1638400
  651.6 145.2 %copy-start.27 = (bf16[160,1024]{1,0:T(8,128)(2,1)}, bf16[160,1024]{1,0:T(8,128)(2,1)S(1)}, u32[]{:S(2)}) copy-start(bf16[160,1024]{1,0:T(8,128)(2,1)S(1)} %reshape.257) | copy-start | bytes 983044
  790.2 107.8 %copy-start.45 = (bf16[160,1024]{1,0:T(8,128)(2,1)S(1)}, bf16[160,1024]{1,0:T(8,128)(2,1)}, u32[]{:S(2)}) copy-start(bf16[160,1024]{1,0:T(8,128)(2,1)} %get-tuple-element.93) | copy-start | bytes 983044
  930.8 48.4 %reduce-scatter.39.cloned.1.call-start = ((), (), s32[]{:S(2)}) async-start(), calls=%async_computation.33 | async-start | bytes 1638400
  946.0 127.8 %reduce-scatter.41.cloned.1.call-start = ((), (), s32[]{:S(2)}) async-start(), calls=%async_computation.34 | async-start | bytes 1638400
  1024.7 52.0 %reduce-scatter.43.cloned.1.call-start = ((), (), s32[]{:S(2)}) async-start(), calls=%async_computation.35 | async-start | bytes 1638400
  1040.0 114.6 %reduce-scatter.27.cloned.1.call-start = ((), (), s32[]{:S(2)}) async-start(), calls=%async_computation.15 | async-start | bytes 2359296 | tf_op jit(solution)/shard_map/reduce_scatter | solution.py:272
  1043.3 189.3 %reduce-scatter.25.cloned.1.call-start = ((), (), s32[]{:S(2)}) async-start(), calls=%async_computation.14 | async-start | bytes 2359296 | tf_op jit(solution)/shard_map/reduce_scatter | solution.py:272
  1046.7 288.0 %reduce-scatter.23.cloned.1.call-start = ((), (), s32[]{:S(2)}) async-start(), calls=%async_computation.13 | async-start | bytes 7077888 | tf_op jit(solution)/shard_map/reduce_scatter | solution.py:269
  1052.9 398.6 %reduce-scatter.31.cloned.1.call-start = ((), (), s32[]{:S(2)}) async-start(), calls=%async_computation.17 | async-start | bytes 9437184 | tf_op jit(solution)/shard_map/reduce_scatter | solution.py:275
  1060.1 507.7 %reduce-scatter.35.cloned.1.call-start = ((), (), s32[]{:S(2)}) async-start(), calls=%async_computation.19 | async-start | bytes 9437184 | tf_op jit(solution)/shard_map/reduce_scatter | solution.py:278
  1067.8 600.3 %reduce-scatter.21.cloned.1.call-start = ((), (), s32[]{:S(2)}) async-start(), calls=%async_computation.12 | async-start | bytes 7077888 | tf_op jit(solution)/shard_map/reduce_scatter | solution.py:269
  1088.8 696.4 %reduce-scatter.29.cloned.1.call-start = ((), (), s32[]{:S(2)}) async-start(), calls=%async_computation.16 | async-start | bytes 9437184 | tf_op jit(solution)/shard_map/reduce_scatter | solution.py:275
  1095.9 805.8 %reduce-scatter.33.cloned.1.call-start = ((), (), s32[]{:S(2)}) async-start(), calls=%async_computation.18 | async-start | bytes 9437184 | tf_op jit(solution)/shard_map/reduce_scatter | solution.py:278
  1104.4 959.9 %all-reduce.21.cloned.1.call-start = ((), (), s32[]{:S(2)}) async-start(), calls=%async_computation.36 | async-start | bytes 12582912 | tf_op jit(solution)/shard_map/psum | solution.py:307
  1927.3 106.7 %copy-start.12 = (f32[160,1024]{1,0:T(8,128)S(1)}, f32[160,1024]{1,0:T(8,128)}, u32[]{:S(2)}) copy-start(f32[160,1024]{1,0:T(8,128)} %copy-done.11) | copy-start | bytes 1966084
  1927.3 106.7 %copy-start.49 = (f32[160]{0:T(256)S(1)}, f32[160]{0:T(256)}, u32[]{:S(2)}) copy-start(f32[160]{0:T(256)} %copy-done.48) | copy-start | bytes 1924
  1927.3 106.7 %copy-start.51 = (f32[160]{0:T(256)S(1)}, f32[160]{0:T(256)}, u32[]{:S(2)}) copy-start(f32[160]{0:T(256)} %copy-done.50) | copy-start | bytes 1924
  (57 other events, 1046.0 us)
Sparse Core Ops, SparseCore 0:
  10.9 92.1 all-gather.41
  113.1 33.6 all-gather.43
  149.0 35.5 all-gather.45
  186.8 53.4 all-gather.47
  243.1 105.0 all-gather.49
  350.9 105.0 all-gather.51
  458.2 86.8 all-gather.53
  555.6 33.6 all-gather.55
  591.5 35.3 all-gather.57
  629.1 53.6 all-gather.59
  685.2 105.0 all-gather.61
  793.0 105.0 all-gather.63
  930.9 21.7 reduce-scatter.36
  955.0 24.0 reduce-scatter.38
  1024.8 24.3 reduce-scatter.40
  1051.5 24.2 reduce-scatter.42
  1079.9 74.5 reduce-scatter.26
  1158.7 73.8 reduce-scatter.24
  1236.5 98.1 reduce-scatter.22
  1338.4 113.1 reduce-scatter.30
  1455.9 111.8 reduce-scatter.34
  1571.6 96.4 reduce-scatter.20
  1671.9 113.2 reduce-scatter.28
  1789.4 112.3 reduce-scatter.32
  1904.8 159.3 all-reduce.20
where the time goes:
time: 2090 us; the launch traced here: 2080 us
  waiting for transfers between devices  1380 us (66%)
  blocking collectives  382 us (18%)
  matrix products  155 us (7%)
  local copies, waits for them, and re-layouts  127 us (6%)
  other arithmetic  21.6 us (1%)
    reduce_scatter x2, waiting for transfers between devices, per_device(): lax.psum_scatter(grad_w_up.astype(jnp.bfloat16), ('seq', 'shard'), scatte...  234 us
    reduce_scatter x2, waiting for transfers between devices, per_device(): lax.psum_scatter(grad_w_down.astype(jnp.bfloat16), ('seq', 'shard'), scat...  233 us
    all_gather x2, waiting for transfers between devices, per_device(): lax.all_gather(weight_down[layer_at], ('seq', 'shard'), axis=0, tiled=True)  203 us
    reduce_scatter x2, waiting for transfers between devices, per_device(): lax.psum_scatter(grad_w_qkv.astype(jnp.bfloat16), ('seq', 'shard'), scatt...  202 us
    all_gather x2, waiting for transfers between devices, per_device(): lax.all_gather(weight_up[layer_at], ('seq', 'shard'), axis=0, tiled=True)  182 us
    reduce_scatter x2, waiting for transfers between devices, per_device(): lax.psum_scatter(grad_w_out.astype(jnp.bfloat16), ('seq', 'shard'), scatt...  128 us
    all_gather x2, waiting for transfers between devices, per_device(): lax.all_gather(weight_qkv[layer_at], ('seq', 'shard'), axis=0, tiled=True)  106 us
    unnamed x152, local copies, waits for them, and re-layouts  66.2 us
  transfers between devices with their start and end apart: 25, of which 18 were waited for; matrix products, arithmetic and copies ran while one was open for 9% of the time, Pallas kernels for 0%

commit v1 on v0

v1 whole, which is shorter than its diff:
```python
import functools
import math

import jax
import jax.numpy as jnp
from jax import lax
from jax.experimental import pallas as pl
from jax.experimental.pallas import tpu as pltpu
from jax.sharding import Mesh
from jax.sharding import PartitionSpec as P

AXES = ("z", "xh", "y", "xl", "core")
RING = 4
ORDERS = ("xyz", "zxy", "yzx", "yzx")


def positions():
    return {
        "z": lax.axis_index("z"),
        "x": lax.axis_index("xh") * 2 + lax.axis_index("xl"),
        "y": lax.axis_index("y"),
    }


def neighbour(pos, axis, step):
    at = lax.rem(pos[axis] + step + RING, RING)
    if axis == "x":
        return {"xh": at // 2, "xl": lax.rem(at, 2)}
    return {axis: at}


def remote(src, dst, send, recv, target):
    return pltpu.make_async_remote_copy(
        src_ref=src,
        dst_ref=dst,
        send_sem=send,
        recv_sem=recv,
        device_id=target,
        device_id_type=pl.DeviceIdType.MESH,
    )


def greet(pos, with_column):
    barrier = pltpu.get_barrier_semaphore()
    targets = [neighbour(pos, axis, step) for axis in "xyz" for step in (1, -1)]
    if with_column:
        targets.append(neighbour(pos, "z", 2))
    targets.append({"core": 1 - lax.axis_index("core")})
    for target in targets:
        pl.semaphore_signal(
            barrier, inc=1, device_id=target, device_id_type=pl.DeviceIdType.MESH
        )
    pl.semaphore_wait(barrier, len(targets))


def half(ref, which, rows, cols):
    lead = (slice(None),) * (len(ref.shape) - 2)
    if rows % 16 == 0:
        return ref.at[lead + (pl.ds(which * (rows // 2), rows // 2), slice(None))]
    return ref.at[lead + (slice(None), pl.ds(which * (cols // 2), cols // 2))]


class Gather:
    def __init__(self, pos, order, own, full, send, recv):
        self.pos, self.order, self.own, self.full = pos, order, own, full
        self.send, self.recv = send, recv
        self.rows, self.cols = full.shape[-2:]

    def view(self, stage, shift):
        index = {}
        for place, axis in enumerate(self.order):
            if place < stage:
                index[axis] = slice(None)
            elif place == stage:
                index[axis] = lax.rem(self.pos[axis] + shift + RING, RING)
            else:
                index[axis] = self.pos[axis]
        return self.full.at[index["z"], index["x"], index["y"]]

    def copy(self, stage, kind):
        axis = self.order[stage]
        sems = (self.send.at[stage * 4 + kind], self.recv.at[stage * 4 + kind])
        target = neighbour(self.pos, axis, 1 if kind % 2 == 0 else -1)
        if kind < 2:
            src = self.own if stage == 0 else self.view(stage, 0)
            return remote(src, self.view(stage, 0), *sems, target)
        piece = half(self.view(stage, -1 if kind == 2 else 1), kind - 2, self.rows, self.cols)
        return remote(piece, piece, *sems, target)

    def arrive(self, stage, kind):
        sems = (self.send.at[stage * 4 + kind], self.recv.at[stage * 4 + kind])
        axis = self.order[stage]
        if kind < 2:
            piece = self.view(stage, -1 if kind == 0 else 1)
        else:
            piece = half(self.view(stage, 2), kind - 2, self.rows, self.cols)
        remote(piece, piece, *sems, neighbour(self.pos, axis, 1)).wait_recv()

    def begin(self, stage):
        for kind in (0, 1):
            self.copy(stage, kind).start()

    def onward(self, stage):
        for kind in (0, 1):
            self.arrive(stage, kind)
            self.copy(stage, kind + 2).start()

    def finish(self, stage):
        for kind in (2, 3):
            self.arrive(stage, kind)

    def drain(self):
        for stage in range(3):
            for kind in range(4):
                self.copy(stage, kind).wait_send()


def gather_kernel(count, moved, *refs):
    owns, parts = refs[:count], refs[count : count + moved]
    refs = refs[count + moved :]
    fulls, wholes = refs[:count], refs[count : count + moved]
    send, recv, local, send_t, recv_t, core_s, core_r, local_t = refs[count + moved :]
    pos = positions()
    core = lax.axis_index("core")
    greet(pos, True)
    for a in range(moved):
        for b in range(2):
            home = 2 * core + b
            here = home == pos["z"]

            @pl.when(here)
            def _():
                pltpu.make_async_copy(
                    parts[a].at[b], wholes[a].at[pos["z"]], local_t.at[a]
                ).start()

            @pl.when(jnp.logical_not(here))
            def _():
                remote(
                    parts[a].at[b],
                    wholes[a].at[pos["z"]],
                    send_t.at[a, b],
                    recv_t.at[a, pos["z"]],
                    {"z": home},
                ).start()

    streams = []
    for m in range(count):
        pltpu.make_async_copy(
            owns[m], fulls[m].at[pos["z"], pos["x"], pos["y"]], local.at[m]
        ).start()
        streams.append(
            Gather(pos, ORDERS[m % 4], owns[m], fulls[m], send.at[m], recv.at[m])
        )
    for s in streams:
        s.begin(0)
    receiver = pos["z"] // 2 == core

    def crossing(a, q):
        return remote(
            wholes[a].at[q],
            wholes[a].at[q],
            core_s.at[a, q],
            core_r.at[a, q],
            {"core": 1 - core},
        )

    @pl.when(receiver)
    def _():
        for a in range(moved):
            for q in range(RING):

                @pl.when(q == pos["z"])
                def _():
                    pltpu.make_async_copy(
                        parts[a].at[0], wholes[a].at[q], local_t.at[a]
                    ).wait()

                @pl.when(q != pos["z"])
                def _():
                    remote(
                        wholes[a].at[q],
                        wholes[a].at[q],
                        send_t.at[a, 0],
                        recv_t.at[a, q],
                        {"z": lax.rem(pos["z"] + 1, RING)},
                    ).wait_recv()

                crossing(a, q).start()

    for stage in range(3):
        for s in streams:
            s.onward(stage)
        for m, s in enumerate(streams):
            if stage == 0:
                pltpu.make_async_copy(
                    owns[m], fulls[m].at[pos["z"], pos["x"], pos["y"]], local.at[m]
                ).wait()
            s.finish(stage)
            if stage < 2:
                s.begin(stage + 1)
    for s in streams:
        s.drain()
    for a in range(moved):
        for b in range(2):

            @pl.when(2 * core + b != pos["z"])
            def _():
                remote(
                    parts[a].at[b],
                    wholes[a].at[pos["z"]],
                    send_t.at[a, b],
                    recv_t.at[a, pos["z"]],
                    {"z": lax.rem(pos["z"] + 1, RING)},
                ).wait_send()

        for q in range(RING):

            @pl.when(receiver)
            def _():
                crossing(a, q).wait_send()

            @pl.when(jnp.logical_not(receiver))
            def _():
                crossing(a, q).wait_recv()


def gather_all(owns, parts):
    count, moved = len(owns), len(parts)
    anyspec = pl.BlockSpec(memory_space=pl.ANY)
    shapes = [jax.ShapeDtypeStruct((RING, RING, RING) + o.shape, o.dtype) for o in owns]
    shapes += [jax.ShapeDtypeStruct((RING,) + p.shape[1:], p.dtype) for p in parts]
    dma = pltpu.SemaphoreType.DMA
    out = pl.pallas_call(
        functools.partial(gather_kernel, count, moved),
        out_shape=shapes,
        in_specs=[anyspec] * (count + moved),
        out_specs=[anyspec] * (count + moved),
        scratch_shapes=[
            dma((count, 12)),
            dma((count, 12)),
            dma((count,)),
            dma((moved, 2)),
            dma((moved, RING)),
            dma((moved, RING)),
            dma((moved, RING)),
            dma((moved,)),
        ],
        compiler_params=pltpu.CompilerParams(collective_id=0, has_side_effects=True),
        name="gather_all",
    )(*owns, *parts)
    return out[:count], out[count:]


class Scatter:
    def __init__(self, pos, order, grad, bufs, final, send, recv, local, sends_f, recvs_f):
        self.pos, self.order, self.grad, self.final = pos, order, grad, final
        self.own, self.boxes, self.sums = bufs[0], bufs[1:4], bufs[4:7]
        self.send, self.recv, self.local = send, recv, local
        self.sends_f, self.recvs_f = sends_f, recvs_f
        self.rows, self.cols = grad.shape[-2:]
        self.part = self.cols // 2
        self.core = lax.axis_index("core")
        self.xl = lax.axis_index("xl")

    def piece(self, stage, shift, which=None):
        axis = self.order[stage]
        left = [a for a in "zxy" if a in self.order[stage:]]
        source = self.grad if stage == 0 else self.sums[stage - 1]
        at = lax.rem(self.pos[axis] + shift + RING, RING)
        index = tuple(at if a == axis else slice(None) for a in left) + (slice(None),)
        if which is None:
            return source.at[index + (slice(None),)]
        return source.at[index + (pl.ds(which * self.part, self.part),)]

    def box(self, stage, kind):
        return self.boxes[stage].at[kind]

    def copy(self, stage, kind):
        src, step = {
            0: (lambda: self.piece(stage, 2, 0), 1),
            1: (lambda: self.piece(stage, 1, 1), 1),
            2: (lambda: self.piece(stage, -2, 1), -1),
            3: (lambda: self.piece(stage, -1, 0), -1),
            4: (lambda: self.box(stage, 0), 1),
            5: (lambda: self.box(stage, 2), -1),
        }[kind]
        return remote(
            src(),
            self.box(stage, kind),
            self.send.at[stage * 6 + kind],
            self.recv.at[stage * 6 + kind],
            neighbour(self.pos, self.order[stage], step),
        )

    def loads(self):
        for slot, (shift, which) in enumerate(((1, 0), (-1, 1), (0, 0), (0, 1))):
            yield pltpu.make_async_copy(
                self.piece(0, shift, which), self.own.at[slot], self.local.at[slot]
            )

    def begin(self, stage):
        for kind in range(4):
            self.copy(stage, kind).start()
        if stage == 0:
            for load in self.loads():
                load.start()

    def term(self, stage, slot):
        if stage == 0:
            return self.own.at[slot]
        shift, which = ((1, 0), (-1, 1), (0, 0), (0, 1))[slot]
        return self.piece(stage, shift, which)

    def add(self, stage, target, terms):
        lead = 2 - stage

        def one(index):
            total = terms[0][index].astype(jnp.float32)
            for t in terms[1:]:
                total = total + t[index].astype(jnp.float32)
            target[index] = total.astype(target.dtype)

        if lead == 0:
            one((slice(None), slice(None)))
            return

        def body(i, carry):
            where = (i // RING, lax.rem(i, RING)) if lead == 2 else (i,)
            one(where + (slice(None), slice(None)))
            return carry

        lax.fori_loop(0, RING**lead, body, 0)

    def onward(self, stage):
        if stage == 0:
            for load in self.loads():
                load.wait()
        for slot, kind in ((0, 0), (1, 2)):
            self.copy(stage, kind).wait_recv()
            box = self.box(stage, kind)
            self.add(stage, box, (box, self.term(stage, slot)))
            self.copy(stage, 4 + slot).start()

    def finish(self, stage):
        for kind in (1, 3, 4, 5):
            self.copy(stage, kind).wait_recv()
        lead = (slice(None),) * (3 - stage)
        for which, kinds in ((0, (3, 4)), (1, (1, 5))):
            target = self.sums[stage].at[lead + (pl.ds(which * self.part, self.part),)]
            self.add(
                stage,
                target,
                (self.term(stage, 2 + which),) + tuple(self.box(stage, k) for k in kinds),
            )

    def across_first(self):
        return self.order[0] != "y"

    def block(self, shift):
        yi = lax.rem(self.pos["y"] + shift + RING, RING)
        xs = slice(None) if self.across_first() else self.xl
        return self.final.at[self.core, xs, yi]

    def spread(self, kind, own=False):
        sems = (self.sends_f.at[kind], self.recvs_f.at[kind])
        if kind == 5:
            whole = self.final.at[self.core]
            return remote(whole, whole, *sems, {"core": 1 - self.core})
        if kind == 4:
            if self.across_first():
                dst = self.final.at[self.core, self.xl, self.pos["y"]]
                src = self.sums[2]
            else:
                src = dst = self.final.at[self.core, self.xl]
            return remote(src, dst, *sems, {"xl": 1 - self.xl})
        target = neighbour(self.pos, "y", 1 if kind % 2 == 0 else -1)
        if kind < 2:
            dst = self.block(0)
            src = dst if self.across_first() else self.sums[2]
            return remote(src, dst, *sems, target)
        ref = self.block(-1 if kind == 2 else 1)
        lead = (slice(None),) * (len(ref.shape) - 1)
        ref = ref.at[lead + (pl.ds((kind - 2) * self.part, self.part),)]
        return remote(ref, ref, *sems, target)

    def spread_arrives(self, kind):
        sems = (self.sends_f.at[kind], self.recvs_f.at[kind])
        if kind == 5:
            ref = self.final.at[1 - self.core]
        elif kind == 4:
            ref = self.final.at[self.core, 1 - self.xl]
            if self.across_first():
                ref = ref.at[self.pos["y"]]
        elif kind < 2:
            ref = self.block(-1 if kind == 0 else 1)
        else:
            ref = self.block(2)
            lead = (slice(None),) * (len(ref.shape) - 1)
            ref = ref.at[lead + (pl.ds((kind - 2) * self.part, self.part),)]
        remote(ref, ref, *sems, {"core": 1 - self.core}).wait_recv()

    def keep(self):
        return pltpu.make_async_copy(
            self.sums[2],
            self.final.at[self.core, self.xl, self.pos["y"]],
            self.local.at[4],
        )

    def publish(self, step):
        if step == 0:
            self.keep().start()
            for kind in (4,) if self.across_first() else (0, 1):
                self.spread(kind).start()
            self.keep().wait()
        elif self.across_first():
            if step == 1:
                self.spread_arrives(4)
                for kind in (0, 1):
                    self.spread(kind).start()
            elif step == 2:
                for kind in (0, 1):
                    self.spread_arrives(kind)
                    self.spread(kind + 2).start()
            elif step == 3:
                for kind in (2, 3):
                    self.spread_arrives(kind)
        else:
            if step == 1:
                for kind in (0, 1):
                    self.spread_arrives(kind)
                    self.spread(kind + 2).start()
            elif step == 2:
                for kind in (2, 3):
                    self.spread_arrives(kind)
                self.spread(4).start()
            elif step == 3:
                self.spread_arrives(4)
        if step == 3:
            self.spread(5).start()
        if step == 4:
            self.spread_arrives(5)

    def drain(self):
        for stage in range(3):
            for kind in range(6):
                self.copy(stage, kind).wait_send()
        for kind in range(6):
            self.spread(kind).wait_send()


def scatter_kernel(count, moved, *refs):
    grads, wholes = refs[:count], refs[count : count + moved]
    refs = refs[count + moved :]
    finals, parts = refs[:count], refs[count : count + moved]
    refs = refs[count + moved :]
    bufs, refs = refs[: 7 * count], refs[7 * count :]
    send, recv, local, sends_f, recvs_f, send_t, recv_t, local_t = refs
    pos = positions()
    core = lax.axis_index("core")
    greet(pos, True)
    streams = [
        Scatter(
            pos,
            ORDERS[m % 4],
            grads[m],
            bufs[7 * m : 7 * m + 7],
            finals[m],
            send.at[m],
            recv.at[m],
            local.at[m],
            sends_f.at[m],
            recvs_f.at[m],
        )
        for m in range(count)
    ]
    for s in streams:
        s.begin(0)
    sender = pos["z"] // 2 == core
    slot = lax.rem(pos["z"], 2)

    def homeward(a, q):
        return remote(
            wholes[a].at[q], parts[a].at[slot], send_t.at[a, q], recv_t.at[a, slot], {"z": q}
        )

    def staying(a):
        return pltpu.make_async_copy(wholes[a].at[pos["z"]], parts[a].at[slot], local_t.at[a])

    for a in range(moved):
        for q in range(RING):

            @pl.when(sender & (pos["z"] == q))
            def _():
                staying(a).start()

            @pl.when(sender & (pos["z"] != q))
            def _():
                homeward(a, q).start()

    for stage in range(3):
        for s in streams:
            s.onward(stage)
        for s in streams:
            s.finish(stage)
            if stage < 2:
                s.begin(stage + 1)
            else:
                s.publish(0)
    for step in range(1, 5):
        for s in streams:
            s.publish(step)
    for s in streams:
        s.drain()
    for a in range(moved):
        for q in range(RING):

            @pl.when(sender & (pos["z"] == q))
            def _():
                staying(a).wait()

            @pl.when(sender & (pos["z"] != q))
            def _():
                homeward(a, q).wait_send()

        for b in range(2):

            @pl.when(2 * core + b != pos["z"])
            def _():
                remote(
                    parts[a].at[b],
                    parts[a].at[b],
                    send_t.at[a, 0],
                    recv_t.at[a, b],
                    {"z": lax.rem(pos["z"] + 1, RING)},
                ).wait_recv()


def scatter_all(grads, wholes):
    count, moved = len(grads), len(wholes)
    anyspec = pl.BlockSpec(memory_space=pl.ANY)
    shapes = [jax.ShapeDtypeStruct((2, 2, RING) + g.shape[3:], g.dtype) for g in grads]
    shapes += [jax.ShapeDtypeStruct((2,) + w.shape[1:], w.dtype) for w in wholes]
    dma = pltpu.SemaphoreType.DMA
    scratch = []
    for g in grads:
        r, c = g.shape[3:]
        scratch.append(pltpu.VMEM((4, RING, RING, r, c // 2), g.dtype))
        for lead in ((RING, RING), (RING,), ()):
            scratch.append(pltpu.VMEM((6,) + lead + (r, c // 2), g.dtype))
        for lead in ((RING, RING), (RING,), ()):
            scratch.append(pltpu.VMEM(lead + (r, c), g.dtype))
    out = pl.pallas_call(
        functools.partial(scatter_kernel, count, moved),
        out_shape=shapes,
        in_specs=[anyspec] * (count + moved),
        out_specs=[anyspec] * (count + moved),
        scratch_shapes=scratch
        + [
            dma((count, 18)),
            dma((count, 18)),
            dma((count, 5)),
            dma((count, 6)),
            dma((count, 6)),
            dma((moved, RING)),
            dma((moved, 2)),
            dma((moved,)),
        ],
        compiler_params=pltpu.CompilerParams(
            collective_id=1, has_side_effects=True, vmem_limit_bytes=62 * 1024 * 1024
        ),
        name="scatter_all",
    )(*grads, *wholes)
    return out[:count], out[count:]


NORM_EPS = 1e-05
GELU_COEF = 0.7978845608028654
CUBIC_COEF = 0.044715
HEAD_DIM = 64
LOW = jnp.bfloat16
F32 = jnp.float32


def dot(left, right, dims=((1,), (0,))):
    return lax.dot_general(left, right, (dims, ((), ())), preferred_element_type=F32)


def head_probs(q, k, allowed, scale):
    scores = jnp.where(allowed, dot(q, k, ((1,), (1,))) * scale, -jnp.inf)
    top = jnp.max(scores, axis=-1, keepdims=True)
    lse = top + jnp.log(jnp.sum(jnp.exp(scores - top), axis=-1, keepdims=True))
    return jnp.exp(scores - lse)


def allowed_pairs(seg_col, seg_row):
    length = seg_col.shape[0]
    row = lax.broadcasted_iota(jnp.int32, (length, length), 0)
    col = lax.broadcasted_iota(jnp.int32, (length, length), 1)
    return (row >= col) & (seg_col == seg_row)


def attention_kernel(qkv_ref, seg_col_ref, seg_row_ref, attn_ref):
    width = attn_ref.shape[1]
    scale = 1.0 / math.sqrt(HEAD_DIM)
    allowed = allowed_pairs(seg_col_ref[...], seg_row_ref[...])
    for h in range(width // HEAD_DIM):
        q, k, v = (
            qkv_ref[:, pl.ds(t * width + h * HEAD_DIM, HEAD_DIM)] for t in range(3)
        )
        probs = head_probs(q, k, allowed, scale).astype(LOW)
        attn_ref[:, pl.ds(h * HEAD_DIM, HEAD_DIM)] = dot(probs, v).astype(LOW)


def attention_back_kernel(qkv_ref, attn_ref, grad_ref, seg_col_ref, seg_row_ref, out_ref, sum_ref):
    width = attn_ref.shape[1]
    scale = 1.0 / math.sqrt(HEAD_DIM)
    allowed = allowed_pairs(seg_col_ref[...], seg_row_ref[...])
    for h in range(width // HEAD_DIM):
        q, k, v = (
            qkv_ref[:, pl.ds(t * width + h * HEAD_DIM, HEAD_DIM)] for t in range(3)
        )
        here = pl.ds(h * HEAD_DIM, HEAD_DIM)
        d_attn = grad_ref[:, here]
        full = head_probs(q, k, allowed, scale)
        delta = jnp.sum(
            d_attn.astype(F32) * attn_ref[:, here].astype(F32), axis=-1, keepdims=True
        )
        d_scores = (full * (dot(d_attn, v, ((1,), (1,))) - delta)).astype(LOW)
        terms = (
            dot(d_scores, k) * scale,
            dot(d_scores, q, ((0,), (0,))) * scale,
            dot(full.astype(LOW), d_attn, ((0,), (0,))),
        )
        for t, term in enumerate(terms):
            place = pl.ds(t * width + h * HEAD_DIM, HEAD_DIM)
            out_ref[:, place] = term.astype(LOW)
            sum_ref[:, place] = jnp.sum(term, axis=0, keepdims=True)


def attention(qkv, seg_col, seg_row):
    length, width = qkv.shape[0], qkv.shape[1] // 3
    return pl.pallas_call(
        attention_kernel,
        out_shape=jax.ShapeDtypeStruct((length, width), LOW),
        name="attention",
    )(qkv, seg_col, seg_row)


def attention_back(qkv, attn, d_attn, seg_col, seg_row):
    length, width = attn.shape
    return pl.pallas_call(
        attention_back_kernel,
        out_shape=(
            jax.ShapeDtypeStruct((length, 3 * width), LOW),
            jax.ShapeDtypeStruct((1, 3 * width), F32),
        ),
        name="attention_back",
    )(qkv, attn, d_attn, seg_col, seg_row)


def layer_norm(state, gain, shift):
    center = state - jnp.mean(state, axis=-1, keepdims=True)
    factor = lax.rsqrt(jnp.mean(center * center, axis=-1, keepdims=True) + NORM_EPS)
    normed = center * factor
    return normed, factor, (normed * gain + shift).astype(LOW)


def norm_backward(d_act, normed, factor, gain):
    d_norm = d_act * gain
    return factor * (
        d_norm
        - jnp.mean(d_norm, axis=-1, keepdims=True)
        - normed * jnp.mean(d_norm * normed, axis=-1, keepdims=True)
    )


def gelu_pair(pre_act):
    cubic = pre_act * pre_act * pre_act
    tangent = jnp.tanh(GELU_COEF * (pre_act + CUBIC_COEF * cubic))
    gelu_value = 0.5 * pre_act * (1.0 + tangent)
    gelu_slope = 0.5 * (1.0 + tangent) + 0.5 * pre_act * (1.0 - tangent * tangent) * GELU_COEF * (
        1.0 + 3.0 * CUBIC_COEF * pre_act * pre_act
    )
    return gelu_value, gelu_slope


def pair_sum(partial):
    return partial + lax.ppermute(partial, "core", ((0, 1), (1, 0)))


def pick(array, at, axis):
    return lax.dynamic_index_in_dim(array, at, axis, keepdims=False)


def per_device(
    inputs,
    segment_ids,
    weight_qkv,
    weight_out,
    weight_up,
    weight_down,
    bias_qv,
    bias_out,
    bias_up,
    bias_down,
    gain_one,
    shift_one,
    gain_two,
    shift_two,
    cotangent,
):
    layers, rows, _ = weight_qkv.shape
    width = inputs.shape[-1]
    inner = weight_up.shape[-1]
    length = inputs.shape[1] * RING
    core = lax.axis_index("core")
    sub = lax.axis_index("xl") * 4 + lax.axis_index("y")
    owns = []
    for l in range(layers):
        up = pick(weight_up[l].reshape(8, rows // 8, 8, 2, inner // 16), sub, 0)
        owns.append(pick(up, core, 2).reshape(rows // 8, inner // 2))
        down = weight_down[l].reshape(2, 8, inner // 128, width)
        owns.append(pick(pick(down, core, 0), sub, 0))
        qkv = pick(weight_qkv[l].reshape(8, rows // 8, 24, 2, HEAD_DIM), sub, 0)
        owns.append(pick(qkv, core, 2).reshape(rows // 8, 3 * width // 2))
        out = weight_out[l].reshape(2, 8, rows // 16, width)
        owns.append(pick(pick(out, core, 0), sub, 0))
    vectors = (bias_qv, bias_out, bias_up, bias_down, gain_one, shift_one, gain_two, shift_two)
    sizes = [v.shape[1] for v in vectors]
    total = sum(sizes)
    packed = jnp.concatenate(vectors, axis=1).reshape(8, layers * total // 8)
    packed = jnp.pad(pick(packed, sub, 0), (0, 2048 - layers * total // 8))
    owns.append(packed.reshape(8, 256))
    segs = jnp.pad(segment_ids.astype(F32), ((0, 0), (0, 1024 - segment_ids.shape[1])))
    fulls, wholes = gather_all(owns, [inputs, cotangent, segs.reshape(2, 8, 128)])
    state = wholes[0].reshape(length, width)
    grad_state = wholes[1].reshape(length, width)
    seg = wholes[2].reshape(RING, 1024)[:, : length // RING].reshape(length)
    seg_col, seg_row = seg[:, None], seg[None, :]
    packed = fulls[-1].reshape(8, 8, 2048)[:, :, : layers * total // 8].reshape(8, layers, total)
    packed = packed.astype(F32)
    params = []
    for l in range(layers):
        weights = [w.reshape(-1, w.shape[-1]) for w in fulls[4 * l : 4 * l + 4]]
        offset, vecs = 0, []
        for size in sizes:
            vecs.append(packed[:, l, offset : offset + size].reshape(8 * size))
            offset += size
        b_qv = pick(vecs[0].reshape(2, 8, 2, HEAD_DIM), core, 2).reshape(2, width // 2)
        b_qkv = jnp.concatenate([b_qv[0], jnp.zeros((width // 2,), F32), b_qv[1]])
        b_up = pick(vecs[2].reshape(8, 2, inner // 16), core, 1).reshape(inner // 2)
        params.append((weights, b_qkv, vecs[1], b_up, vecs[3], vecs[4:]))
    records = []
    for l in range(layers):
        (w_up, w_down, w_qkv, w_out), b_qkv, b_out, b_up, b_down, (g1, s1, g2, s2) = params[l]
        norm_one, factor_one, act_one = layer_norm(state, g1, s1)
        qkv = (dot(act_one, w_qkv) + b_qkv).astype(LOW)
        attn = attention(qkv, seg_col, seg_row)
        middle = state + pair_sum(dot(attn, w_out)) + b_out
        norm_two, factor_two, act_two = layer_norm(middle, g2, s2)
        gelu_value, gelu_slope = gelu_pair(dot(act_two, w_up) + b_up)
        hidden = gelu_value.astype(LOW)
        state = middle + pair_sum(dot(hidden, w_down)) + b_down
        records.append(
            (norm_one, factor_one, act_one, qkv, attn, norm_two, factor_two, act_two, gelu_slope, hidden)
        )
    grads, small = [None] * layers, [None] * layers
    first = (core == 0).astype(F32)
    for l in reversed(range(layers)):
        (w_up, w_down, w_qkv, w_out), _, _, _, _, (g1, _, g2, _) = params[l]
        norm_one, factor_one, act_one, qkv, attn, norm_two, factor_two, act_two, gelu_slope, hidden = records[l]
        grad_low = grad_state.astype(LOW)
        gb_down = jnp.sum(grad_state, axis=0)
        d_pre = dot(grad_low, w_down, ((1,), (1,))) * gelu_slope
        d_pre_low = d_pre.astype(LOW)
        gb_up = jnp.sum(d_pre, axis=0)
        d_act_two = pair_sum(dot(d_pre_low, w_up, ((1,), (1,))))
        gg_two = jnp.sum(d_act_two * norm_two, axis=0)
        gs_two = jnp.sum(d_act_two, axis=0)
        grad_middle = grad_state + norm_backward(d_act_two, norm_two, factor_two, g2)
        grad_attn_low = grad_middle.astype(LOW)
        gb_out = jnp.sum(grad_middle, axis=0)
        d_attn = dot(grad_attn_low, w_out, ((1,), (1,))).astype(LOW)
        d_qkv, gb_qkv = attention_back(qkv, attn, d_attn, seg_col, seg_row)
        d_act_one = pair_sum(dot(d_qkv, w_qkv, ((1,), (1,))))
        gg_one = jnp.sum(d_act_one * norm_one, axis=0)
        gs_one = jnp.sum(d_act_one, axis=0)
        grad_state = grad_middle + norm_backward(d_act_one, norm_one, factor_one, g1)
        tokens = ((0,), (0,))
        grads[l] = [
            dot(act_two, d_pre_low, tokens),
            dot(hidden, grad_low, tokens),
            dot(act_one, d_qkv, tokens),
            dot(attn, grad_attn_low, tokens),
        ]
        gb_qkv = gb_qkv.reshape(3, 8, HEAD_DIM)
        mine = lambda v, axis: jnp.stack(
            [jnp.where(core == c, v, 0.0) for c in range(2)], axis=axis
        )
        gb_qv = mine(jnp.stack([gb_qkv[0], gb_qkv[2]]), 2)
        gb_up = mine(gb_up.reshape(8, inner // 16), 1)
        parts = (gb_qv, gb_out * first, gb_up, gb_down * first)
        parts += (gg_one * first, gs_one * first, gg_two * first, gs_two * first)
        small[l] = jnp.concatenate(
            [v.reshape(8, size) for v, size in zip(parts, sizes)], axis=1
        )
    small = jnp.stack(small, axis=1).reshape(8, 8, layers * total // 8)
    small = jnp.pad(small, ((0, 0), (0, 0), (0, 2048 - layers * total // 8)))
    pieces = [
        g.astype(LOW).reshape(RING, RING, RING, -1, g.shape[-1]) for l in range(layers) for g in grads[l]
    ]
    pieces.append(small.astype(LOW).reshape(RING, RING, RING, 8, 256))
    finals, parts = scatter_all(
        pieces,
        [state.reshape(RING, length // RING, width), grad_state.reshape(RING, length // RING, width)],
    )
    outs = [[], [], [], []]
    for l in range(layers):
        up, down, qkv, out = (f.astype(F32) for f in finals[4 * l : 4 * l + 4])
        up = up.reshape(2, rows, 8, inner // 16).transpose(1, 2, 0, 3)
        outs[2].append(up.reshape(rows, inner))
        outs[3].append(down.reshape(inner // 8, width))
        qkv = qkv.reshape(2, rows, 24, HEAD_DIM).transpose(1, 2, 0, 3)
        outs[0].append(qkv.reshape(rows, 3 * width))
        outs[1].append(out.reshape(rows, width))
    small = jnp.sum(finals[-1].astype(F32), axis=0).reshape(8, 2048)[:, : layers * total // 8]
    small = small.reshape(layers, total)
    ends = []
    offset = 0
    for size in sizes:
        ends.append(small[:, offset : offset + size])
        offset += size
    return (parts[0], parts[1]) + tuple(jnp.stack(o) for o in outs) + tuple(ends)


def solution(mesh):
    torus = Mesh(mesh.devices.reshape(4, 2, 4, 2, 2), AXES)
    tokens = P(("xh", "y", "xl", "core"), "z", None)
    weight = P(None, ("z", "xh"), None)
    vector = P(None, ("z", "xh"))
    return jax.shard_map(
        per_device,
        mesh=torus,
        in_specs=(tokens, P(("xh", "y", "xl", "core"), "z")) + (weight,) * 4 + (vector,) * 8 + (tokens,),
        out_specs=(tokens, tokens) + (weight,) * 4 + (vector,) * 8,
        check_vma=False,
    )
```

time: 2090 us -> 477 us (0.23)
  waiting for transfers between devices: 1380 us -> 6.54 us
  blocking collectives: 382 us -> 0 us
  Pallas kernels: 0 us -> 295 us
  matrix products: 155 us -> 72.3 us
  local copies, waits for them, and re-layouts: 127 us -> 52.7 us
    reduce_scatter x8 -> x0, waiting for transfers between devices: 797 us -> none  [the longest x2 234 us: per_device(): lax.psum_scatter(grad_w_up.astype(jnp.bfloat16), ('seq', 'shard'), scatte...]
    all_gather x12 -> x0, waiting for transfers between devices: 522 us -> none  [the longest x2 203 us: per_device(): lax.all_gather(weight_down[layer_at], ('seq', 'shard'), axis=0, tiled=True)]
    pallas_call x0 -> x6, Pallas kernels: none -> 295 us  [the longest x1 143 us: scatter_all(): pl.pallas_call(functools.partial(scatter_kernel, count, moved), out_shape...]
    all_gather x17 -> x0, blocking collectives: 286 us -> none  [the longest x2 51.9 us: per_device(): lax.all_gather(bias_up[layer_at], ('seq', 'shard'), axis=0, tiled=True)]
    dot_general x36 -> x24, matrix products: 155 us -> 72.3 us  [dot(): lax.dot_general(left, right, (dims, ((), ())), preferred_element_type=F32)]
    psum x1 -> x0, blocking collectives: 60.1 us -> none  [per_device(): lax.psum(shares[4].astype(jnp.bfloat16), 'dp').astype(jnp.float32)]
    unnamed x152 -> x123, local copies, waits for them, and re-layouts: 66.2 us -> 16.6 us
    unnamed x1 -> x0, blocking collectives: 35 us -> none
  transfers between devices with their start and end apart: 25 -> 8, of which waited for: 18 -> 3; matrix products, arithmetic and copies ran while one was open for 9% -> 8% of each run, Pallas kernels for 0% -> 0%
where the time goes in v1:
time: 477 us; the launch traced here: 471 us
  Pallas kernels  295 us (62%)
  matrix products  72.3 us (15%)
  local copies, waits for them, and re-layouts  52.7 us (11%)
  other arithmetic  39.8 us (8%)
  waiting for transfers between devices  6.54 us (1%)
    pallas_call x1, Pallas kernels, scatter_all(): pl.pallas_call(functools.partial(scatter_kernel, count, moved), out_shape...  143 us
    pallas_call x1, Pallas kernels, gather_all(): pl.pallas_call(functools.partial(gather_kernel, count, moved), out_shape=...  124 us
    dot_general x24, matrix products, dot(): lax.dot_general(left, right, (dims, ((), ())), preferred_element_type=F32)  72.3 us
    unnamed x123, local copies, waits for them, and re-layouts  16.6 us
    pallas_call x2, Pallas kernels, attention_back(): pl.pallas_call(attention_back_kernel, out_shape=(jax.ShapeDtypeStruct((le...  16.5 us
    pallas_call x2, Pallas kernels, attention(): pl.pallas_call(attention_kernel, out_shape=jax.ShapeDtypeStruct((length,...  11.9 us
  transfers between devices with their start and end apart: 8, of which 3 were waited for; matrix products, arithmetic and copies ran while one was open for 8% of the time, Pallas kernels for 0%

profile of v1, /device:TPU:1, one launch (start us, length us, event | category | flops | bytes accessed | tf_op | source)
XLA Modules:
  0.0 470.9 jit_solution(7353866158695023969)
XLA Ops:
  13.1 2.3 dynamic-slice_reduce_fusion
  21.1 123.6 %gather_all.1 = (bf16[4,4,4,16,2048]{4,3,2,1,0:T(8,128)(2,1)}, bf16[4,4,4,32,1024]{4,3,2,1,0:T(8,128)(2,1)}, bf16[4,4,4,16,1536]{4,3,2,1,0:T(8,128)(2,1)}, bf16[...) custom-call(bf16[16,2048]{1,0:T(8,128)(2,1)} %bitcast.235, ...), custom_call_target="tpu_custom_call" | custom-call | tf_op jit(solution)/shard_map/gather_all/pallas_call | solution.py:234
  151.0 4.0 fusion.qkv_ref
  155.0 6.0 %attention.2.attn_ref = bf16[320,512]{1,0:T(8,128)(2,1)} custom-call(bf16[320,1536]{1,0:T(8,128)(2,1)} %fusion.qkv_ref, f32[320,1]{1,0:T(8,128)} %broadcast_in_dim_reshape.10.seg_col_ref, f32[1,320]{1,0:T(1,128)} %broadcast_in_dim_reshape.9.seg_row_ref), custom_call_target="tpu_custom_call" | custom-call | tf_op jit(solution)/shard_map/attention/pallas_call | solution.py:643
  163.3 2.8 collective-permute-done
  168.3 3.1 fusion.16
  176.8 2.9 collective-permute-done.1
  182.2 4.2 fusion.1.qkv_ref
  186.3 6.0 %attention.3.attn_ref = bf16[320,512]{1,0:T(8,128)(2,1)} custom-call(bf16[320,1536]{1,0:T(8,128)(2,1)} %fusion.1.qkv_ref, f32[320,1]{1,0:T(8,128)} %broadcast_in_dim_reshape.10.seg_col_ref, f32[1,320]{1,0:T(1,128)} %broadcast_in_dim_reshape.9.seg_row_ref), custom_call_target="tpu_custom_call" | custom-call | tf_op jit(solution)/shard_map/attention/pallas_call | solution.py:643
  202.6 3.1 fusion.63
  205.7 2.6 fusion.23
  208.4 2.9 fusion.51
  211.9 5.9 %convolution_convert_fusion.2 = bf16[1024,2048]{1,0:T(8,128)(2,1)} fusion(bf16[320,2048]{1,0:T(8,128)(2,1)} %copy-done.49, f32[320,1024]{1,0:T(8,128)S(1)} %get-tuple-element.135, f32[1024]{0:T(1024)S(1)} %bitcast.281, f32[1024]{0:T(1024)S(1)} %bitcast.255, f32[320]{0:T(512)S(1)} %add_rsqrt_fusion, f32[320]{0:T(512)S(1)} %broadcast_multiply_fusion.8), kind=kOutput, calls=%fused_computation.6 | convolution fusion | flops 1345912832 | bytes 6826496 | tf_op jit(solution)/shard_map/dot_general | solution.py:586
  217.9 4.6 convolution_convert_fusion.1
  222.4 2.5 multiply_reduce_fusion.1
  225.0 4.1 fusion.54
  230.3 8.5 %attention_back.2 = (bf16[320,1536]{1,0:T(8,128)(2,1)}, f32[1,1536]{1,0:T(1,128)}) custom-call(bf16[320,1536]{1,0:T(8,128)(2,1)} %fusion.1.qkv_ref, bf16[320,512]{1,0:T(8,128)(2,1)} %attention.3.attn_ref, bf16[320,512]{1,0:T(8,128)(2,1)} %convolution_convert_fusion.9.grad_ref, f32[320,1]{1,0:T(8,128)} %broadcast_in_dim_reshape.10.seg_col_ref, ...), custom_call_target="tpu_custom_call" | custom-call | tf_op jit(solution)/shard_map/attention_back/pallas_call | solution.py:652
  238.8 4.5 fusion.67
  245.5 3.7 convolution_convert_fusion
  249.2 2.6 multiply_reduce_fusion.2
  254.5 3.1 fusion.64
  259.9 5.9 %convolution_convert_fusion.5 = bf16[1024,2048]{1,0:T(8,128)(2,1)} fusion(bf16[320,2048]{1,0:T(8,128)(2,1)} %copy-done.48, f32[320,1024]{1,0:T(8,128)S(1)} %copy-done.6, f32[1024]{0:T(1024)S(1)} %bitcast.277, f32[1024]{0:T(1024)S(1)} %bitcast.247), kind=kOutput, calls=%fused_computation.9 | convolution fusion | flops 1345257472 | bytes 6823936 | tf_op jit(solution)/shard_map/dot_general | solution.py:586
  265.8 4.6 convolution_convert_fusion.4
  274.8 8.1 %attention_back.3 = (bf16[320,1536]{1,0:T(8,128)(2,1)}, f32[1,1536]{1,0:T(1,128)}) custom-call(bf16[320,1536]{1,0:T(8,128)(2,1)} %fusion.qkv_ref, bf16[320,512]{1,0:T(8,128)(2,1)} %attention.2.attn_ref, bf16[320,512]{1,0:T(8,128)(2,1)} %convolution_convert_fusion.8.grad_ref, f32[320,1]{1,0:T(8,128)} %broadcast_in_dim_reshape.10.seg_col_ref, ...), custom_call_target="tpu_custom_call" | custom-call | tf_op jit(solution)/shard_map/attention_back/pallas_call | solution.py:652
  283.9 3.4 fusion.68
  289.3 3.5 convolution_convert_fusion.3
  295.4 2.7 multiply_add_fusion
  298.1 143.0 %scatter_all.1 = (bf16[2,2,4,16,2048]{4,3,2,1,0:T(8,128)(2,1)}, bf16[2,2,4,32,1024]{4,3,2,1,0:T(8,128)(2,1)}, bf16[2,2,4,16,1536]{4,3,2,1,0:T(8,128)(2,1)}, bf16...) custom-call(bf16[4,4,4,16,2048]{4,3,2,1,0:T(8,128)(2,1)} %bitcast.20, ...), custom_call_target="tpu_custom_call" | custom-call | tf_op jit(solution)/shard_map/scatter_all/pallas_call | solution.py:553
  443.8 2.4 reshape.619
  452.1 2.4 copy.71
  463.8 2.3 maximum_convert_fusion
  466.2 2.3 maximum_convert_fusion.1
  (275 shorter events, 85.8 us)
Async XLA Ops:
  3.9 4.0 copy-start.15
  11.1 5.0 %copy-start.23 = (bf16[2,128,1024]{2,1,0:T(8,128)(2,1)S(1)}, bf16[2,128,1024]{2,1,0:T(8,128)(2,1)}, u32[]{:S(2)}) copy-start(bf16[2,128,1024]{2,1,0:T(8,128)(2,1)} %param.18) | copy-start | bytes 1572868
  13.0 4.5 copy-start.27
  13.0 4.5 copy-start.37
  13.0 4.6 copy-start.26
  13.1 4.6 copy-start.38
  13.1 4.6 copy-start.39
  13.1 4.6 copy-start.40
  13.1 4.6 copy-start.41
  13.1 4.6 copy-start.42
  13.1 5.3 %copy-start.28 = (s32[2,80]{1,0:T(2,128)S(1)}, s32[2,80]{1,0:T(2,128)}, u32[]{:S(2)}) copy-start(s32[2,80]{1,0:T(2,128)} %param.16) | copy-start | bytes 1924
  144.8 5.0 %copy-start = (f32[4,80,1024]{2,1,0:T(8,128)S(1)}, f32[4,80,1024]{2,1,0:T(8,128)}, u32[]{:S(2)}) copy-start(f32[4,80,1024]{2,1,0:T(8,128)} %get-tuple-element.41) | copy-start | bytes 3932164
  162.8 5.5 %copy-start.1 = (f32[320,1024]{1,0:T(8,128)}, f32[320,1024]{1,0:T(8,128)S(1)}, u32[]{:S(2)}) copy-start(f32[320,1024]{1,0:T(8,128)S(1)} %fusion.65) | copy-start | bytes 3932164
  162.8 3.2 collective-permute-start
  174.4 5.4 %copy-start.2 = (f32[320,1024]{1,0:T(8,128)S(1)}, f32[320,1024]{1,0:T(8,128)}, u32[]{:S(2)}) copy-start(f32[320,1024]{1,0:T(8,128)} %copy-done.1) | copy-start | bytes 3932164
  176.2 3.5 collective-permute-start.1
  194.1 3.2 collective-permute-start.2
  199.5 22.9 %copy-start.3 = (f32[320,1024]{1,0:T(8,128)}, f32[320,1024]{1,0:T(8,128)S(1)}, u32[]{:S(2)}) copy-start(f32[320,1024]{1,0:T(8,128)S(1)} %get-tuple-element.135) | copy-start | bytes 3932164
  202.0 6.4 %copy-start.46 = (f32[320,2048]{1,0:T(8,128)}, f32[320,2048]{1,0:T(8,128)S(1)}, u32[]{:S(2)}) copy-start(f32[320,2048]{1,0:T(8,128)S(1)} %convolution_add_fusion.2) | copy-start | bytes 7864324
  208.3 14.1 %collective-permute-start.3 = (f32[320,1024]{1,0:T(8,128)}, f32[320,1024]{1,0:T(8,128)}, u32[]{:S(2)}, u32[]{:S(2)}) collective-permute-start(f32[320,1024]{1,0:T(8,128)} %fusion.23), channel_id=1, source_target_pairs={{0,1},{1,0},{2,3},{3,2},{4,5},{5,4},{6,7},{7,6},{8,9},{9,8},{10,11... | collective-permute-start | bytes 3932168 | tf_op jit(solution)/shard_map/ppermute | solution.py:689
  211.4 13.6 %collective-permute-start.7 = (f32[320,1024]{1,0:T(8,128)}, f32[320,1024]{1,0:T(8,128)}, u32[]{:S(2)}, u32[]{:S(2)}) collective-permute-start(f32[320,1024]{1,0:T(8,128)} %fusion.51), channel_id=1, source_target_pairs={{0,1},{1,0},{2,3},{3,2},{4,5},{5,4},{6,7},{7,6},{8,9},{9,8},{10,11... | collective-permute-start | bytes 3932168 | tf_op jit(solution)/shard_map/ppermute | solution.py:689
  211.9 5.9 %copy-start.47 = (f32[320,2048]{1,0:T(8,128)S(1)}, f32[320,2048]{1,0:T(8,128)}, u32[]{:S(2)}) copy-start(f32[320,2048]{1,0:T(8,128)} %copy-done.46) | copy-start | bytes 7864324
  225.0 4.1 copy-start.14
  238.8 4.6 copy-start.25
  238.8 5.0 %copy-start.12 = (bf16[320,512]{1,0:T(8,128)(2,1)S(1)}, bf16[320,512]{1,0:T(8,128)(2,1)}, u32[]{:S(2)}) copy-start(bf16[320,512]{1,0:T(8,128)(2,1)} %attention.3.attn_ref) | copy-start | bytes 983044
  243.3 5.9 %collective-permute-start.4 = (f32[320,1024]{1,0:T(8,128)}, f32[320,1024]{1,0:T(8,128)}, u32[]{:S(2)}, u32[]{:S(2)}) collective-permute-start(f32[320,1024]{1,0:T(8,128)} %fusion.67), channel_id=1, source_target_pairs={{0,1},{1,0},{2,3},{3,2},{4,5},{5,4},{6,7},{7,6},{8,9},{9,8},{10,11... | collective-permute-start | bytes 3932168 | tf_op jit(solution)/shard_map/ppermute | solution.py:689
  252.3 5.3 %copy-start.7 = (f32[320,1024]{1,0:T(8,128)}, f32[320,1024]{1,0:T(8,128)S(1)}, u32[]{:S(2)}) copy-start(f32[320,1024]{1,0:T(8,128)S(1)} %get-tuple-element.126) | copy-start | bytes 3932164
  259.2 11.3 %collective-permute-start.5 = (f32[320,1024]{1,0:T(8,128)S(1)}, f32[320,1024]{1,0:T(8,128)}, u32[]{:S(2)}, u32[]{:S(2)}) collective-permute-start(f32[320,1024]{1,0:T(8,128)S(1)} %fusion.19), channel_id=1, source_target_pairs={{0,1},{1,0},{2,3},{3,2},{4,5},{5,4},{6,7},{7,6},{8,9},{9,8},{10,11... | collective-permute-start | bytes 3932168 | tf_op jit(solution)/shard_map/ppermute | solution.py:689
  259.9 5.9 %copy-start.8 = (f32[320,1024]{1,0:T(8,128)S(1)}, f32[320,1024]{1,0:T(8,128)}, u32[]{:S(2)}) copy-start(f32[320,1024]{1,0:T(8,128)} %copy-done.7) | copy-start | bytes 3932164
  259.9 5.9 %copy-start.45 = (f32[320,2048]{1,0:T(8,128)S(1)}, f32[320,2048]{1,0:T(8,128)}, u32[]{:S(2)}) copy-start(f32[320,2048]{1,0:T(8,128)} %copy-done.43) | copy-start | bytes 7864324
  283.9 3.7 copy-start.11
  287.3 5.5 %collective-permute-start.6 = (f32[320,1024]{1,0:T(8,128)S(1)}, f32[320,1024]{1,0:T(8,128)S(1)}, u32[]{:S(2)}, u32[]{:S(2)}) collective-permute-start(f32[320,1024]{1,0:T(8,128)S(1)} %fusion.68), channel_id=1, source_target_pairs={{0,1},{1,0},{2,3},{3,2},{4,5},{5,4},{6,7},{7,6},{8,9},{9,8},{10,11... | collective-permute-start | bytes 3932168 | tf_op jit(solution)/shard_map/ppermute | solution.py:689
  (26 other events, 57.1 us)

commit v2 on v1

v2 whole, which is shorter than its diff:
```python
import functools
import math

import jax
import jax.numpy as jnp
from jax import lax
from jax.experimental import pallas as pl
from jax.experimental.pallas import tpu as pltpu
from jax.sharding import Mesh
from jax.sharding import PartitionSpec as P

AXES = ("z", "xh", "y", "xl", "core")
RING = 4
ANY = pl.BlockSpec(memory_space=pl.ANY)
VMEM = pl.BlockSpec(memory_space=pltpu.VMEM)
DMA = pltpu.SemaphoreType.DMA
ORDERS = ("xyz", "zxy", "yzx", "yzx")


def positions():
    return {
        "z": lax.axis_index("z"),
        "x": lax.axis_index("xh") * 2 + lax.axis_index("xl"),
        "y": lax.axis_index("y"),
    }


def neighbour(pos, axis, step):
    at = lax.rem(pos[axis] + step + RING, RING)
    if axis == "x":
        return {"xh": at // 2, "xl": lax.rem(at, 2)}
    return {axis: at}


def remote(src, dst, send, recv, target):
    return pltpu.make_async_remote_copy(
        src_ref=src,
        dst_ref=dst,
        send_sem=send,
        recv_sem=recv,
        device_id=target,
        device_id_type=pl.DeviceIdType.MESH,
    )


def greet(pos, with_column):
    barrier = pltpu.get_barrier_semaphore()
    targets = [neighbour(pos, axis, step) for axis in "xyz" for step in (1, -1)]
    if with_column:
        targets.append(neighbour(pos, "z", 2))
    targets.append({"core": 1 - lax.axis_index("core")})
    for target in targets:
        pl.semaphore_signal(
            barrier, inc=1, device_id=target, device_id_type=pl.DeviceIdType.MESH
        )
    pl.semaphore_wait(barrier, len(targets))


def half(ref, which, rows, cols):
    lead = (slice(None),) * (len(ref.shape) - 2)
    if rows % 16 == 0:
        return ref.at[lead + (pl.ds(which * (rows // 2), rows // 2), slice(None))]
    return ref.at[lead + (slice(None), pl.ds(which * (cols // 2), cols // 2))]


class Gather:
    def __init__(self, pos, order, own, full, send, recv):
        self.pos, self.order, self.own, self.full = pos, order, own, full
        self.send, self.recv = send, recv
        self.rows, self.cols = full.shape[-2:]

    def view(self, stage, shift):
        index = {}
        for place, axis in enumerate(self.order):
            if place < stage:
                index[axis] = slice(None)
            elif place == stage:
                index[axis] = lax.rem(self.pos[axis] + shift + RING, RING)
            else:
                index[axis] = self.pos[axis]
        return self.full.at[index["z"], index["x"], index["y"]]

    def copy(self, stage, kind):
        axis = self.order[stage]
        sems = (self.send.at[stage * 4 + kind], self.recv.at[stage * 4 + kind])
        target = neighbour(self.pos, axis, 1 if kind % 2 == 0 else -1)
        if kind < 2:
            src = self.own if stage == 0 else self.view(stage, 0)
            return remote(src, self.view(stage, 0), *sems, target)
        piece = half(self.view(stage, -1 if kind == 2 else 1), kind - 2, self.rows, self.cols)
        return remote(piece, piece, *sems, target)

    def arrive(self, stage, kind):
        sems = (self.send.at[stage * 4 + kind], self.recv.at[stage * 4 + kind])
        axis = self.order[stage]
        if kind < 2:
            piece = self.view(stage, -1 if kind == 0 else 1)
        else:
            piece = half(self.view(stage, 2), kind - 2, self.rows, self.cols)
        remote(piece, piece, *sems, neighbour(self.pos, axis, 1)).wait_recv()

    def begin(self, stage):
        for kind in (0, 1):
            self.copy(stage, kind).start()

    def onward(self, stage):
        for kind in (0, 1):
            self.arrive(stage, kind)
            self.copy(stage, kind + 2).start()

    def finish(self, stage):
        for kind in (2, 3):
            self.arrive(stage, kind)

    def drain(self, stages):
        for stage in stages:
            for kind in range(4):
                self.copy(stage, kind).wait_send()


class Sequences:
    def __init__(self, pos, parts, wholes, sems):
        self.pos, self.parts, self.wholes = pos, parts, wholes
        self.send, self.recv, self.core_send, self.core_recv, self.local = sems
        self.core = lax.axis_index("core")
        self.receiver = pos["z"] // 2 == self.core

    def outward(self, a, b, home):
        return remote(
            self.parts[a].at[b],
            self.wholes[a].at[self.pos["z"]],
            self.send.at[a, b],
            self.recv.at[a, self.pos["z"]],
            {"z": home},
        )

    def crossing(self, a, q):
        piece = self.wholes[a].at[q]
        return remote(
            piece, piece, self.core_send.at[a, q], self.core_recv.at[a, q], {"core": 1 - self.core}
        )

    def staying(self, a, b):
        return pltpu.make_async_copy(
            self.parts[a].at[b], self.wholes[a].at[self.pos["z"]], self.local.at[a]
        )

    def begin(self):
        for a in range(len(self.parts)):
            for b in range(2):
                home = 2 * self.core + b

                @pl.when(home == self.pos["z"])
                def _():
                    self.staying(a, b).start()

                @pl.when(home != self.pos["z"])
                def _():
                    self.outward(a, b, home).start()

    def cross(self):
        @pl.when(self.receiver)
        def _():
            for a in range(len(self.parts)):
                for q in range(RING):

                    @pl.when(q == self.pos["z"])
                    def _():
                        self.staying(a, 0).wait()

                    @pl.when(q != self.pos["z"])
                    def _():
                        piece = self.wholes[a].at[q]
                        remote(
                            piece,
                            piece,
                            self.send.at[a, 0],
                            self.recv.at[a, q],
                            {"z": lax.rem(self.pos["z"] + 1, RING)},
                        ).wait_recv()

                    self.crossing(a, q).start()

    def drain(self):
        for a in range(len(self.parts)):
            for b in range(2):
                home = 2 * self.core + b

                @pl.when(home != self.pos["z"])
                def _():
                    self.outward(a, b, lax.rem(self.pos["z"] + 1, RING)).wait_send()

            for q in range(RING):

                @pl.when(self.receiver)
                def _():
                    self.crossing(a, q).wait_send()

                @pl.when(jnp.logical_not(self.receiver))
                def _():
                    self.crossing(a, q).wait_recv()


def sequence_scratch(moved):
    sems = [DMA((moved, 2)), DMA((moved, RING)), DMA((moved, RING)), DMA((moved, RING)), DMA((moved,))]
    return sems if moved else []


def sequence_shapes(parts):
    return [jax.ShapeDtypeStruct((RING,) + p.shape[1:], p.dtype) for p in parts]


def gather_kernel(count, whole, moved, *refs):
    owns, parts = refs[:count], refs[count : count + moved]
    refs = refs[count + moved :]
    fulls, wholes = refs[:count], refs[count : count + moved]
    send, recv, local = refs[count + moved : count + moved + 3]
    pos = positions()
    greet(pos, True)
    sequences = Sequences(pos, parts, wholes, refs[count + moved + 3 :])
    streams, keeps = [], []
    for m in range(count):
        keeps.append(
            pltpu.make_async_copy(
                owns[m], fulls[m].at[pos["z"], pos["x"], pos["y"]], local.at[m]
            )
        )
        streams.append(
            Gather(pos, ORDERS[m % whole % 4], owns[m], fulls[m], send.at[m], recv.at[m])
        )
    for keep in keeps:
        keep.start()
    for s in streams:
        s.begin(0)
    sequences.begin()
    for stage in range(3):
        running = streams if stage < 2 else streams[:whole]
        for s in running:
            s.onward(stage)
        if stage == 0:
            for keep in keeps:
                keep.wait()
        for m, s in enumerate(running):
            s.finish(stage)
            if stage == 0 or (stage == 1 and m < whole):
                s.begin(stage + 1)
        if stage == 1:
            sequences.cross()
    for m, s in enumerate(streams):
        s.drain(range(3 if m < whole else 2))
    sequences.drain()


def gather_all(owns, begun, parts):
    count, moved = len(owns) + len(begun), len(parts)
    shapes = [
        jax.ShapeDtypeStruct((RING, RING, RING) + o.shape, o.dtype) for o in owns + begun
    ]
    out = pl.pallas_call(
        functools.partial(gather_kernel, count, len(owns), moved),
        out_shape=shapes + sequence_shapes(parts),
        in_specs=[ANY] * (count + moved),
        out_specs=[ANY] * (count + moved),
        scratch_shapes=[DMA((count, 12)), DMA((count, 12)), DMA((count,))]
        + sequence_scratch(moved),
        compiler_params=pltpu.CompilerParams(collective_id=0, has_side_effects=True),
        name="gather_all",
    )(*owns, *begun, *parts)
    return out[: len(owns)], out[len(owns) : count], out[count:]


def scatter_scratch(ends, kinds, stages):
    scratch = []
    for (r, c), kind in zip(ends, kinds):
        if 0 in stages:
            scratch.append(pltpu.VMEM((4, RING, RING, r, c // 2), kind))
        for stage in stages:
            scratch.append(pltpu.VMEM((6,) + (RING,) * (2 - stage) + (r, c // 2), kind))
        if len(stages) > 1:
            for stage in stages:
                scratch.append(pltpu.VMEM((RING,) * (2 - stage) + (r, c), kind))
    return scratch


class Scatter:
    def __init__(self, pos, order, grad, own, boxes, sums, send, recv, local):
        self.pos, self.order, self.grad = pos, order, grad
        self.own, self.boxes, self.sums = own, boxes, sums
        self.send, self.recv, self.local = send, recv, local
        self.part = sums[0].shape[-1] // 2

    def piece(self, stage, shift, which=None):
        axis = self.order[stage]
        left = [a for a in "zxy" if a in self.order[stage:]]
        source = self.grad if stage == 0 else self.sums[stage - 1]
        at = lax.rem(self.pos[axis] + shift + RING, RING)
        index = tuple(at if a == axis else slice(None) for a in left) + (slice(None),)
        if which is None:
            return source.at[index + (slice(None),)]
        return source.at[index + (pl.ds(which * self.part, self.part),)]

    def box(self, stage, kind):
        return self.boxes[stage].at[kind]

    def copy(self, stage, kind):
        src, step = {
            0: (lambda: self.piece(stage, 2, 0), 1),
            1: (lambda: self.piece(stage, 1, 1), 1),
            2: (lambda: self.piece(stage, -2, 1), -1),
            3: (lambda: self.piece(stage, -1, 0), -1),
            4: (lambda: self.box(stage, 0), 1),
            5: (lambda: self.box(stage, 2), -1),
        }[kind]
        return remote(
            src(),
            self.box(stage, kind),
            self.send.at[stage * 6 + kind],
            self.recv.at[stage * 6 + kind],
            neighbour(self.pos, self.order[stage], step),
        )

    def loads(self):
        for slot, (shift, which) in enumerate(((1, 0), (-1, 1), (0, 0), (0, 1))):
            yield pltpu.make_async_copy(
                self.piece(0, shift, which), self.own.at[slot], self.local.at[slot]
            )

    def begin(self, stage):
        for kind in range(4):
            self.copy(stage, kind).start()
        if stage == 0:
            for load in self.loads():
                load.start()

    def term(self, stage, slot):
        if stage == 0:
            return self.own.at[slot]
        shift, which = ((1, 0), (-1, 1), (0, 0), (0, 1))[slot]
        return self.piece(stage, shift, which)

    def add(self, stage, target, terms):
        lead = 2 - stage

        def one(index):
            total = terms[0][index].astype(jnp.float32)
            for t in terms[1:]:
                total = total + t[index].astype(jnp.float32)
            target[index] = total.astype(target.dtype)

        if lead == 0:
            one((slice(None), slice(None)))
            return

        def body(i, carry):
            where = (i // RING, lax.rem(i, RING)) if lead == 2 else (i,)
            one(where + (slice(None), slice(None)))
            return carry

        lax.fori_loop(0, RING**lead, body, 0)

    def onward(self, stage):
        if stage == 0:
            for load in self.loads():
                load.wait()
        for slot, kind in ((0, 0), (1, 2)):
            self.copy(stage, kind).wait_recv()
            box = self.box(stage, kind)
            self.add(stage, box, (box, self.term(stage, slot)))
            self.copy(stage, 4 + slot).start()

    def finish(self, stage):
        for kind in (1, 3, 4, 5):
            self.copy(stage, kind).wait_recv()
        lead = (slice(None),) * (3 - stage)
        for which, kinds in ((0, (3, 4)), (1, (1, 5))):
            target = self.sums[stage].at[lead + (pl.ds(which * self.part, self.part),)]
            self.add(
                stage,
                target,
                (self.term(stage, 2 + which),) + tuple(self.box(stage, k) for k in kinds),
            )

    def drain(self, stages):
        for stage in stages:
            for kind in range(6):
                self.copy(stage, kind).wait_send()


class Publish:
    def __init__(self, pos, order, source, final, sends, recvs, local):
        self.pos, self.order, self.source, self.final = pos, order, source, final
        self.sends_f, self.recvs_f, self.local = sends, recvs, local
        self.core, self.xl = lax.axis_index("core"), lax.axis_index("xl")
        self.part = source.shape[-1] // 2

    def across_first(self):
        return self.order[0] != "y"

    def block(self, shift):
        yi = lax.rem(self.pos["y"] + shift + RING, RING)
        xs = slice(None) if self.across_first() else self.xl
        return self.final.at[self.core, xs, yi]

    def spread(self, kind, own=False):
        sems = (self.sends_f.at[kind], self.recvs_f.at[kind])
        if kind == 5:
            whole = self.final.at[self.core]
            return remote(whole, whole, *sems, {"core": 1 - self.core})
        if kind == 4:
            if self.across_first():
                dst = self.final.at[self.core, self.xl, self.pos["y"]]
                src = self.source
            else:
                src = dst = self.final.at[self.core, self.xl]
            return remote(src, dst, *sems, {"xl": 1 - self.xl})
        target = neighbour(self.pos, "y", 1 if kind % 2 == 0 else -1)
        if kind < 2:
            dst = self.block(0)
            src = dst if self.across_first() else self.source
            return remote(src, dst, *sems, target)
        ref = self.block(-1 if kind == 2 else 1)
        lead = (slice(None),) * (len(ref.shape) - 1)
        ref = ref.at[lead + (pl.ds((kind - 2) * self.part, self.part),)]
        return remote(ref, ref, *sems, target)

    def spread_arrives(self, kind):
        sems = (self.sends_f.at[kind], self.recvs_f.at[kind])
        if kind == 5:
            ref = self.final.at[1 - self.core]
        elif kind == 4:
            ref = self.final.at[self.core, 1 - self.xl]
            if self.across_first():
                ref = ref.at[self.pos["y"]]
        elif kind < 2:
            ref = self.block(-1 if kind == 0 else 1)
        else:
            ref = self.block(2)
            lead = (slice(None),) * (len(ref.shape) - 1)
            ref = ref.at[lead + (pl.ds((kind - 2) * self.part, self.part),)]
        remote(ref, ref, *sems, {"core": 1 - self.core}).wait_recv()

    def keep(self):
        return pltpu.make_async_copy(
            self.source,
            self.final.at[self.core, self.xl, self.pos["y"]],
            self.local,
        )

    def publish(self, step):
        if step == 0:
            self.keep().start()
            for kind in (4,) if self.across_first() else (0, 1):
                self.spread(kind).start()
            self.keep().wait()
        elif self.across_first():
            if step == 1:
                self.spread_arrives(4)
                for kind in (0, 1):
                    self.spread(kind).start()
            elif step == 2:
                for kind in (0, 1):
                    self.spread_arrives(kind)
                    self.spread(kind + 2).start()
            elif step == 3:
                for kind in (2, 3):
                    self.spread_arrives(kind)
        else:
            if step == 1:
                for kind in (0, 1):
                    self.spread_arrives(kind)
                    self.spread(kind + 2).start()
            elif step == 2:
                for kind in (2, 3):
                    self.spread_arrives(kind)
                self.spread(4).start()
            elif step == 3:
                self.spread_arrives(4)
        if step == 3:
            self.spread(5).start()
        if step == 4:
            self.spread_arrives(5)

    def drain(self):
        for kind in range(6):
            self.spread(kind).wait_send()


def scatter_kernel(count, done, moved, *refs):
    grads, given, wholes = refs[:count], refs[count : count + done], refs[count + done : count + done + moved]
    refs = refs[count + done + moved :]
    finals, parts = refs[: count + done], refs[count + done : count + done + moved]
    refs = refs[count + done + moved :]
    bufs, more = refs[: 7 * count], refs[7 * count : 7 * count + 4 * done]
    send, recv, local, sends_f, recvs_f, keeps, send_t, recv_t, local_t = refs[7 * count + 4 * done :]
    pos = positions()
    core = lax.axis_index("core")
    greet(pos, True)
    streams = []
    for m in range(count):
        own = bufs[7 * m : 7 * m + 7]
        streams.append((ORDERS[m % 4], grads[m], own[0], own[1:4], own[4:7]))
    for m in range(done):
        own = more[4 * m : 4 * m + 4]
        streams.append((ORDERS[m % 4], None, None, (None,) + own[:2], (given[m],) + own[2:]))
    streams = [
        Scatter(pos, *args, send.at[m], recv.at[m], local.at[m]) for m, args in enumerate(streams)
    ]
    news = [
        Publish(pos, s.order, s.sums[2], finals[m], sends_f.at[m], recvs_f.at[m], keeps.at[m])
        for m, s in enumerate(streams)
    ]
    late, ahead = streams[:count], streams[count:]
    last, early = news[:count], news[count:]
    for s in ahead:
        s.begin(1)
    for s in late:
        s.begin(0)
    sender = pos["z"] // 2 == core
    slot = lax.rem(pos["z"], 2)

    def homeward(a, q):
        return remote(
            wholes[a].at[q], parts[a].at[slot], send_t.at[a, q], recv_t.at[a, slot], {"z": q}
        )

    def staying(a):
        return pltpu.make_async_copy(wholes[a].at[pos["z"]], parts[a].at[slot], local_t.at[a])

    for a in range(moved):
        for q in range(RING):

            @pl.when(sender & (pos["z"] == q))
            def _():
                staying(a).start()

            @pl.when(sender & (pos["z"] != q))
            def _():
                homeward(a, q).start()

    def move(group, places, stage):
        for s, n in zip(group, places):
            s.finish(stage)
            if stage < 2:
                s.begin(stage + 1)
            else:
                n.publish(0)

    def step(places, at):
        for n in places:
            n.publish(at)

    for s in ahead:
        s.onward(1)
    for s in late:
        s.onward(0)
    move(ahead, early, 1)
    move(late, last, 0)
    for s in ahead:
        s.onward(2)
    for s in late:
        s.onward(1)
    move(ahead, early, 2)
    move(late, last, 1)
    step(early, 1)
    for s in late:
        s.onward(2)
    step(early, 2)
    move(late, last, 2)
    step(early, 3)
    step(last, 1)
    step(last, 2)
    step(early, 4)
    step(last, 3)
    step(last, 4)
    for s in late:
        s.drain((0, 1, 2))
    for s in ahead:
        s.drain((1, 2))
    for n in news:
        n.drain()
    for a in range(moved):
        for q in range(RING):

            @pl.when(sender & (pos["z"] == q))
            def _():
                staying(a).wait()

            @pl.when(sender & (pos["z"] != q))
            def _():
                homeward(a, q).wait_send()

        for b in range(2):

            @pl.when(2 * core + b != pos["z"])
            def _():
                remote(
                    parts[a].at[b],
                    parts[a].at[b],
                    send_t.at[a, 0],
                    recv_t.at[a, b],
                    {"z": lax.rem(pos["z"] + 1, RING)},
                ).wait_recv()


def scatter_all(grads, given, wholes):
    count, done, moved = len(grads), len(given), len(wholes)
    ends = [g.shape[-2:] for g in grads + given]
    kinds = [g.dtype for g in grads + given]
    shapes = [jax.ShapeDtypeStruct((2, 2, RING) + e, k) for e, k in zip(ends, kinds)]
    shapes += [jax.ShapeDtypeStruct((2,) + w.shape[1:], w.dtype) for w in wholes]
    bufs = scatter_scratch(ends[:count], kinds[:count], (0, 1, 2))
    bufs += scatter_scratch(ends[count:], kinds[count:], (1, 2))
    out = pl.pallas_call(
        functools.partial(scatter_kernel, count, done, moved),
        out_shape=shapes,
        in_specs=[ANY] * count + [VMEM] * done + [ANY] * moved,
        out_specs=[ANY] * (count + done + moved),
        scratch_shapes=bufs
        + [
            DMA((count + done, 18)),
            DMA((count + done, 18)),
            DMA((count + done, 5)),
            DMA((count + done, 6)),
            DMA((count + done, 6)),
            DMA((count + done,)),
            DMA((moved, RING)),
            DMA((moved, 2)),
            DMA((moved,)),
        ],
        compiler_params=pltpu.CompilerParams(
            collective_id=1, has_side_effects=True, vmem_limit_bytes=62 * 1024 * 1024
        ),
        name="scatter_all",
    )(*grads, *given, *wholes)
    return out[: count + done], out[count + done :]


NORM_EPS = 1e-05
GELU_COEF = 0.7978845608028654
CUBIC_COEF = 0.044715
HEAD_DIM = 64
LOW = jnp.bfloat16
F32 = jnp.float32
TILE = 256
ROWS = 32
B_QV, B_OUT, B_UP, B_DOWN, G_ONE, S_ONE, G_TWO, S_TWO = range(8)


def dot(left, right, dims=((1,), (0,))):
    return lax.dot_general(left, right, (dims, ((), ())), preferred_element_type=F32)


def tile_at(t, size=TILE):
    return pl.ds(pl.multiple_of(t * size, size), size)


def over_rows(count, body):
    def step(i, carry):
        body(pl.ds(pl.multiple_of(i * ROWS, ROWS), ROWS))
        return carry

    lax.fori_loop(0, count // ROWS, step, 0)


def over_tiles(count, body):
    def step(t, carry):
        body(t)
        return carry

    lax.fori_loop(0, count, step, 0)


def head_probs(q, k, allowed, scale):
    scores = jnp.where(allowed, dot(q, k, ((1,), (1,))) * scale, -jnp.inf)
    top = jnp.max(scores, axis=-1, keepdims=True)
    lse = top + jnp.log(jnp.sum(jnp.exp(scores - top), axis=-1, keepdims=True))
    return jnp.exp(scores - lse)


def allowed_pairs(seg_col, seg_row):
    length = seg_col.shape[0]
    row = lax.broadcasted_iota(jnp.int32, (length, length), 0)
    col = lax.broadcasted_iota(jnp.int32, (length, length), 1)
    return (row >= col) & (seg_col == seg_row)


def norm_of(x):
    center = x - jnp.mean(x, axis=-1, keepdims=True)
    factor = lax.rsqrt(jnp.mean(center * center, axis=-1, keepdims=True) + NORM_EPS)
    return center * factor, factor


def norm_backward(d_act, normed, factor, gain):
    d_norm = d_act * gain
    return factor * (
        d_norm
        - jnp.mean(d_norm, axis=-1, keepdims=True)
        - normed * jnp.mean(d_norm * normed, axis=-1, keepdims=True)
    )


def gelu_pair(pre_act):
    cubic = pre_act * pre_act * pre_act
    tangent = jnp.tanh(GELU_COEF * (pre_act + CUBIC_COEF * cubic))
    gelu_value = 0.5 * pre_act * (1.0 + tangent)
    gelu_slope = 0.5 * (1.0 + tangent) + 0.5 * pre_act * (1.0 - tangent * tangent) * GELU_COEF * (
        1.0 + 3.0 * CUBIC_COEF * pre_act * pre_act
    )
    return gelu_value, gelu_slope


def vector_row(small, shard, vector, layer, part, size):
    return small[shard, vector, pl.ds(2 * layer + part, 1), pl.ds(0, size)]


def fill_vector(target, small, vector, layer):
    for s in range(8):
        target[:, pl.ds(s * 128, 128)] = vector_row(small, s, vector, layer, 0, 128)


class Pair:
    def __init__(self, terms, box, send, recv):
        self.terms, self.box, self.send, self.recv = terms, box, send, recv
        self.other = {"core": 1 - lax.axis_index("core")}

    def copy(self, which, t):
        return remote(
            self.terms.at[which, t],
            self.box.at[which, t],
            self.send.at[which, t],
            self.recv.at[which, t],
            self.other,
        )

    def fill(self, which, make):
        count = self.terms.shape[1]

        def body(t):
            self.terms[which, t] = make(t)

            @pl.when(t > 0)
            def _():
                self.copy(which, t - 1).start()

        over_tiles(count, body)
        self.copy(which, count - 1).start()

    def wait(self, which):
        for t in range(self.terms.shape[1]):
            self.copy(which, t).wait()

    def total(self, which, rows):
        return jnp.concatenate(
            [
                self.terms[which, t, rows, :] + self.box[which, t, rows, :]
                for t in range(self.terms.shape[1])
            ],
            axis=-1,
        )


def greet_pair():
    barrier = pltpu.get_barrier_semaphore()
    pl.semaphore_signal(
        barrier,
        inc=1,
        device_id={"core": 1 - lax.axis_index("core")},
        device_id_type=pl.DeviceIdType.MESH,
    )
    pl.semaphore_wait(barrier, 1)


def nothing(*_):
    pass


def seg_row_col(segs):
    row = jnp.concatenate([segs[q, 0:1, 0:80] for q in range(RING)], axis=-1)
    length = row.shape[1]
    at = lax.broadcasted_iota(jnp.int32, (length, length), 0)
    to = lax.broadcasted_iota(jnp.int32, (length, length), 1)
    return row, jnp.sum(jnp.where(at == to, row, 0.0), axis=-1, keepdims=True)


def forward_kernel(layer, count, moved, *refs):
    state, segs, small, w_up, w_down, w_qkv, w_out = refs[:7]
    parts, refs = refs[7 + count : 7 + count + moved], refs[7 + count + moved :]
    new_state, act_one, qkv, attn, middle, act_two, slope, hidden = refs[:8]
    fulls, wholes = refs[8 : 8 + count], refs[8 + count : 8 + count + moved]
    refs = refs[8 + count + moved :]
    v_qkv, v_out, v_up, v_down, terms, box, vec, vec_up = refs[:8]
    load, p_send, p_recv = refs[8:11]
    rings = refs[11:]
    core = lax.axis_index("core")
    length, width = state.shape
    half_width = width // 2
    loads = [
        pltpu.make_async_copy(w, v, load.at[i])
        for i, (w, v) in enumerate(((w_qkv, v_qkv), (w_out, v_out), (w_up, v_up), (w_down, v_down)))
    ]
    for copy in loads:
        copy.start()
    pos = positions()
    streams = sequences = None
    if count:
        greet(pos, False)
        streams = [
            Gather(pos, ORDERS[m], None, fulls[m], rings[0].at[m], rings[1].at[m])
            for m in range(count)
        ]
        for s in streams:
            s.begin(2)
    elif moved:
        greet(pos, True)
        sequences = Sequences(pos, parts, wholes, rings)
        sequences.begin()
    else:
        greet_pair()
    pair = Pair(terms, box, p_send, p_recv)
    for i, vector in enumerate((G_ONE, S_ONE, B_OUT, G_TWO, S_TWO, B_DOWN)):
        fill_vector(vec.at[i], small, vector, layer)
    for s in range(8):
        vec_up[0:1, pl.ds(s * TILE, TILE)] = vector_row(small, s, B_UP, layer, core, TILE)
    q_bias = []
    for s in range(8):
        row = vector_row(small, s, B_QV, layer, 0, 256)
        for at in (0, 2 * HEAD_DIM):
            q_bias.append(
                jnp.where(
                    core == 0,
                    row[:, at : at + HEAD_DIM],
                    row[:, at + HEAD_DIM : at + 2 * HEAD_DIM],
                )
            )
    vec_up[1:2, pl.ds(0, half_width)] = jnp.concatenate(q_bias[:8], axis=-1)
    vec_up[1:2, pl.ds(half_width, half_width)] = jnp.zeros((1, half_width), F32)
    vec_up[1:2, pl.ds(2 * half_width, half_width)] = jnp.concatenate(q_bias[8:], axis=-1)

    def first_norm(rows):
        normed, _ = norm_of(state[rows, :])
        act_one[rows, :] = (normed * vec[0] + vec[1]).astype(LOW)

    over_rows(length, first_norm)
    loads[0].wait()

    def project(t):
        here = tile_at(t)
        bias = vec_up[1:2, here]
        qkv[:, here] = (dot(act_one[...], v_qkv[:, here]) + bias).astype(LOW)

    over_tiles(3 * half_width // TILE, project)
    seg_row, seg_col = seg_row_col(segs)
    allowed = allowed_pairs(seg_col, seg_row)
    scale = 1.0 / math.sqrt(HEAD_DIM)
    for h in range(half_width // HEAD_DIM):
        q, k, v = (qkv[:, pl.ds(t * half_width + h * HEAD_DIM, HEAD_DIM)] for t in range(3))
        probs = head_probs(q, k, allowed, scale).astype(LOW)
        attn[:, pl.ds(h * HEAD_DIM, HEAD_DIM)] = dot(probs, v).astype(LOW)
    loads[1].wait()
    pair.fill(0, lambda t: dot(attn[...], v_out[:, tile_at(t)]))
    if moved:
        sequences.cross()
    pair.wait(0)

    def second_norm(rows):
        x = state[rows, :] + pair.total(0, rows) + vec[2]
        middle[rows, :] = x
        normed, _ = norm_of(x)
        act_two[rows, :] = (normed * vec[3] + vec[4]).astype(LOW)

    over_rows(length, second_norm)
    loads[2].wait()

    def expand(t):
        here = tile_at(t)
        value, rise = gelu_pair(dot(act_two[...], v_up[:, here]) + vec_up[0:1, here])
        hidden[:, here] = value.astype(LOW)
        slope[:, here] = rise

    over_tiles(slope.shape[1] // TILE, expand)
    if count:
        for s in streams:
            s.onward(2)
    loads[3].wait()
    pair.fill(1, lambda t: dot(hidden[...], v_down[:, tile_at(t)]))
    pair.wait(1)

    def close(rows):
        new_state[rows, :] = middle[rows, :] + pair.total(1, rows) + vec[5]

    over_rows(length, close)
    if count:
        for s in streams:
            s.finish(2)
        for s in streams:
            s.drain((2,))
    if moved:
        sequences.drain()


def weight_scratch(weights):
    w_up, w_down, w_qkv, w_out = weights
    return [pltpu.VMEM(w.shape, LOW) for w in (w_qkv, w_out, w_up, w_down)]


def pair_scratch(length, width):
    shape = (2, width // TILE, length, TILE)
    return [pltpu.VMEM(shape, F32), pltpu.VMEM(shape, F32)]


def forward_block(layer, state, segs, small, weights, begun, parts):
    count, moved = len(begun), len(parts)
    length, width = state.shape
    inner = weights[0].shape[1]
    shapes = [
        ((length, width), F32),
        ((length, width), LOW),
        ((length, 3 * width // 2), LOW),
        ((length, width // 2), LOW),
        ((length, width), F32),
        ((length, width), LOW),
        ((length, inner), F32),
        ((length, inner), LOW),
    ]
    shapes = [jax.ShapeDtypeStruct(*s) for s in shapes]
    shapes += [jax.ShapeDtypeStruct(b.shape, b.dtype) for b in begun]
    out = pl.pallas_call(
        functools.partial(forward_kernel, layer, count, moved),
        out_shape=shapes + sequence_shapes(parts),
        in_specs=[VMEM] * 3 + [ANY] * (4 + count + moved),
        out_specs=[VMEM] * 8 + [ANY] * (count + moved),
        input_output_aliases={7 + m: 8 + m for m in range(count)},
        scratch_shapes=weight_scratch(weights)
        + pair_scratch(length, width)
        + [
            pltpu.VMEM((6, 1, width), F32),
            pltpu.VMEM((2, inner), F32),
            DMA((4,)),
            DMA((2, width // TILE)),
            DMA((2, width // TILE)),
        ]
        + ([DMA((count, 12)), DMA((count, 12))] if count else [])
        + sequence_scratch(moved),
        compiler_params=pltpu.CompilerParams(
            collective_id=2 + layer, has_side_effects=True, vmem_limit_bytes=60 * 1024 * 1024
        ),
        name="forward_block",
    )(state, segs, small, *weights, *begun, *parts)
    return out[:8], out[8 : 8 + count], out[8 + count :]


def column_sum(target, row, value):
    target[row : row + 1, :] += jnp.sum(value, axis=0, keepdims=True)


def backward_kernel(layer, count, *refs):
    grad_state, state, middle, qkv, attn, slope, segs, small = refs[:8]
    w_up, w_down, w_qkv, w_out = refs[8:12]
    grads, refs = refs[12 : 12 + count], refs[12 + count :]
    new_grad, grad_low, d_pre_low, mid_low, d_qkv, small_grad = refs[:6]
    sums, refs = refs[6 : 6 + count], refs[6 + count :]
    v_qkv, v_out, v_up, v_down, terms, box, vec, acc, acc_up, acc_qkv, d_attn, grad_mid = refs[:12]
    load, p_send, p_recv = refs[12:15]
    rings = refs[15:]
    core = lax.axis_index("core")
    length, width = state.shape
    half_width = width // 2
    inner = slope.shape[1]
    loads = [
        pltpu.make_async_copy(w, v, load.at[i])
        for i, (w, v) in enumerate(((w_down, v_down), (w_up, v_up), (w_out, v_out), (w_qkv, v_qkv)))
    ]
    for copy in loads:
        copy.start()
    if count:
        pos = positions()
        greet(pos, False)
        send, recv, local = rings[2 * count :]
        streams = [
            Scatter(
                pos,
                ORDERS[m % 4],
                grads[m],
                rings[2 * m],
                (rings[2 * m + 1],),
                (sums[m],),
                send.at[m],
                recv.at[m],
                local.at[m],
            )
            for m in range(count)
        ]
        for s in streams:
            s.begin(0)
    else:
        greet_pair()
        streams = ()
    pair = Pair(terms, box, p_send, p_recv)
    fill_vector(vec.at[0], small, G_ONE, layer)
    fill_vector(vec.at[1], small, G_TWO, layer)
    acc[...] = jnp.zeros_like(acc)

    def lower(rows):
        g = grad_state[rows, :]
        grad_low[rows, :] = g.astype(LOW)
        column_sum(acc, 0, g)

    over_rows(length, lower)
    loads[0].wait()

    def contract(t):
        here = tile_at(t)
        d_pre = dot(grad_low[...], v_down[here, :], ((1,), (1,))) * slope[:, here]
        d_pre_low[:, here] = d_pre.astype(LOW)
        acc_up[:, here] = jnp.sum(d_pre, axis=0, keepdims=True)

    over_tiles(inner // TILE, contract)
    loads[1].wait()
    pair.fill(0, lambda t: dot(d_pre_low[...], v_up[tile_at(t), :], ((1,), (1,))))
    pair.wait(0)

    def second_norm(rows):
        d_act = pair.total(0, rows)
        normed, factor = norm_of(middle[rows, :])
        column_sum(acc, 1, d_act * normed)
        column_sum(acc, 2, d_act)
        g = grad_state[rows, :] + norm_backward(d_act, normed, factor, vec[1])
        grad_mid[rows, :] = g
        mid_low[rows, :] = g.astype(LOW)
        column_sum(acc, 3, g)

    over_rows(length, second_norm)
    loads[2].wait()

    def attn_grad(t):
        here = tile_at(t)
        d_attn[:, here] = dot(mid_low[...], v_out[here, :], ((1,), (1,))).astype(LOW)

    over_tiles(half_width // TILE, attn_grad)
    for s in streams:
        s.onward(0)
    seg_row, seg_col = seg_row_col(segs)
    allowed = allowed_pairs(seg_col, seg_row)
    scale = 1.0 / math.sqrt(HEAD_DIM)
    for h in range(half_width // HEAD_DIM):
        q, k, v = (qkv[:, pl.ds(t * half_width + h * HEAD_DIM, HEAD_DIM)] for t in range(3))
        here = pl.ds(h * HEAD_DIM, HEAD_DIM)
        d_head = d_attn[:, here]
        full = head_probs(q, k, allowed, scale)
        delta = jnp.sum(
            d_head.astype(F32) * attn[:, here].astype(F32), axis=-1, keepdims=True
        )
        d_scores = (full * (dot(d_head, v, ((1,), (1,))) - delta)).astype(LOW)
        ends = (
            dot(d_scores, k) * scale,
            dot(d_scores, q, ((0,), (0,))) * scale,
            dot(full.astype(LOW), d_head, ((0,), (0,))),
        )
        for t, end in enumerate(ends):
            place = pl.ds(t * half_width + h * HEAD_DIM, HEAD_DIM)
            d_qkv[:, place] = end.astype(LOW)
            acc_qkv[:, place] = jnp.sum(end, axis=0, keepdims=True)
    loads[3].wait()
    pair.fill(1, lambda t: dot(d_qkv[...], v_qkv[tile_at(t), :], ((1,), (1,))))
    pair.wait(1)

    def first_norm(rows):
        d_act = pair.total(1, rows)
        normed, factor = norm_of(state[rows, :])
        column_sum(acc, 4, d_act * normed)
        column_sum(acc, 5, d_act)
        new_grad[rows, :] = grad_mid[rows, :] + norm_backward(d_act, normed, factor, vec[0])

    over_rows(length, first_norm)
    small_grad[...] = jnp.zeros_like(small_grad)
    first = (core == 0).astype(F32)
    for s in range(8):
        here = pl.ds(s * 128, 128)
        for vector, row in ((B_DOWN, 0), (G_TWO, 1), (S_TWO, 2), (B_OUT, 3), (G_ONE, 4), (S_ONE, 5)):
            small_grad[s, vector, 0:1, 0:128] = acc[row : row + 1, here] * first
        block = acc_up[:, pl.ds(s * TILE, TILE)]
        small_grad[s, B_UP, 0:1, :] = block * first
        small_grad[s, B_UP, 1:2, :] = block * (1.0 - first)
        at = (s // 4) * 2 * half_width + (s % 4) * 2 * HEAD_DIM
        heads = []
        for k in range(2):
            value = acc_qkv[:, pl.ds(at + k * HEAD_DIM, HEAD_DIM)]
            heads += [value * first, value * (1.0 - first)]
        small_grad[s, B_QV, 0:1, :] = jnp.concatenate(heads, axis=-1)
    for s in streams:
        s.finish(0)
    for s in streams:
        s.drain((0,))


def backward_block(layer, grad_state, record, segs, small, weights, grads):
    state, middle, qkv, attn, slope = record
    count = len(grads)
    length, width = state.shape
    inner = slope.shape[1]
    shapes = [
        ((length, width), F32),
        ((length, width), LOW),
        ((length, inner), LOW),
        ((length, width), LOW),
        ((length, 3 * width // 2), LOW),
        ((8, 8, 8, 256), F32),
    ]
    shapes = [jax.ShapeDtypeStruct(*s) for s in shapes]
    shapes += [jax.ShapeDtypeStruct(g.shape[1:], g.dtype) for g in grads]
    bufs = scatter_scratch([g.shape[3:] for g in grads], [g.dtype for g in grads], (0,))
    sems = [DMA((count, 18)), DMA((count, 18)), DMA((count, 5))] if count else []
    out = pl.pallas_call(
        functools.partial(backward_kernel, layer, count),
        out_shape=shapes,
        in_specs=[VMEM] * 8 + [ANY] * (4 + count),
        out_specs=[VMEM] * (6 + count),
        scratch_shapes=weight_scratch(weights)
        + pair_scratch(length, width)
        + [
            pltpu.VMEM((2, 1, width), F32),
            pltpu.VMEM((6, width), F32),
            pltpu.VMEM((1, inner), F32),
            pltpu.VMEM((1, 3 * width // 2), F32),
            pltpu.VMEM((length, width // 2), LOW),
            pltpu.VMEM((length, width), F32),
            DMA((4,)),
            DMA((2, width // TILE)),
            DMA((2, width // TILE)),
        ]
        + bufs
        + sems,
        compiler_params=pltpu.CompilerParams(
            collective_id=4 + layer, has_side_effects=True, vmem_limit_bytes=63 * 1024 * 1024
        ),
        name="backward_block",
    )(grad_state, state, middle, qkv, attn, slope, segs, small, *weights, *grads)
    return out[:6], out[6:]


def finish_kernel(layers, *refs):
    ins, outs = refs[: 5 * layers], refs[5 * layers :]
    o_qkv, o_out, o_up, o_down = outs[:4]
    for l in range(layers):
        up, down, qkv, out, small = ins[5 * l : 5 * l + 5]
        for s in range(8):
            for c in range(2):
                o_up[l, :, pl.ds((2 * s + c) * TILE, TILE)] = up[c, 0, :, pl.ds(s * TILE, TILE)].astype(F32)
        for c in range(2):
            o_down[l, c, 0] = down[c, 0].astype(F32)
            o_out[l, c, 0] = out[c, 0].astype(F32)
        for k in range(24):
            here = pl.ds(k * HEAD_DIM, HEAD_DIM)
            both = jnp.concatenate([qkv[0, 0, :, here], qkv[1, 0, :, here]], axis=-1)
            o_qkv[l, :, pl.ds(k * 128, 128)] = both.astype(F32)

        @pl.when(pl.program_id(0) == 0)
        def _():
            for v in range(8):
                o = outs[4 + v]
                size = o.shape[1]
                for part in range((size + 255) // 256):
                    span = min(size, 256)
                    o[l : l + 1, pl.ds(part * 256, span)] = (
                        small[0, v, part : part + 1, 0:span] + small[1, v, part : part + 1, 0:span]
                    )


def finish(finals, sizes):
    layers = len(finals)
    in_specs, args = [], []
    for f in finals:
        for m, a in enumerate(f):
            r, c = a.shape[3:]
            args.append(a.reshape(2, 8, r, c))
            if m < 4:
                in_specs.append(pl.BlockSpec((2, 1, r, c), lambda p: (0, p, 0, 0)))
            else:
                in_specs.append(pl.BlockSpec((2, 8, r, c), lambda p: (0, 0, 0, 0)))
    up, down, qkv, out = (a.shape[2:] for a in args[:4])
    shapes, specs = [], []
    for rows, cols in ((qkv[0], 2 * qkv[1]), (0, 0), (up[0], 2 * up[1])):
        if rows:
            shapes.append(jax.ShapeDtypeStruct((layers, 8 * rows, cols), F32))
            specs.append(pl.BlockSpec((layers, rows, cols), lambda p: (0, p, 0)))
        else:
            shapes.append(jax.ShapeDtypeStruct((layers, 2, 8) + out, F32))
            specs.append(pl.BlockSpec((layers, 2, 1) + out, lambda p: (0, 0, p, 0, 0)))
    shapes.append(jax.ShapeDtypeStruct((layers, 2, 8) + down, F32))
    specs.append(pl.BlockSpec((layers, 2, 1) + down, lambda p: (0, 0, p, 0, 0)))
    for size in sizes:
        shapes.append(jax.ShapeDtypeStruct((layers, size), F32))
        specs.append(pl.BlockSpec((layers, size), lambda p: (0, 0)))
    res = pl.pallas_call(
        functools.partial(finish_kernel, layers),
        out_shape=shapes,
        grid=(8,),
        in_specs=in_specs,
        out_specs=specs,
        name="finish",
    )(*args)
    o_out = res[1].reshape(layers, 16 * out[0], out[1])
    o_down = res[3].reshape(layers, 16 * down[0], down[1])
    return (res[0], o_out, res[2], o_down) + tuple(res[4:])


def prepare_kernel(where, up, down, qkv, out, segment_ids, *refs):
    vectors, refs = refs[:8], refs[8:]
    layers = up.shape[0]
    sub, core = where[0], where[1]
    for l in range(layers):
        o_up, o_down, o_qkv, o_out = refs[4 * l : 4 * l + 4]
        o_down[...] = down[l]
        o_out[...] = out[l]
        for s in range(8):
            at = pl.multiple_of((2 * s + core) * TILE, TILE)
            o_up[:, pl.ds(s * TILE, TILE)] = up[l, :, pl.ds(at, TILE)]
        for k in range(12):
            two = []
            for j in range(2):
                pair = qkv[l, :, pl.ds((2 * k + j) * 128, 128)]
                two.append(jnp.where(core == 0, pair[:, :HEAD_DIM], pair[:, HEAD_DIM:]))
            o_qkv[:, pl.ds(k * 128, 128)] = jnp.concatenate(two, axis=-1)
    small, segs = refs[4 * layers :]
    small[...] = jnp.zeros_like(small)
    for v, vector in enumerate(vectors):

        @pl.when(sub == v)
        def _():
            size = vector.shape[1]
            for part in range((size + 255) // 256):
                span = min(size, 256)
                block = vector[:, pl.ds(part * 256, span)].astype(F32)
                for l in range(layers):
                    small[2 * l + part : 2 * l + part + 1, 0:span] = block[l : l + 1]

    segs[...] = jnp.zeros_like(segs)
    for b in range(segs.shape[0]):
        segs[b, 0:1, 0 : segment_ids.shape[1]] = segment_ids[b : b + 1, :].astype(F32)


def prepare(weights, segment_ids, vectors):
    up, down, qkv, out = weights
    layers, rows = up.shape[:2]
    piece, down_rows, out_rows = rows // 8, down.shape[1] // 16, rows // 16
    where = jnp.stack(
        [lax.axis_index("xl") * 4 + lax.axis_index("y"), lax.axis_index("core")]
    ).astype(jnp.int32)
    per_layer = [
        (piece, up.shape[2] // 2),
        (down_rows, down.shape[2]),
        (piece, qkv.shape[2] // 2),
        (out_rows, out.shape[2]),
    ]
    shapes = [jax.ShapeDtypeStruct(e, LOW) for e in per_layer] * layers
    shapes += [jax.ShapeDtypeStruct((8, 256), F32), jax.ShapeDtypeStruct((2, 8, 128), F32)]
    by_row = lambda i, where: (0, where[0], 0)
    by_half = lambda i, where: (0, 8 * where[1] + where[0], 0)
    whole = lambda a: pl.BlockSpec(a.shape, lambda i, where: (0,) * len(a.shape))
    made = pl.pallas_call(
        prepare_kernel,
        out_shape=shapes,
        grid_spec=pltpu.PrefetchScalarGridSpec(
            num_scalar_prefetch=1,
            grid=(1,),
            in_specs=[
                pl.BlockSpec((layers, piece, up.shape[2]), by_row),
                pl.BlockSpec((layers, down_rows, down.shape[2]), by_half),
                pl.BlockSpec((layers, piece, qkv.shape[2]), by_row),
                pl.BlockSpec((layers, out_rows, out.shape[2]), by_half),
                whole(segment_ids),
            ]
            + [whole(v) for v in vectors],
            out_specs=[whole(e) for e in shapes],
        ),
        name="prepare",
    )(where, up, down, qkv, out, segment_ids, *vectors)
    owns = [made[4 * l : 4 * l + 4] for l in range(layers)]
    return owns, made[4 * layers], made[4 * layers + 1]


def per_device(
    inputs,
    segment_ids,
    weight_qkv,
    weight_out,
    weight_up,
    weight_down,
    bias_qv,
    bias_out,
    bias_up,
    bias_down,
    gain_one,
    shift_one,
    gain_two,
    shift_two,
    cotangent,
):
    layers, width = weight_qkv.shape[0], inputs.shape[-1]
    length = inputs.shape[1] * RING
    vectors = (bias_qv, bias_out, bias_up, bias_down, gain_one, shift_one, gain_two, shift_two)
    sizes = [v.shape[1] for v in vectors]
    owns, packed, segs = prepare((weight_up, weight_down, weight_qkv, weight_out), segment_ids, vectors)
    fulls, begun, wholes = gather_all(list(owns[0]) + [packed], list(owns[1]), [inputs, segs])
    state, segs = wholes[0].reshape(length, width), wholes[1]
    small = fulls[4].reshape(8, 8, 8, 256)
    records = []
    weights = [[w.reshape(-1, w.shape[-1]) for w in fulls[:4]]]
    for l in range(layers):
        carried, parts = (begun, []) if l == 0 else ([], [cotangent])
        made, fulls, wholes = forward_block(l, state, segs, small, weights[l], list(carried), parts)
        weights.append([w.reshape(-1, w.shape[-1]) for w in fulls])
        new_state, act_one, qkv, attn, middle, act_two, slope, hidden = made
        records.append(((state, middle, qkv, attn, slope), (act_one, act_two, hidden, attn)))
        state = new_state
    grad_state = wholes[0].reshape(length, width)
    pieces, sums = [], []
    for l in reversed(range(layers)):
        kept, (act_one, act_two, hidden, attn) = records[l]
        made, done = backward_block(l, grad_state, kept, segs, small, weights[l], pieces)
        sums += done
        grad_state, grad_low, d_pre_low, mid_low, d_qkv, small_grad = made
        tokens = ((0,), (0,))
        pieces = [
            dot(act_two, d_pre_low, tokens),
            dot(hidden, grad_low, tokens),
            dot(act_one, d_qkv, tokens),
            dot(attn, mid_low, tokens),
        ]
        pieces = [g.astype(LOW).reshape(RING, RING, RING, -1, g.shape[-1]) for g in pieces]
        pieces.append(small_grad.reshape(RING, RING, RING, 8, 256))
    quarter = (RING, length // RING, width)
    finals, parts = scatter_all(
        pieces, sums, [state.reshape(quarter), grad_state.reshape(quarter)]
    )
    finals = [finals[5 * l : 5 * l + 5] for l in range(layers)]
    return (parts[0], parts[1]) + finish(finals, sizes)


def solution(mesh):
    torus = Mesh(mesh.devices.reshape(4, 2, 4, 2, 2), AXES)
    tokens = P(("xh", "y", "xl", "core"), "z", None)
    weight = P(None, ("z", "xh"), None)
    vector = P(None, ("z", "xh"))
    return jax.shard_map(
        per_device,
        mesh=torus,
        in_specs=(tokens, P(("xh", "y", "xl", "core"), "z")) + (weight,) * 4 + (vector,) * 8 + (tokens,),
        out_specs=(tokens, tokens) + (weight,) * 4 + (vector,) * 8,
        check_vma=False,
    )
```

time: 477 us -> 409 us (0.86)
  Pallas kernels: 295 us -> 368 us
  local copies, waits for them, and re-layouts: 52.7 us -> 1.73 us
  matrix products: 72.3 us -> 33 us
  other arithmetic: 39.8 us -> 0.59 us
  waiting for transfers between devices: 6.54 us -> 0 us
    pallas_call x6 -> x8, Pallas kernels: 295 us -> 368 us  [the longest x1 114 us: scatter_all(): pl.pallas_call(functools.partial(scatter_kernel, count, done, moved), out...]
    dot_general x24 -> x8, matrix products: 72.3 us -> 33 us  [dot(): lax.dot_general(left, right, (dims, ((), ())), preferred_element_type=F32)]
    reduce_sum x17 -> x0, other arithmetic: 21.6 us -> none  [the longest x2 4.45 us: per_device(): gb_out = jnp.sum(grad_middle, axis=0)]
    unnamed x123 -> x30, local copies, waits for them, and re-layouts: 16.6 us -> 1.73 us
    another operation x18 -> x0, local copies, waits for them, and re-layouts: 9.72 us -> none  [the longest x2 3.15 us: per_device(): up = pick(weight_up[l].reshape(8, rows // 8, 8, 2, inner // 16), sub, 0)]
    another operation x13 -> x1, other arithmetic: 8.26 us -> 0.59 us  [prepare(): jnp.stack([lax.axis_index('xl') * 4 + lax.axis_index('y'), lax.axis_index...]
    reshape x11 -> x0, local copies, waits for them, and re-layouts: 6.79 us -> none  [the longest x2 3.3 us: per_device(): qkv = qkv.reshape(2, rows, 24, HEAD_DIM).transpose(1, 2, 0, 3)]
    transpose x6 -> x0, local copies, waits for them, and re-layouts: 6.72 us -> none  [the longest x4 3.38 us: per_device(): up = up.reshape(2, rows, 8, inner // 16).transpose(1, 2, 0, 3)]
  transfers between devices with their start and end apart: 8 -> 0, of which waited for: 3 -> 0; matrix products, arithmetic and copies ran while one was open for 8% -> 0% of each run, Pallas kernels for 0% -> 0%
where the time goes in v2:
time: 409 us; the launch traced here: 404 us
  Pallas kernels  368 us (90%)
  matrix products  33 us (8%)
    pallas_call x1, Pallas kernels, scatter_all(): pl.pallas_call(functools.partial(scatter_kernel, count, done, moved), out...  114 us
    pallas_call x2, Pallas kernels, backward_block(): pl.pallas_call(functools.partial(backward_kernel, layer, count), out_shap...  85.8 us
    pallas_call x1, Pallas kernels, gather_all(): pl.pallas_call(functools.partial(gather_kernel, count, len(owns), moved),...  80.2 us
    pallas_call x2, Pallas kernels, forward_block(): pl.pallas_call(functools.partial(forward_kernel, layer, count, moved), ou...  75.2 us
    dot_general x8, matrix products, dot(): lax.dot_general(left, right, (dims, ((), ())), preferred_element_type=F32)  33 us
    pallas_call x1, Pallas kernels, finish(): pl.pallas_call(functools.partial(finish_kernel, layers), out_shape=shapes...  9.81 us

profile of v2, /device:TPU:1, one launch (start us, length us, event | category | flops | bytes accessed | tf_op | source)
XLA Modules:
  0.0 404.4 jit_solution(18407114456930893439)
XLA Ops:
  0.7 0.6 pad_add_fusion.where
  1.2 2.8 prepare.1
  4.0 80.2 %gather_all.1 = (bf16[4,4,4,16,2048]{4,3,2,1,0:T(8,128)(2,1)}, bf16[4,4,4,32,1024]{4,3,2,1,0:T(8,128)(2,1)}, bf16[4,4,4,16,1536]{4,3,2,1,0:T(8,128)(2,1)}, bf16[...) custom-call(bf16[16,2048]{1,0:T(8,128)(2,1)} %get-tuple-element.97.r, ...), custom_call_target="tpu_custom_call" | custom-call | tf_op jit(solution)/shard_map/gather_all/pallas_call | solution.py:259
  84.2 44.4 %forward_block.2 = (f32[320,1024]{1,0:T(8,128)}, bf16[320,1024]{1,0:T(8,128)(2,1)}, bf16[320,1536]{1,0:T(8,128)(2,1)}, bf16[320,512]{1,0:T(8,128)(2,1)}, f32[320...) custom-call(f32[320,1024]{1,0:T(8,128)} %bitcast.71, ...), custom_call_target="tpu_custom_call", output_to_operand_aliasing={{8}: (7, {}), {9}: (8, {}), {10}: (9, {}), {11}: (10, {})} | custom-call | tf_op jit(solution)/shard_map/forward_block/pallas_call | solution.py:927
  128.6 30.8 %forward_block.3 = (f32[320,1024]{1,0:T(8,128)}, bf16[320,1024]{1,0:T(8,128)(2,1)}, bf16[320,1536]{1,0:T(8,128)(2,1)}, bf16[320,512]{1,0:T(8,128)(2,1)}, f32[320...) custom-call(f32[320,1024]{1,0:T(8,128)} %get-tuple-element.119.refs_, ...), custom_call_target="tpu_custom_call" | custom-call | tf_op jit(solution)/shard_map/forward_block/pallas_call | solution.py:927
  159.4 0.0 copy-start.1
  159.4 0.0 copy-start.12
  159.4 31.5 %backward_block.2 = (f32[320,1024]{1,0:T(8,128)}, bf16[320,1024]{1,0:T(8,128)(2,1)}, bf16[320,2048]{1,0:T(8,128)(2,1)}, bf16[320,1024]{1,0:T(8,128)(2,1)}, bf16[...) custom-call(f32[320,1024]{1,0:T(8,128)} %bitcast.85, f32[320,1024]{1,0:T(8,128)} %get-tuple-element.119.refs_0_.refs_1_, ...), custom_call_target="tpu_custom_call" | custom-call | tf_op jit(solution)/shard_map/backward_block/pallas_call | solution.py:1113
  190.9 0.0 copy-done.1
  190.9 2.8 convolution_convert_fusion.7
  193.7 0.0 copy-done.12
  193.7 4.8 %convolution_convert_fusion.3 = bf16[1024,1536]{1,0:T(8,128)(2,1)} fusion(bf16[320,1024]{1,0:T(8,128)(2,1)S(1)} %copy-done.12, bf16[320,1536]{1,0:T(8,128)(2,1)} %get-tuple-element.139), kind=kOutput, calls=%fused_computation.3 | convolution fusion | flops 1008205824 | bytes 4784128 | tf_op jit(solution)/shard_map/dot_general | solution.py:650
  198.6 0.0 copy-done.5
  198.6 0.0 copy-done.13
  198.6 4.4 %convolution_convert_fusion.4 = bf16[2048,1024]{1,0:T(8,128)(2,1)} fusion(bf16[320,2048]{1,0:T(8,128)(2,1)S(1)} %copy-done.5, bf16[320,1024]{1,0:T(8,128)(2,1)S(1)} %copy-done.13), kind=kOutput, calls=%fused_computation.4 | convolution fusion | flops 1344274432 | bytes 6160384 | tf_op jit(solution)/shard_map/dot_general | solution.py:650
  203.0 0.0 copy-done.6
  203.0 0.0 copy-done.11
  203.0 4.4 %convolution_convert_fusion.5 = bf16[1024,2048]{1,0:T(8,128)(2,1)} fusion(bf16[320,1024]{1,0:T(8,128)(2,1)S(1)} %copy-done.11, bf16[320,2048]{1,0:T(8,128)(2,1)S(1)} %copy-done.6), kind=kOutput, calls=%fused_computation.5 | convolution fusion | flops 1344274432 | bytes 6160384 | tf_op jit(solution)/shard_map/dot_general | solution.py:650
  207.4 54.3 %backward_block.3 = (f32[320,1024]{1,0:T(8,128)}, bf16[320,1024]{1,0:T(8,128)(2,1)}, bf16[320,2048]{1,0:T(8,128)(2,1)}, bf16[320,1024]{1,0:T(8,128)(2,1)}, bf16[...) custom-call(f32[320,1024]{1,0:T(8,128)} %get-tuple-element.129.refs_, ...), custom_call_target="tpu_custom_call" | custom-call | tf_op jit(solution)/shard_map/backward_block/pallas_call | solution.py:1113
  261.7 0.0 copy-done
  261.7 2.8 convolution_convert_fusion.6
  264.5 0.0 copy-done.9
  264.5 5.8 %convolution_convert_fusion.2 = bf16[1024,2048]{1,0:T(8,128)(2,1)} fusion(bf16[320,1024]{1,0:T(8,128)(2,1)S(1)} %copy-done.9, bf16[320,2048]{1,0:T(8,128)(2,1)} %get-tuple-element.142), kind=kOutput, calls=%fused_computation.2 | convolution fusion | flops 1344274432 | bytes 6160384 | tf_op jit(solution)/shard_map/dot_general | solution.py:650
  270.3 0.0 copy-done.7
  270.3 0.0 copy-done.8
  270.4 3.5 convolution_convert_fusion
  273.9 0.0 copy-done.10
  273.9 4.4 %convolution_convert_fusion.1 = bf16[2048,1024]{1,0:T(8,128)(2,1)} fusion(bf16[320,2048]{1,0:T(8,128)(2,1)S(1)} %copy-done.4, bf16[320,1024]{1,0:T(8,128)(2,1)S(1)} %copy-done.10), kind=kOutput, calls=%fused_computation.1 | convolution fusion | flops 1344274432 | bytes 6160384 | tf_op jit(solution)/shard_map/dot_general | solution.py:650
  278.3 114.4 %scatter_all.1 = (bf16[2,2,4,16,2048]{4,3,2,1,0:T(8,128)(2,1)}, bf16[2,2,4,32,1024]{4,3,2,1,0:T(8,128)(2,1)}, bf16[2,2,4,16,1536]{4,3,2,1,0:T(8,128)(2,1)}, bf16...) custom-call(bf16[4,4,4,16,2048]{4,3,2,1,0:T(8,128)(2,1)} %bitcast.74, ...), custom_call_target="tpu_custom_call" | custom-call | tf_op jit(solution)/shard_map/scatter_all/pallas_call | solution.py:613
  392.7 9.8 %finish.1 = (f32[2,128,3072]{2,1,0:T(8,128)}, f32[2,2,8,8,1024]{4,3,2,1,0:T(8,128)}, f32[2,128,4096]{2,1,0:T(8,128)}, f32[2,2,8,32,1024]{4,3,2,1,0:T(8,128)}, f3...) custom-call(bf16[2,8,16,2048]{3,2,1,0:T(8,128)(2,1)} %bitcast.86, ...), custom_call_target="tpu_custom_call" | custom-call | tf_op jit(solution)/shard_map/finish/pallas_call | solution.py:1194
  402.6 0.8 copy.39
  403.4 0.8 copy.40
  (15 shorter events, 0.0 us)
Async XLA Ops:
  159.4 31.5 %copy-start.1 = (bf16[320,512]{1,0:T(8,128)(2,1)S(1)}, bf16[320,512]{1,0:T(8,128)(2,1)}, u32[]{:S(2)}) copy-start(bf16[320,512]{1,0:T(8,128)(2,1)} %get-tuple-element.127.refs_4_) | copy-start | bytes 983044
  159.4 34.3 %copy-start.12 = (bf16[320,1024]{1,0:T(8,128)(2,1)S(1)}, bf16[320,1024]{1,0:T(8,128)(2,1)}, u32[]{:S(2)}) copy-start(bf16[320,1024]{1,0:T(8,128)(2,1)} %get-tuple-element.138) | copy-start | bytes 1966084
  193.7 4.9 %copy-start.5 = (bf16[320,2048]{1,0:T(8,128)(2,1)S(1)}, bf16[320,2048]{1,0:T(8,128)(2,1)}, u32[]{:S(2)}) copy-start(bf16[320,2048]{1,0:T(8,128)(2,1)} %get-tuple-element.136) | copy-start | bytes 3932164
  193.7 4.9 %copy-start.13 = (bf16[320,1024]{1,0:T(8,128)(2,1)S(1)}, bf16[320,1024]{1,0:T(8,128)(2,1)}, u32[]{:S(2)}) copy-start(bf16[320,1024]{1,0:T(8,128)(2,1)} %get-tuple-element.137) | copy-start | bytes 1966084
  198.6 4.4 %copy-start.6 = (bf16[320,2048]{1,0:T(8,128)(2,1)S(1)}, bf16[320,2048]{1,0:T(8,128)(2,1)}, u32[]{:S(2)}) copy-start(bf16[320,2048]{1,0:T(8,128)(2,1)} %get-tuple-element.135) | copy-start | bytes 3932164
  198.6 4.4 %copy-start.11 = (bf16[320,1024]{1,0:T(8,128)(2,1)S(1)}, bf16[320,1024]{1,0:T(8,128)(2,1)}, u32[]{:S(2)}) copy-start(bf16[320,1024]{1,0:T(8,128)(2,1)} %get-tuple-element.134) | copy-start | bytes 1966084
  207.4 54.3 %copy-start = (bf16[320,512]{1,0:T(8,128)(2,1)S(1)}, bf16[320,512]{1,0:T(8,128)(2,1)}, u32[]{:S(2)}) copy-start(bf16[320,512]{1,0:T(8,128)(2,1)} %get-tuple-element.132.refs_4_) | copy-start | bytes 983044
  207.4 57.1 %copy-start.9 = (bf16[320,1024]{1,0:T(8,128)(2,1)S(1)}, bf16[320,1024]{1,0:T(8,128)(2,1)}, u32[]{:S(2)}) copy-start(bf16[320,1024]{1,0:T(8,128)(2,1)} %get-tuple-element.118) | copy-start | bytes 1966084
  264.5 5.8 %copy-start.7 = (bf16[320,1536]{1,0:T(8,128)(2,1)S(1)}, bf16[320,1536]{1,0:T(8,128)(2,1)}, u32[]{:S(2)}) copy-start(bf16[320,1536]{1,0:T(8,128)(2,1)} %get-tuple-element.146) | copy-start | bytes 2949124
  264.5 5.8 %copy-start.8 = (bf16[320,1024]{1,0:T(8,128)(2,1)S(1)}, bf16[320,1024]{1,0:T(8,128)(2,1)}, u32[]{:S(2)}) copy-start(bf16[320,1024]{1,0:T(8,128)(2,1)} %get-tuple-element.145) | copy-start | bytes 1966084
  270.4 3.5 copy-start.4
  270.4 3.5 copy-start.10
  392.7 9.8 %copy-start.3 = (f32[2,80,1024]{2,1,0:T(8,128)S(1)}, f32[2,80,1024]{2,1,0:T(8,128)}, u32[]{:S(2)}) copy-start(f32[2,80,1024]{2,1,0:T(8,128)} %get-tuple-element.194) | copy-start | bytes 1966084
  392.7 10.7 %copy-start.2 = (f32[2,80,1024]{2,1,0:T(8,128)S(1)}, f32[2,80,1024]{2,1,0:T(8,128)}, u32[]{:S(2)}) copy-start(f32[2,80,1024]{2,1,0:T(8,128)} %get-tuple-element.195) | copy-start | bytes 1966084

commit v3 on v2

--- a/solution.py
+++ b/solution.py
@@ -14,6 +14,9 @@
 ANY = pl.BlockSpec(memory_space=pl.ANY)
 VMEM = pl.BlockSpec(memory_space=pltpu.VMEM)
 DMA = pltpu.SemaphoreType.DMA
+SCATTERS = ("xyz", "yzx", "zxy", "yxz", "xyz", "zyx", "yzx", "yxz", "yzx")
+SPLIT = 4
+UP_PART, DOWN_PART = (5, 8), (3, 4)
 ORDERS = ("xyz", "zxy", "yzx", "yzx")
 
 
@@ -269,35 +272,41 @@
     return out[: len(owns)], out[len(owns) : count], out[count:]
 
 
-def scatter_scratch(ends, kinds, stages):
-    scratch = []
-    for (r, c), kind in zip(ends, kinds):
-        if 0 in stages:
-            scratch.append(pltpu.VMEM((4, RING, RING, r, c // 2), kind))
-        for stage in stages:
-            scratch.append(pltpu.VMEM((6,) + (RING,) * (2 - stage) + (r, c // 2), kind))
-        if len(stages) > 1:
-            for stage in stages:
-                scratch.append(pltpu.VMEM((RING,) * (2 - stage) + (r, c), kind))
+def scatter_scratch(end, kind, start, last):
+    r, c = end
+    scratch = [] if start else [pltpu.VMEM((4, RING, RING, r, c // 2), kind)]
+    for stage in range(start, 3):
+        scratch.append(pltpu.VMEM((6,) + (RING,) * (2 - stage) + (r, c // 2), kind))
+    for stage in range(start, 3 if last else 2):
+        scratch.append(pltpu.VMEM((RING,) * (2 - stage) + (r, c), kind))
     return scratch
 
 
+def scatter_of(pos, m, source, bufs, sums, sems):
+    start = 1 if m < SPLIT else 0
+    stages = 3 - start
+    own = None if start else bufs[0]
+    rest = list(bufs[1 - start :])
+    boxes, more = [None] * start + rest[:stages], rest[stages:]
+    sums = ([source] if start else []) + more + list(sums)
+    return Scatter(pos, SCATTERS[m], start, None if start else source, own, boxes, sums, *sems)
+
+
 class Scatter:
-    def __init__(self, pos, order, grad, own, boxes, sums, send, recv, local):
-        self.pos, self.order, self.grad = pos, order, grad
+    def __init__(self, pos, order, start, grad, own, boxes, sums, send, recv, local, base=0):
+        self.pos, self.order, self.start, self.grad = pos, order, start, grad
         self.own, self.boxes, self.sums = own, boxes, sums
         self.send, self.recv, self.local = send, recv, local
-        self.part = sums[0].shape[-1] // 2
-
-    def piece(self, stage, shift, which=None):
+        self.part, self.base = sums[0].shape[-1] // 2, base
+
+    def piece(self, stage, shift, which):
         axis = self.order[stage]
         left = [a for a in "zxy" if a in self.order[stage:]]
         source = self.grad if stage == 0 else self.sums[stage - 1]
         at = lax.rem(self.pos[axis] + shift + RING, RING)
         index = tuple(at if a == axis else slice(None) for a in left) + (slice(None),)
-        if which is None:
-            return source.at[index + (slice(None),)]
-        return source.at[index + (pl.ds(which * self.part, self.part),)]
+        base = self.base if stage == 0 else 0
+        return source.at[index + (pl.ds(base + which * self.part, self.part),)]
 
     def box(self, stage, kind):
         return self.boxes[stage].at[kind]
@@ -328,12 +337,12 @@
     def begin(self, stage):
         for kind in range(4):
             self.copy(stage, kind).start()
-        if stage == 0:
+        if stage == 0 and self.own is not None:
             for load in self.loads():
                 load.start()
 
     def term(self, stage, slot):
-        if stage == 0:
+        if stage == 0 and self.own is not None:
             return self.own.at[slot]
         shift, which = ((1, 0), (-1, 1), (0, 0), (0, 1))[slot]
         return self.piece(stage, shift, which)
@@ -347,19 +356,18 @@
                 total = total + t[index].astype(jnp.float32)
             target[index] = total.astype(target.dtype)
 
-        if lead == 0:
-            one((slice(None), slice(None)))
+        if lead < 2:
+            one((slice(None),) * (lead + 2))
             return
 
         def body(i, carry):
-            where = (i // RING, lax.rem(i, RING)) if lead == 2 else (i,)
-            one(where + (slice(None), slice(None)))
+            one((i, slice(None), slice(None), slice(None)))
             return carry
 
-        lax.fori_loop(0, RING**lead, body, 0)
+        lax.fori_loop(0, RING, body, 0)
 
     def onward(self, stage):
-        if stage == 0:
+        if stage == 0 and self.own is not None:
             for load in self.loads():
                 load.wait()
         for slot, kind in ((0, 0), (1, 2)):
@@ -380,21 +388,36 @@
                 (self.term(stage, 2 + which),) + tuple(self.box(stage, k) for k in kinds),
             )
 
-    def drain(self, stages):
-        for stage in stages:
+    def steps(self):
+        return 2 * (3 - self.start) + 1
+
+    def step(self, at):
+        if at == 0:
+            self.begin(self.start)
+        elif at < self.steps():
+            stage = self.start + (at - 1) // 2
+            if at % 2:
+                self.onward(stage)
+            else:
+                self.finish(stage)
+                if stage < 2:
+                    self.begin(stage + 1)
+
+    def drain(self, stages=None):
+        for stage in range(self.start, 3) if stages is None else stages:
             for kind in range(6):
                 self.copy(stage, kind).wait_send()
 
 
 class Publish:
-    def __init__(self, pos, order, source, final, sends, recvs, local):
-        self.pos, self.order, self.source, self.final = pos, order, source, final
+    def __init__(self, pos, across, source, final, sends, recvs, local):
+        self.pos, self.across, self.source, self.final = pos, across, source, final
         self.sends_f, self.recvs_f, self.local = sends, recvs, local
         self.core, self.xl = lax.axis_index("core"), lax.axis_index("xl")
         self.part = source.shape[-1] // 2
 
     def across_first(self):
-        return self.order[0] != "y"
+        return self.across
 
     def block(self, shift):
         yi = lax.rem(self.pos["y"] + shift + RING, RING)
@@ -485,36 +508,30 @@
             self.spread(kind).wait_send()
 
 
-def scatter_kernel(count, done, moved, *refs):
-    grads, given, wholes = refs[:count], refs[count : count + done], refs[count + done : count + done + moved]
-    refs = refs[count + done + moved :]
-    finals, parts = refs[: count + done], refs[count + done : count + done + moved]
-    refs = refs[count + done + moved :]
-    bufs, more = refs[: 7 * count], refs[7 * count : 7 * count + 4 * done]
-    send, recv, local, sends_f, recvs_f, keeps, send_t, recv_t, local_t = refs[7 * count + 4 * done :]
+MATRICES = 9
+
+
+def scatter_kernel(moved, *refs):
+    grads, given = refs[:MATRICES], refs[MATRICES : 2 * MATRICES]
+    wholes, refs = refs[2 * MATRICES : 2 * MATRICES + moved], refs[2 * MATRICES + moved :]
+    finals, parts = refs[: 2 * MATRICES], refs[2 * MATRICES : 2 * MATRICES + moved]
+    refs = refs[2 * MATRICES + moved :]
+    send, recv, local, sends_f, recvs_f, keeps, send_t, recv_t, local_t = refs[-9:]
     pos = positions()
     core = lax.axis_index("core")
     greet(pos, True)
-    streams = []
-    for m in range(count):
-        own = bufs[7 * m : 7 * m + 7]
-        streams.append((ORDERS[m % 4], grads[m], own[0], own[1:4], own[4:7]))
-    for m in range(done):
-        own = more[4 * m : 4 * m + 4]
-        streams.append((ORDERS[m % 4], None, None, (None,) + own[:2], (given[m],) + own[2:]))
-    streams = [
-        Scatter(pos, *args, send.at[m], recv.at[m], local.at[m]) for m, args in enumerate(streams)
+    streams, at = [], 0
+    for m in range(MATRICES):
+        take = 4 if m < SPLIT else 7
+        sems = (send.at[m], recv.at[m], local.at[m])
+        streams.append(scatter_of(pos, m, grads[m], refs[at : at + take], (), sems))
+        at += take
+    news = [
+        Publish(
+            pos, m % MATRICES in (0, 1, 4, 5, 6), source, finals[m], sends_f.at[m], recvs_f.at[m], keeps.at[m]
+        )
+        for m, source in enumerate([s.sums[2] for s in streams] + list(given))
     ]
-    news = [
-        Publish(pos, s.order, s.sums[2], finals[m], sends_f.at[m], recvs_f.at[m], keeps.at[m])
-        for m, s in enumerate(streams)
-    ]
-    late, ahead = streams[:count], streams[count:]
-    last, early = news[:count], news[count:]
-    for s in ahead:
-        s.begin(1)
-    for s in late:
-        s.begin(0)
     sender = pos["z"] // 2 == core
     slot = lax.rem(pos["z"], 2)
 
@@ -537,45 +554,16 @@
             def _():
                 homeward(a, q).start()
 
-    def move(group, places, stage):
-        for s, n in zip(group, places):
-            s.finish(stage)
-            if stage < 2:
-                s.begin(stage + 1)
-            else:
-                n.publish(0)
-
-    def step(places, at):
-        for n in places:
-            n.publish(at)
-
-    for s in ahead:
-        s.onward(1)
-    for s in late:
-        s.onward(0)
-    move(ahead, early, 1)
-    move(late, last, 0)
-    for s in ahead:
-        s.onward(2)
-    for s in late:
-        s.onward(1)
-    move(ahead, early, 2)
-    move(late, last, 1)
-    step(early, 1)
-    for s in late:
-        s.onward(2)
-    step(early, 2)
-    move(late, last, 2)
-    step(early, 3)
-    step(last, 1)
-    step(last, 2)
-    step(early, 4)
-    step(last, 3)
-    step(last, 4)
-    for s in late:
-        s.drain((0, 1, 2))
-    for s in ahead:
-        s.drain((1, 2))
+    for at in range(11):
+        for n in news[MATRICES:]:
+            if at < 5:
+                n.publish(at)
+        for s, n in zip(streams, news):
+            s.step(at)
+            if 0 <= at - s.steps() + 1 < 5:
+                n.publish(at - s.steps() + 1)
+    for s in streams:
+        s.drain()
     for n in news:
         n.drain()
     for a in range(moved):
@@ -603,26 +591,27 @@
 
 
 def scatter_all(grads, given, wholes):
-    count, done, moved = len(grads), len(given), len(wholes)
-    ends = [g.shape[-2:] for g in grads + given]
-    kinds = [g.dtype for g in grads + given]
+    moved = len(wholes)
+    ends = [g.shape[-2:] for g in grads] * 2
+    kinds = [g.dtype for g in grads] * 2
     shapes = [jax.ShapeDtypeStruct((2, 2, RING) + e, k) for e, k in zip(ends, kinds)]
     shapes += [jax.ShapeDtypeStruct((2,) + w.shape[1:], w.dtype) for w in wholes]
-    bufs = scatter_scratch(ends[:count], kinds[:count], (0, 1, 2))
-    bufs += scatter_scratch(ends[count:], kinds[count:], (1, 2))
+    bufs = []
+    for m in range(MATRICES):
+        bufs += scatter_scratch(ends[m], kinds[m], 1 if m < SPLIT else 0, True)
     out = pl.pallas_call(
-        functools.partial(scatter_kernel, count, done, moved),
+        functools.partial(scatter_kernel, moved),
         out_shape=shapes,
-        in_specs=[ANY] * count + [VMEM] * done + [ANY] * moved,
-        out_specs=[ANY] * (count + done + moved),
+        in_specs=[VMEM] * SPLIT + [ANY] * (2 * MATRICES - SPLIT + moved),
+        out_specs=[ANY] * (2 * MATRICES + moved),
         scratch_shapes=bufs
         + [
-            DMA((count + done, 18)),
-            DMA((count + done, 18)),
-            DMA((count + done, 5)),
-            DMA((count + done, 6)),
-            DMA((count + done, 6)),
-            DMA((count + done,)),
+            DMA((MATRICES, 18)),
+            DMA((MATRICES, 18)),
+            DMA((MATRICES, 5)),
+            DMA((2 * MATRICES, 6)),
+            DMA((2 * MATRICES, 6)),
+            DMA((2 * MATRICES,)),
             DMA((moved, RING)),
             DMA((moved, 2)),
             DMA((moved,)),
@@ -632,7 +621,7 @@
         ),
         name="scatter_all",
     )(*grads, *given, *wholes)
-    return out[: count + done], out[count + done :]
+    return out[:MATRICES], out[MATRICES : 2 * MATRICES], out[2 * MATRICES :]
 
 
 NORM_EPS = 1e-05
@@ -954,14 +943,17 @@
 
 
 def backward_kernel(layer, count, *refs):
-    grad_state, state, middle, qkv, attn, slope, segs, small = refs[:8]
-    w_up, w_down, w_qkv, w_out = refs[8:12]
-    grads, refs = refs[12 : 12 + count], refs[12 + count :]
-    new_grad, grad_low, d_pre_low, mid_low, d_qkv, small_grad = refs[:6]
-    sums, refs = refs[6 : 6 + count], refs[6 + count :]
-    v_qkv, v_out, v_up, v_down, terms, box, vec, acc, acc_up, acc_qkv, d_attn, grad_mid = refs[:12]
-    load, p_send, p_recv = refs[12:15]
-    rings = refs[15:]
+    grad_state, state, middle, qkv, attn, slope, hidden, act_one, act_two, segs, small = refs[:11]
+    w_up, w_down, w_qkv, w_out = refs[11:15]
+    given, refs = refs[15 : 15 + count], refs[15 + count :]
+    new_grad, totals = refs[0], refs[1:5]
+    g_heads, g_out, small_grad = refs[5:8], refs[8], refs[9]
+    sums, refs = refs[10 : 10 + count], refs[10 + count :]
+    v_qkv, v_out, v_up, v_down, terms, box, vec, acc, acc_up, acc_qkv = refs[:10]
+    grad_low, d_pre_low, mid_low, d_qkv, d_attn = refs[10:15]
+    boxes, refs = refs[15:19], refs[19:]
+    load, p_send, p_recv, o_send, o_recv = refs[:5]
+    rings = refs[5:]
     core = lax.axis_index("core")
     length, width = state.shape
     half_width = width // 2
@@ -972,33 +964,44 @@
     ]
     for copy in loads:
         copy.start()
-    if count:
-        pos = positions()
-        greet(pos, False)
-        send, recv, local = rings[2 * count :]
-        streams = [
-            Scatter(
-                pos,
-                ORDERS[m % 4],
-                grads[m],
-                rings[2 * m],
-                (rings[2 * m + 1],),
-                (sums[m],),
-                send.at[m],
-                recv.at[m],
-                local.at[m],
-            )
-            for m in range(count)
-        ]
+    pos = positions()
+    greet(pos, False)
+    streams, at = [], 0
+    for m in range(count):
+        take = 3 if m < SPLIT else 6
+        sems = [rings[len(rings) - 3 + k].at[m] for k in range(3)]
+        streams.append(scatter_of(pos, m, given[m], rings[at : at + take], (sums[m],), sems))
+        at += take
+    own = [
+        Scatter(
+            pos,
+            SCATTERS[m],
+            0,
+            v_up if m < 2 else v_down,
+            None,
+            (boxes[m],),
+            (totals[m],),
+            o_send.at[m],
+            o_recv.at[m],
+            None,
+            totals[m - 1].shape[-1] if m % 2 else 0,
+        )
+        for m in range(SPLIT)
+    ]
+
+    def carry(at):
         for s in streams:
-            s.begin(0)
-    else:
-        greet_pair()
-        streams = ()
+            s.step(at)
+
+    carry(0)
     pair = Pair(terms, box, p_send, p_recv)
     fill_vector(vec.at[0], small, G_ONE, layer)
     fill_vector(vec.at[1], small, G_TWO, layer)
     acc[...] = jnp.zeros_like(acc)
+    tokens = ((0,), (0,))
+
+    def down_rows(t):
+        return (t // 2, pl.ds(lax.rem(t, 2) * 2, 2))
 
     def lower(rows):
         g = grad_state[rows, :]
@@ -1010,13 +1013,32 @@
 
     def contract(t):
         here = tile_at(t)
-        d_pre = dot(grad_low[...], v_down[here, :], ((1,), (1,))) * slope[:, here]
+        w = v_down[down_rows(t)].reshape(TILE, width)
+        d_pre = dot(grad_low[...], w, ((1,), (1,))) * slope[:, here]
         d_pre_low[:, here] = d_pre.astype(LOW)
         acc_up[:, here] = jnp.sum(d_pre, axis=0, keepdims=True)
 
     over_tiles(inner // TILE, contract)
+    carry(1)
+
+    def down_grad(t):
+        value = dot(hidden[:, tile_at(t)], grad_low[...], tokens)
+        v_down[down_rows(t)] = value.reshape(2, RING, 32, width).astype(LOW)
+
+    over_tiles(inner // TILE, down_grad)
+    for s in own[2:]:
+        s.begin(0)
     loads[1].wait()
-    pair.fill(0, lambda t: dot(d_pre_low[...], v_up[tile_at(t), :], ((1,), (1,))))
+    pair.fill(0, lambda t: dot(d_pre_low[...], v_up[t].reshape(TILE, inner), ((1,), (1,))))
+
+
+    def up_grad(t):
+        value = dot(act_two[:, tile_at(t)], d_pre_low[...], tokens)
+        v_up[t] = value.reshape(RING, RING, 16, inner).astype(LOW)
+
+    over_tiles(width // TILE, up_grad)
+    for s in own[:2]:
+        s.begin(0)
     pair.wait(0)
 
     def second_norm(rows):
@@ -1025,11 +1047,12 @@
         column_sum(acc, 1, d_act * normed)
         column_sum(acc, 2, d_act)
         g = grad_state[rows, :] + norm_backward(d_act, normed, factor, vec[1])
-        grad_mid[rows, :] = g
+        new_grad[rows, :] = g
         mid_low[rows, :] = g.astype(LOW)
         column_sum(acc, 3, g)
 
     over_rows(length, second_norm)
+    carry(2)
     loads[2].wait()
 
     def attn_grad(t):
@@ -1037,8 +1060,12 @@
         d_attn[:, here] = dot(mid_low[...], v_out[here, :], ((1,), (1,))).astype(LOW)
 
     over_tiles(half_width // TILE, attn_grad)
-    for s in streams:
-        s.onward(0)
+
+    def out_grad(t):
+        value = dot(attn[:, tile_at(t)], mid_low[...], tokens)
+        g_out[pl.ds(t * 2, 2)] = value.reshape(2, RING, RING, 8, width).astype(LOW)
+
+    over_tiles(half_width // TILE, out_grad)
     seg_row, seg_col = seg_row_col(segs)
     allowed = allowed_pairs(seg_col, seg_row)
     scale = 1.0 / math.sqrt(HEAD_DIM)
@@ -1060,8 +1087,21 @@
             place = pl.ds(t * half_width + h * HEAD_DIM, HEAD_DIM)
             d_qkv[:, place] = end.astype(LOW)
             acc_qkv[:, place] = jnp.sum(end, axis=0, keepdims=True)
+        if h == 5:
+            for s in own:
+                s.onward(0)
+    carry(3)
     loads[3].wait()
     pair.fill(1, lambda t: dot(d_qkv[...], v_qkv[tile_at(t), :], ((1,), (1,))))
+
+    def head_grad(t):
+        value = dot(act_one[:, tile_at(t)], d_qkv[...], tokens)
+        for part in range(3):
+            third = value[:, part * half_width : (part + 1) * half_width]
+            g_heads[part][t] = third.reshape(RING, RING, 16, half_width).astype(LOW)
+
+    over_tiles(width // TILE, head_grad)
+    carry(4)
     pair.wait(1)
 
     def first_norm(rows):
@@ -1069,89 +1109,108 @@
         normed, factor = norm_of(state[rows, :])
         column_sum(acc, 4, d_act * normed)
         column_sum(acc, 5, d_act)
-        new_grad[rows, :] = grad_mid[rows, :] + norm_backward(d_act, normed, factor, vec[0])
+        new_grad[rows, :] += norm_backward(d_act, normed, factor, vec[0])
 
     over_rows(length, first_norm)
     small_grad[...] = jnp.zeros_like(small_grad)
     first = (core == 0).astype(F32)
     for s in range(8):
         here = pl.ds(s * 128, 128)
+        target = small_grad.at[s // 2, pl.ds((s % 2) * 2, 2)]
         for vector, row in ((B_DOWN, 0), (G_TWO, 1), (S_TWO, 2), (B_OUT, 3), (G_ONE, 4), (S_ONE, 5)):
-            small_grad[s, vector, 0:1, 0:128] = acc[row : row + 1, here] * first
+            target[vector // 4, vector % 4, 0:1, 0:128] = acc[row : row + 1, here] * first
         block = acc_up[:, pl.ds(s * TILE, TILE)]
-        small_grad[s, B_UP, 0:1, :] = block * first
-        small_grad[s, B_UP, 1:2, :] = block * (1.0 - first)
+        target[B_UP // 4, B_UP % 4, 0:1, :] = block * first
+        target[B_UP // 4, B_UP % 4, 1:2, :] = block * (1.0 - first)
         at = (s // 4) * 2 * half_width + (s % 4) * 2 * HEAD_DIM
         heads = []
         for k in range(2):
             value = acc_qkv[:, pl.ds(at + k * HEAD_DIM, HEAD_DIM)]
             heads += [value * first, value * (1.0 - first)]
-        small_grad[s, B_QV, 0:1, :] = jnp.concatenate(heads, axis=-1)
+        target[B_QV // 4, B_QV % 4, 0:1, :] = jnp.concatenate(heads, axis=-1)
+    carry(5)
+    for s in own:
+        s.finish(0)
+    carry(6)
     for s in streams:
-        s.finish(0)
-    for s in streams:
+        s.drain()
+    for s in own:
         s.drain((0,))
 
 
-def backward_block(layer, grad_state, record, segs, small, weights, grads):
-    state, middle, qkv, attn, slope = record
-    count = len(grads)
+def backward_block(layer, grad_state, record, segs, small, weights, given):
+    state = record[0]
+    count = len(given)
     length, width = state.shape
-    inner = slope.shape[1]
-    shapes = [
-        ((length, width), F32),
-        ((length, width), LOW),
-        ((length, inner), LOW),
-        ((length, width), LOW),
-        ((length, 3 * width // 2), LOW),
-        ((8, 8, 8, 256), F32),
-    ]
-    shapes = [jax.ShapeDtypeStruct(*s) for s in shapes]
-    shapes += [jax.ShapeDtypeStruct(g.shape[1:], g.dtype) for g in grads]
-    bufs = scatter_scratch([g.shape[3:] for g in grads], [g.dtype for g in grads], (0,))
+    inner = record[4].shape[1]
+    cube = (RING, RING, RING)
+    w_up, w_down, w_qkv, w_out = weights
+    halves = []
+    for w, (share, of) in ((w_up, UP_PART), (w_down, DOWN_PART)):
+        rows, cols = w.shape[3:]
+        halves += [(rows, cols * share // of), (rows, cols - cols * share // of)]
+    ends = [((length, width), F32)] + [((RING, RING) + h, LOW) for h in halves]
+    ends += [(cube + (width // 64, width // 2), LOW)] * 3
+    ends += [(cube + w_out.shape[3:], LOW), (cube + (8, 256), F32)]
+    shapes = [jax.ShapeDtypeStruct(*e) for e in ends]
+    shapes += [jax.ShapeDtypeStruct(g.shape[-2:], g.dtype) for g in given]
+    bufs = []
+    for m, g in enumerate(given):
+        bufs += scatter_scratch(g.shape[-2:], g.dtype, 1 if m < SPLIT else 0, False)
     sems = [DMA((count, 18)), DMA((count, 18)), DMA((count, 5))] if count else []
+    flat = [w.reshape(-1, w.shape[-1]) for w in (w_qkv, w_out)]
     out = pl.pallas_call(
         functools.partial(backward_kernel, layer, count),
         out_shape=shapes,
-        in_specs=[VMEM] * 8 + [ANY] * (4 + count),
-        out_specs=[VMEM] * (6 + count),
-        scratch_shapes=weight_scratch(weights)
+        in_specs=[VMEM] * 11 + [ANY] * 4 + [VMEM] * min(count, SPLIT) + [ANY] * max(count - SPLIT, 0),
+        out_specs=[VMEM] * (10 + count),
+        scratch_shapes=[pltpu.VMEM(w.shape, LOW) for w in flat + [w_up, w_down]]
         + pair_scratch(length, width)
         + [
             pltpu.VMEM((2, 1, width), F32),
             pltpu.VMEM((6, width), F32),
             pltpu.VMEM((1, inner), F32),
             pltpu.VMEM((1, 3 * width // 2), F32),
+            pltpu.VMEM((length, width), LOW),
+            pltpu.VMEM((length, inner), LOW),
+            pltpu.VMEM((length, width), LOW),
+            pltpu.VMEM((length, 3 * width // 2), LOW),
             pltpu.VMEM((length, width // 2), LOW),
-            pltpu.VMEM((length, width), F32),
+        ]
+        + [pltpu.VMEM((6, RING, RING, r, c // 2), LOW) for r, c in halves]
+        + [
             DMA((4,)),
             DMA((2, width // TILE)),
             DMA((2, width // TILE)),
+            DMA((SPLIT, 6)),
+            DMA((SPLIT, 6)),
         ]
         + bufs
         + sems,
         compiler_params=pltpu.CompilerParams(
-            collective_id=4 + layer, has_side_effects=True, vmem_limit_bytes=63 * 1024 * 1024
+            collective_id=4 + layer, has_side_effects=True, vmem_limit_bytes=67043328
         ),
         name="backward_block",
-    )(grad_state, state, middle, qkv, attn, slope, segs, small, *weights, *grads)
-    return out[:6], out[6:]
+    )(grad_state, *record, segs, small, w_up, w_down, *flat, *given)
+    return out[0], list(out[1:10]), list(out[10:])
 
 
 def finish_kernel(layers, *refs):
-    ins, outs = refs[: 5 * layers], refs[5 * layers :]
+    ins, outs = refs[: 9 * layers], refs[9 * layers :]
     o_qkv, o_out, o_up, o_down = outs[:4]
     for l in range(layers):
-        up, down, qkv, out, small = ins[5 * l : 5 * l + 5]
+        up_a, up_b, down_a, down_b, *qkv, out, small = ins[9 * l : 9 * l + 9]
+        blocks = up_a.shape[-1] // TILE
         for s in range(8):
             for c in range(2):
-                o_up[l, :, pl.ds((2 * s + c) * TILE, TILE)] = up[c, 0, :, pl.ds(s * TILE, TILE)].astype(F32)
+                up, at = (up_a, s) if s < blocks else (up_b, s - blocks)
+                o_up[l, :, pl.ds((2 * s + c) * TILE, TILE)] = up[c, 0, :, pl.ds(at * TILE, TILE)].astype(F32)
         for c in range(2):
-            o_down[l, c, 0] = down[c, 0].astype(F32)
+            o_down[l, c, 0] = jnp.concatenate([down_a[c, 0], down_b[c, 0]], axis=-1).astype(F32)
             o_out[l, c, 0] = out[c, 0].astype(F32)
         for k in range(24):
-            here = pl.ds(k * HEAD_DIM, HEAD_DIM)
-            both = jnp.concatenate([qkv[0, 0, :, here], qkv[1, 0, :, here]], axis=-1)
+            here = pl.ds((k % 8) * HEAD_DIM, HEAD_DIM)
+            both = jnp.concatenate([qkv[k // 8][c, 0, :, here] for c in range(2)], axis=-1)
             o_qkv[l, :, pl.ds(k * 128, 128)] = both.astype(F32)
 
         @pl.when(pl.program_id(0) == 0)
@@ -1173,13 +1232,14 @@
         for m, a in enumerate(f):
             r, c = a.shape[3:]
             args.append(a.reshape(2, 8, r, c))
-            if m < 4:
+            if m < 8:
                 in_specs.append(pl.BlockSpec((2, 1, r, c), lambda p: (0, p, 0, 0)))
             else:
                 in_specs.append(pl.BlockSpec((2, 8, r, c), lambda p: (0, 0, 0, 0)))
-    up, down, qkv, out = (a.shape[2:] for a in args[:4])
+    up, up_b, down, down_b, qkv, _, _, out = (a.shape[2:] for a in args[:8])
+    up, down = (up[0], up[1] + up_b[1]), (down[0], down[1] + down_b[1])
     shapes, specs = [], []
-    for rows, cols in ((qkv[0], 2 * qkv[1]), (0, 0), (up[0], 2 * up[1])):
+    for rows, cols in ((qkv[0], 6 * qkv[1]), (0, 0), (up[0], 2 * up[1])):
         if rows:
             shapes.append(jax.ShapeDtypeStruct((layers, 8 * rows, cols), F32))
             specs.append(pl.BlockSpec((layers, rows, cols), lambda p: (0, p, 0)))
@@ -1305,36 +1365,26 @@
     state, segs = wholes[0].reshape(length, width), wholes[1]
     small = fulls[4].reshape(8, 8, 8, 256)
     records = []
-    weights = [[w.reshape(-1, w.shape[-1]) for w in fulls[:4]]]
+    weights = [fulls[:4]]
     for l in range(layers):
         carried, parts = (begun, []) if l == 0 else ([], [cotangent])
-        made, fulls, wholes = forward_block(l, state, segs, small, weights[l], list(carried), parts)
-        weights.append([w.reshape(-1, w.shape[-1]) for w in fulls])
+        flat = [w.reshape(-1, w.shape[-1]) for w in weights[l]]
+        made, fulls, wholes = forward_block(l, state, segs, small, flat, list(carried), parts)
+        weights.append(fulls)
         new_state, act_one, qkv, attn, middle, act_two, slope, hidden = made
-        records.append(((state, middle, qkv, attn, slope), (act_one, act_two, hidden, attn)))
+        records.append((state, middle, qkv, attn, slope, hidden, act_one, act_two))
         state = new_state
     grad_state = wholes[0].reshape(length, width)
-    pieces, sums = [], []
+    pieces = []
     for l in reversed(range(layers)):
-        kept, (act_one, act_two, hidden, attn) = records[l]
-        made, done = backward_block(l, grad_state, kept, segs, small, weights[l], pieces)
-        sums += done
-        grad_state, grad_low, d_pre_low, mid_low, d_qkv, small_grad = made
-        tokens = ((0,), (0,))
-        pieces = [
-            dot(act_two, d_pre_low, tokens),
-            dot(hidden, grad_low, tokens),
-            dot(act_one, d_qkv, tokens),
-            dot(attn, mid_low, tokens),
-        ]
-        pieces = [g.astype(LOW).reshape(RING, RING, RING, -1, g.shape[-1]) for g in pieces]
-        pieces.append(small_grad.reshape(RING, RING, RING, 8, 256))
+        grad_state, pieces, sums = backward_block(
+            l, grad_state, records[l], segs, small, weights[l], pieces
+        )
     quarter = (RING, length // RING, width)
-    finals, parts = scatter_all(
+    finals, others, parts = scatter_all(
         pieces, sums, [state.reshape(quarter), grad_state.reshape(quarter)]
     )
-    finals = [finals[5 * l : 5 * l + 5] for l in range(layers)]
-    return (parts[0], parts[1]) + finish(finals, sizes)
+    return (parts[0], parts[1]) + finish([finals, others], sizes)
 
 
 def solution(mesh):

time: 409 us -> 402 us (0.983)
  matrix products: 33 us -> 0 us
  Pallas kernels: 368 us -> 396 us
    pallas_call x2, Pallas kernels: 85.8 us -> 121 us  [backward_block(): pl.pallas_call(functools.partial(backward_kernel, layer, count), out_shap...]
    dot_general x8 -> x0, matrix products: 33 us -> none  [dot(): lax.dot_general(left, right, (dims, ((), ())), preferred_element_type=F32)]
    pallas_call x1, Pallas kernels: 114 us -> 107 us  [scatter_all(): pl.pallas_call(functools.partial(scatter_kernel, moved), out_shape=shapes...]
where the time goes in v3:
time: 402 us; the launch traced here: 399 us
  Pallas kernels  396 us (99%)
    pallas_call x2, Pallas kernels, backward_block(): pl.pallas_call(functools.partial(backward_kernel, layer, count), out_shap...  121 us
    pallas_call x1, Pallas kernels, scatter_all(): pl.pallas_call(functools.partial(scatter_kernel, moved), out_shape=shapes...  107 us
    pallas_call x1, Pallas kernels, gather_all(): pl.pallas_call(functools.partial(gather_kernel, count, len(owns), moved),...  80.2 us
    pallas_call x2, Pallas kernels, forward_block(): pl.pallas_call(functools.partial(forward_kernel, layer, count, moved), ou...  75.2 us
    pallas_call x1, Pallas kernels, finish(): pl.pallas_call(functools.partial(finish_kernel, layers), out_shape=shapes...  9.86 us

profile of v3, /device:TPU:1, one launch (start us, length us, event | category | flops | bytes accessed | tf_op | source)
XLA Modules:
  0.0 398.7 jit_solution(11870945129753206951)
XLA Ops:
  0.7 0.6 pad_add_fusion.where
  1.2 2.8 prepare.1
  4.0 80.2 %gather_all.1 = (bf16[4,4,4,16,2048]{4,3,2,1,0:T(8,128)(2,1)}, bf16[4,4,4,32,1024]{4,3,2,1,0:T(8,128)(2,1)}, bf16[4,4,4,16,1536]{4,3,2,1,0:T(8,128)(2,1)}, bf16[...) custom-call(bf16[16,2048]{1,0:T(8,128)(2,1)} %get-tuple-element.117., ...), custom_call_target="tpu_custom_call" | custom-call | tf_op jit(solution)/shard_map/gather_all/pallas_call | solution.py:262
  84.2 44.4 %forward_block.2 = (f32[320,1024]{1,0:T(8,128)}, bf16[320,1024]{1,0:T(8,128)(2,1)}, bf16[320,1536]{1,0:T(8,128)(2,1)}, bf16[320,512]{1,0:T(8,128)(2,1)}, f32[320...) custom-call(f32[320,1024]{1,0:T(8,128)} %bitcast.49, ...), custom_call_target="tpu_custom_call", output_to_operand_aliasing={{8}: (7, {}), {9}: (8, {}), {10}: (9, {}), {11}: (10, {})} | custom-call | tf_op jit(solution)/shard_map/forward_block/pallas_call | solution.py:916
  128.6 30.9 %forward_block.3 = (f32[320,1024]{1,0:T(8,128)}, bf16[320,1024]{1,0:T(8,128)(2,1)}, bf16[320,1536]{1,0:T(8,128)(2,1)}, bf16[320,512]{1,0:T(8,128)(2,1)}, f32[320...) custom-call(f32[320,1024]{1,0:T(8,128)} %get-tuple-element.138.refs_, ...), custom_call_target="tpu_custom_call" | custom-call | tf_op jit(solution)/shard_map/forward_block/pallas_call | solution.py:916
  159.5 46.9 %backward_block.2 = (f32[320,1024]{1,0:T(8,128)}, bf16[4,4,16,1280]{3,2,1,0:T(8,128)(2,1)}, bf16[4,4,16,768]{3,2,1,0:T(8,128)(2,1)}, bf16[4,4,32,768]{3,2,1,0:T(...) custom-call(f32[320,1024]{1,0:T(8,128)} %bitcast.53, ...), custom_call_target="tpu_custom_call" | custom-call | tf_op jit(solution)/shard_map/backward_block/pallas_call | solution.py:1162
  206.4 74.0 %backward_block.3 = (f32[320,1024]{1,0:T(8,128)}, bf16[4,4,16,1280]{3,2,1,0:T(8,128)(2,1)}, bf16[4,4,16,768]{3,2,1,0:T(8,128)(2,1)}, bf16[4,4,32,768]{3,2,1,0:T(...) custom-call(f32[320,1024]{1,0:T(8,128)} %get-tuple-element.151.refs_, ...), custom_call_target="tpu_custom_call" | custom-call | tf_op jit(solution)/shard_map/backward_block/pallas_call | solution.py:1162
  280.4 106.5 %scatter_all.1 = (bf16[2,2,4,16,1280]{4,3,2,1,0:T(8,128)(2,1)}, bf16[2,2,4,16,768]{4,3,2,1,0:T(8,128)(2,1)}, bf16[2,2,4,32,768]{4,3,2,1,0:T(8,128)(2,1)}, bf16[2...) custom-call(bf16[4,4,16,1280]{3,2,1,0:T(8,128)(2,1)} %get-tuple-elem, ...), custom_call_target="tpu_custom_call" | custom-call | tf_op jit(solution)/shard_map/scatter_all/pallas_call | solution.py:602
  386.9 0.0 copy-start.1
  386.9 0.0 copy-start
  387.0 9.9 %finish.1 = (f32[2,128,3072]{2,1,0:T(8,128)}, f32[2,2,8,8,1024]{4,3,2,1,0:T(8,128)}, f32[2,128,4096]{2,1,0:T(8,128)}, f32[2,2,8,32,1024]{4,3,2,1,0:T(8,128)}, f3...) custom-call(bf16[2,8,16,1280]{3,2,1,0:T(8,128)(2,1)} %bitcast.58, ...), custom_call_target="tpu_custom_call" | custom-call | tf_op jit(solution)/shard_map/finish/pallas_call | solution.py:1254
  396.8 0.0 copy-done.1
  396.8 0.8 copy.39
  397.7 0.0 copy-done
  397.7 0.8 copy.40
Async XLA Ops:
  386.9 9.9 %copy-start.1 = (f32[2,80,1024]{2,1,0:T(8,128)S(1)}, f32[2,80,1024]{2,1,0:T(8,128)}, u32[]{:S(2)}) copy-start(f32[2,80,1024]{2,1,0:T(8,128)} %get-tuple-element.234) | copy-start | bytes 1966084
  386.9 10.7 %copy-start = (f32[2,80,1024]{2,1,0:T(8,128)S(1)}, f32[2,80,1024]{2,1,0:T(8,128)}, u32[]{:S(2)}) copy-start(f32[2,80,1024]{2,1,0:T(8,128)} %get-tuple-element.235) | copy-start | bytes 1966084

commit v4 on v3

--- a/solution.py
+++ b/solution.py
@@ -474,9 +474,9 @@
             self.keep().start()
             for kind in (4,) if self.across_first() else (0, 1):
                 self.spread(kind).start()
-            self.keep().wait()
         elif self.across_first():
             if step == 1:
+                self.keep().wait()
                 self.spread_arrives(4)
                 for kind in (0, 1):
                     self.spread(kind).start()
@@ -489,6 +489,7 @@
                     self.spread_arrives(kind)
         else:
             if step == 1:
+                self.keep().wait()
                 for kind in (0, 1):
                     self.spread_arrives(kind)
                     self.spread(kind + 2).start()

time: 402 us -> 379 us (0.943)
  Pallas kernels: 396 us -> 373 us
    pallas_call x1, Pallas kernels: 107 us -> 83.6 us  [scatter_all(): pl.pallas_call(functools.partial(scatter_kernel, moved), out_shape=shapes...]
where the time goes in v4:
time: 379 us; the launch traced here: 376 us
  Pallas kernels  373 us (98%)
    pallas_call x2, Pallas kernels, backward_block(): pl.pallas_call(functools.partial(backward_kernel, layer, count), out_shap...  121 us
    pallas_call x1, Pallas kernels, scatter_all(): pl.pallas_call(functools.partial(scatter_kernel, moved), out_shape=shapes...  83.6 us
    pallas_call x1, Pallas kernels, gather_all(): pl.pallas_call(functools.partial(gather_kernel, count, len(owns), moved),...  80.2 us
    pallas_call x2, Pallas kernels, forward_block(): pl.pallas_call(functools.partial(forward_kernel, layer, count, moved), ou...  75.2 us
    pallas_call x1, Pallas kernels, finish(): pl.pallas_call(functools.partial(finish_kernel, layers), out_shape=shapes...  9.86 us

profile of v4, /device:TPU:1, one launch (start us, length us, event | category | flops | bytes accessed | tf_op | source)
XLA Modules:
  0.0 375.8 jit_solution(15109668757515758738)
XLA Ops:
  0.7 0.6 pad_add_fusion.where
  1.2 2.8 prepare.1
  4.0 80.2 %gather_all.1 = (bf16[4,4,4,16,2048]{4,3,2,1,0:T(8,128)(2,1)}, bf16[4,4,4,32,1024]{4,3,2,1,0:T(8,128)(2,1)}, bf16[4,4,4,16,1536]{4,3,2,1,0:T(8,128)(2,1)}, bf16[...) custom-call(bf16[16,2048]{1,0:T(8,128)(2,1)} %get-tuple-element.117., ...), custom_call_target="tpu_custom_call" | custom-call | tf_op jit(solution)/shard_map/gather_all/pallas_call | solution.py:262
  84.2 44.4 %forward_block.2 = (f32[320,1024]{1,0:T(8,128)}, bf16[320,1024]{1,0:T(8,128)(2,1)}, bf16[320,1536]{1,0:T(8,128)(2,1)}, bf16[320,512]{1,0:T(8,128)(2,1)}, f32[320...) custom-call(f32[320,1024]{1,0:T(8,128)} %bitcast.49, ...), custom_call_target="tpu_custom_call", output_to_operand_aliasing={{8}: (7, {}), {9}: (8, {}), {10}: (9, {}), {11}: (10, {})} | custom-call | tf_op jit(solution)/shard_map/forward_block/pallas_call | solution.py:917
  128.6 30.9 %forward_block.3 = (f32[320,1024]{1,0:T(8,128)}, bf16[320,1024]{1,0:T(8,128)(2,1)}, bf16[320,1536]{1,0:T(8,128)(2,1)}, bf16[320,512]{1,0:T(8,128)(2,1)}, f32[320...) custom-call(f32[320,1024]{1,0:T(8,128)} %get-tuple-element.138.refs_, ...), custom_call_target="tpu_custom_call" | custom-call | tf_op jit(solution)/shard_map/forward_block/pallas_call | solution.py:917
  159.5 46.9 %backward_block.2 = (f32[320,1024]{1,0:T(8,128)}, bf16[4,4,16,1280]{3,2,1,0:T(8,128)(2,1)}, bf16[4,4,16,768]{3,2,1,0:T(8,128)(2,1)}, bf16[4,4,32,768]{3,2,1,0:T(...) custom-call(f32[320,1024]{1,0:T(8,128)} %bitcast.53, ...), custom_call_target="tpu_custom_call" | custom-call | tf_op jit(solution)/shard_map/backward_block/pallas_call | solution.py:1163
  206.4 74.0 %backward_block.3 = (f32[320,1024]{1,0:T(8,128)}, bf16[4,4,16,1280]{3,2,1,0:T(8,128)(2,1)}, bf16[4,4,16,768]{3,2,1,0:T(8,128)(2,1)}, bf16[4,4,32,768]{3,2,1,0:T(...) custom-call(f32[320,1024]{1,0:T(8,128)} %get-tuple-element.151.refs_, ...), custom_call_target="tpu_custom_call" | custom-call | tf_op jit(solution)/shard_map/backward_block/pallas_call | solution.py:1163
  280.4 83.6 %scatter_all.1 = (bf16[2,2,4,16,1280]{4,3,2,1,0:T(8,128)(2,1)}, bf16[2,2,4,16,768]{4,3,2,1,0:T(8,128)(2,1)}, bf16[2,2,4,32,768]{4,3,2,1,0:T(8,128)(2,1)}, bf16[2...) custom-call(bf16[4,4,16,1280]{3,2,1,0:T(8,128)(2,1)} %get-tuple-elem, ...), custom_call_target="tpu_custom_call" | custom-call | tf_op jit(solution)/shard_map/scatter_all/pallas_call | solution.py:603
  364.0 0.0 copy-start.1
  364.0 0.0 copy-start
  364.0 9.9 %finish.1 = (f32[2,128,3072]{2,1,0:T(8,128)}, f32[2,2,8,8,1024]{4,3,2,1,0:T(8,128)}, f32[2,128,4096]{2,1,0:T(8,128)}, f32[2,2,8,32,1024]{4,3,2,1,0:T(8,128)}, f3...) custom-call(bf16[2,8,16,1280]{3,2,1,0:T(8,128)(2,1)} %bitcast.58, ...), custom_call_target="tpu_custom_call" | custom-call | tf_op jit(solution)/shard_map/finish/pallas_call | solution.py:1255
  373.9 0.0 copy-done.1
  373.9 0.8 copy.39
  374.8 0.0 copy-done
  374.8 0.8 copy.40
Async XLA Ops:
  364.0 9.9 %copy-start.1 = (f32[2,80,1024]{2,1,0:T(8,128)S(1)}, f32[2,80,1024]{2,1,0:T(8,128)}, u32[]{:S(2)}) copy-start(f32[2,80,1024]{2,1,0:T(8,128)} %get-tuple-element.234) | copy-start | bytes 1966084
  364.0 10.7 %copy-start = (f32[2,80,1024]{2,1,0:T(8,128)S(1)}, f32[2,80,1024]{2,1,0:T(8,128)}, u32[]{:S(2)}) copy-start(f32[2,80,1024]{2,1,0:T(8,128)} %get-tuple-element.235) | copy-start | bytes 1966084

commit v5 on v4

--- a/solution.py
+++ b/solution.py
@@ -556,13 +556,13 @@
                 homeward(a, q).start()
 
     for at in range(11):
-        for n in news[MATRICES:]:
-            if at < 5:
-                n.publish(at)
         for s, n in zip(streams, news):
             s.step(at)
             if 0 <= at - s.steps() + 1 < 5:
                 n.publish(at - s.steps() + 1)
+        if at % 2 == 0 and at < 10:
+            for n in news[MATRICES:]:
+                n.publish(at // 2)
     for s in streams:
         s.drain()
     for n in news:

time: 379 us -> 377 us (level)
  no operation moved by 1% of the time
where the time goes in v5:
time: 377 us; the launch traced here: 374 us
  Pallas kernels  371 us (98%)
    pallas_call x2, Pallas kernels, backward_block(): pl.pallas_call(functools.partial(backward_kernel, layer, count), out_shap...  121 us
    pallas_call x1, Pallas kernels, scatter_all(): pl.pallas_call(functools.partial(scatter_kernel, moved), out_shape=shapes...  81.9 us
    pallas_call x1, Pallas kernels, gather_all(): pl.pallas_call(functools.partial(gather_kernel, count, len(owns), moved),...  80.2 us
    pallas_call x2, Pallas kernels, forward_block(): pl.pallas_call(functools.partial(forward_kernel, layer, count, moved), ou...  75.2 us
    pallas_call x1, Pallas kernels, finish(): pl.pallas_call(functools.partial(finish_kernel, layers), out_shape=shapes...  9.86 us

profile of v5, /device:TPU:1, one launch (start us, length us, event | category | flops | bytes accessed | tf_op | source)
XLA Modules:
  0.0 374.0 jit_solution(1912734029126980862)
XLA Ops:
  0.7 0.6 pad_add_fusion.where
  1.2 2.8 prepare.1
  4.0 80.2 %gather_all.1 = (bf16[4,4,4,16,2048]{4,3,2,1,0:T(8,128)(2,1)}, bf16[4,4,4,32,1024]{4,3,2,1,0:T(8,128)(2,1)}, bf16[4,4,4,16,1536]{4,3,2,1,0:T(8,128)(2,1)}, bf16[...) custom-call(bf16[16,2048]{1,0:T(8,128)(2,1)} %get-tuple-element.117., ...), custom_call_target="tpu_custom_call" | custom-call | tf_op jit(solution)/shard_map/gather_all/pallas_call | solution.py:262
  84.2 44.4 %forward_block.2 = (f32[320,1024]{1,0:T(8,128)}, bf16[320,1024]{1,0:T(8,128)(2,1)}, bf16[320,1536]{1,0:T(8,128)(2,1)}, bf16[320,512]{1,0:T(8,128)(2,1)}, f32[320...) custom-call(f32[320,1024]{1,0:T(8,128)} %bitcast.49, ...), custom_call_target="tpu_custom_call", output_to_operand_aliasing={{8}: (7, {}), {9}: (8, {}), {10}: (9, {}), {11}: (10, {})} | custom-call | tf_op jit(solution)/shard_map/forward_block/pallas_call | solution.py:917
  128.6 30.9 %forward_block.3 = (f32[320,1024]{1,0:T(8,128)}, bf16[320,1024]{1,0:T(8,128)(2,1)}, bf16[320,1536]{1,0:T(8,128)(2,1)}, bf16[320,512]{1,0:T(8,128)(2,1)}, f32[320...) custom-call(f32[320,1024]{1,0:T(8,128)} %get-tuple-element.138.refs_, ...), custom_call_target="tpu_custom_call" | custom-call | tf_op jit(solution)/shard_map/forward_block/pallas_call | solution.py:917
  159.5 46.9 %backward_block.2 = (f32[320,1024]{1,0:T(8,128)}, bf16[4,4,16,1280]{3,2,1,0:T(8,128)(2,1)}, bf16[4,4,16,768]{3,2,1,0:T(8,128)(2,1)}, bf16[4,4,32,768]{3,2,1,0:T(...) custom-call(f32[320,1024]{1,0:T(8,128)} %bitcast.53, ...), custom_call_target="tpu_custom_call" | custom-call | tf_op jit(solution)/shard_map/backward_block/pallas_call | solution.py:1163
  206.4 74.0 %backward_block.3 = (f32[320,1024]{1,0:T(8,128)}, bf16[4,4,16,1280]{3,2,1,0:T(8,128)(2,1)}, bf16[4,4,16,768]{3,2,1,0:T(8,128)(2,1)}, bf16[4,4,32,768]{3,2,1,0:T(...) custom-call(f32[320,1024]{1,0:T(8,128)} %get-tuple-element.151.refs_, ...), custom_call_target="tpu_custom_call" | custom-call | tf_op jit(solution)/shard_map/backward_block/pallas_call | solution.py:1163
  280.4 81.9 %scatter_all.1 = (bf16[2,2,4,16,1280]{4,3,2,1,0:T(8,128)(2,1)}, bf16[2,2,4,16,768]{4,3,2,1,0:T(8,128)(2,1)}, bf16[2,2,4,32,768]{4,3,2,1,0:T(8,128)(2,1)}, bf16[2...) custom-call(bf16[4,4,16,1280]{3,2,1,0:T(8,128)(2,1)} %get-tuple-elem, ...), custom_call_target="tpu_custom_call" | custom-call | tf_op jit(solution)/shard_map/scatter_all/pallas_call | solution.py:603
  362.3 0.0 copy-start.1
  362.3 0.0 copy-start
  362.3 9.9 %finish.1 = (f32[2,128,3072]{2,1,0:T(8,128)}, f32[2,2,8,8,1024]{4,3,2,1,0:T(8,128)}, f32[2,128,4096]{2,1,0:T(8,128)}, f32[2,2,8,32,1024]{4,3,2,1,0:T(8,128)}, f3...) custom-call(bf16[2,8,16,1280]{3,2,1,0:T(8,128)(2,1)} %bitcast.58, ...), custom_call_target="tpu_custom_call" | custom-call | tf_op jit(solution)/shard_map/finish/pallas_call | solution.py:1255
  372.2 0.0 copy-done.1
  372.2 0.8 copy.39
  373.0 0.0 copy-done
  373.0 0.8 copy.40
Async XLA Ops:
  362.3 9.9 %copy-start.1 = (f32[2,80,1024]{2,1,0:T(8,128)S(1)}, f32[2,80,1024]{2,1,0:T(8,128)}, u32[]{:S(2)}) copy-start(f32[2,80,1024]{2,1,0:T(8,128)} %get-tuple-element.234) | copy-start | bytes 1966084
  362.3 10.7 %copy-start = (f32[2,80,1024]{2,1,0:T(8,128)S(1)}, f32[2,80,1024]{2,1,0:T(8,128)}, u32[]{:S(2)}) copy-start(f32[2,80,1024]{2,1,0:T(8,128)} %get-tuple-element.235) | copy-start | bytes 1966084
